TPU v7x, 512 devices: a whole 4x8x8 slice. The times are simulated.
512 devices in a mesh: depth: 128 (over z, y, core), rows: 4 (over x).
Axes of the slice: x: 4, y: 8, z: 8, core: 2. Of those that a mesh axis runs over, the one named last changes fastest.
Arguments:
- density: float32 [256, 512, 512], P('depth', 'rows'), may hold values from 0 to 6
- transfer_table: float32 [4, 16], replicated, may hold values from 0.2 to 1
Outputs:
- picture: float32 [4, 512, 512], P(None, ('rows', 'depth'))
All inputs are finite; a program needn't handle non-finite values.
Results may differ from a plain program's by a relative error of at most 0.000021.
Values sent between devices are 32-bit elements; how exact they have to be, the bound alone decides.
No kernel may reach another device: no remote copies, remote signals or barrier semaphores. Data moves between devices by JAX's collectives and lax.ppermute only.
A program may use at most 64 MiB of HBM per device.

v0:
```python
import jax
import jax.numpy as jnp
from jax import lax
from jax.sharding import PartitionSpec as P

PASSES = 3
KNOTS = 16


TIME_STEP = 0.15
OPTICAL_DEPTH = 3.0
UPPER_DENSITY = 6.0
AMBIENT = 0.35


def extended(cells, sides, width):
    for axis, dim in sides:
        count = lax.axis_size(axis)
        ends = count - 1
        head = lax.slice_in_dim(cells, 0, width, axis=dim)
        tail = lax.slice_in_dim(cells, cells.shape[dim] - width, cells.shape[dim], axis=dim)
        cells = jnp.concatenate(
            [
                lax.ppermute(tail, axis, [(i, (i + 1) % count) for i in range(ends)]),
                cells,
                lax.ppermute(head, axis, [((i + 1) % count, i) for i in range(ends)]),
            ],
            axis=dim,
        )
    return cells


def partner(value, axis, stride):
    mask = 2**stride
    pairs = [(source, source ^ mask) for source in range(lax.axis_size(axis))]
    return lax.ppermute(value, axis, pairs)


def diffusion_flux(center, neighbours):
    summed = jnp.zeros_like(center)
    for other in neighbours:
        change = other - center
        summed = summed + change / (1.0 + change * change)
    return center + TIME_STEP * summed


def appearance(center, neighbours, transfer_table, depth_count):
    deeper, nearer, next_row, prev_row, next_col, prev_col = neighbours
    grad_depth = (deeper - nearer) * 0.5
    grad_row = (next_row - prev_row) * 0.5
    grad_col = (next_col - prev_col) * 0.5
    shading = AMBIENT + (1.0 - AMBIENT) * jnp.abs(
        0.64 * grad_depth + 0.6 * grad_row + 0.48 * grad_col
    ) / jnp.sqrt(grad_depth * grad_depth + grad_row * grad_row + grad_col * grad_col + 0.25)
    position = center * ((KNOTS - 1) / UPPER_DENSITY)
    mixed = [jnp.zeros_like(center) for channel in range(4)]
    for knot in range(KNOTS):
        hat_weight = jnp.maximum(0.0, 1.0 - jnp.abs(position - knot))
        mixed = [
            mixed[channel] + transfer_table[channel, knot] * hat_weight for channel in range(4)
        ]
    opacity = 1.0 - jnp.exp(-mixed[3] * (OPTICAL_DEPTH / depth_count))
    colors = jnp.stack([mixed[0] * shading, mixed[1] * shading, mixed[2] * shading])
    return (colors, opacity)


def neighbour_fields(field):
    padded = extended(field, (("depth", 0), ("rows", 1)), 1)
    depth_index = lax.axis_index("depth")
    depth_count = lax.axis_size("depth")
    rows_index = lax.axis_index("rows")
    rows_count = lax.axis_size("rows")
    above = jnp.where(depth_index == 0, field[:1], padded[:1, 1:-1])
    below = jnp.where(depth_index == depth_count - 1, field[-1:], padded[-1:, 1:-1])
    first_row = jnp.where(rows_index == 0, field[:, :1], padded[1:-1, :1])
    last_row = jnp.where(rows_index == rows_count - 1, field[:, -1:], padded[1:-1, -1:])
    deeper = jnp.concatenate([field[1:], below], axis=0)
    nearer = jnp.concatenate([above, field[:-1]], axis=0)
    next_row = jnp.concatenate([field[:, 1:], last_row], axis=1)
    prev_row = jnp.concatenate([first_row, field[:, :-1]], axis=1)
    next_col = jnp.concatenate([field[:, :, 1:], field[:, :, -1:]], axis=2)
    prev_col = jnp.concatenate([field[:, :, :1], field[:, :, :-1]], axis=2)
    return (deeper, nearer, next_row, prev_row, next_col, prev_col)


def composite(front_part, back_part):
    return front_part + (1.0 - front_part[3:4]) * back_part


def per_device(density, transfer_table):
    planes_here = density.shape[0]
    band_rows = density.shape[1]
    columns = density.shape[2]
    depth_count = lax.axis_size("depth")
    depth_index = lax.axis_index("depth")
    total_planes = planes_here * depth_count
    field = density
    for sweep in range(PASSES):
        field = diffusion_flux(field, neighbour_fields(field))
    colors, opacity = appearance(field, neighbour_fields(field), transfer_table, total_planes)
    color_sum = jnp.zeros((3, band_rows, columns), jnp.float32)
    remaining = jnp.ones((band_rows, columns), jnp.float32)
    for plane in range(planes_here):
        color_sum = color_sum + remaining * opacity[plane] * colors[:, plane]
        remaining = remaining * (1.0 - opacity[plane])
    partial_value = jnp.concatenate([color_sum, (1.0 - remaining)[None]], axis=0)
    strip_rows = band_rows // depth_count
    current = partial_value.reshape(4, depth_count, strip_rows, columns)
    levels = depth_count.bit_length() - 1
    for bit in range(levels):
        blocks = current.shape[1]
        paired = current.reshape(4, blocks // 2, 2, strip_rows, columns)
        own_bit = depth_index // 2**bit % 2
        kept_half = jnp.where(own_bit == 0, paired[:, :, 0], paired[:, :, 1])
        sent_half = jnp.where(own_bit == 0, paired[:, :, 1], paired[:, :, 0])
        received = partner(sent_half, "depth", bit)
        front_part = jnp.where(own_bit == 0, kept_half, received)
        back_part = jnp.where(own_bit == 0, received, kept_half)
        current = composite(front_part, back_part)
    return current.reshape(4, strip_rows, columns)


def solution(mesh):
    placed = (P("depth", "rows", None), P())
    return jax.shard_map(
        per_device,
        mesh=mesh,
        in_specs=placed,
        out_specs=P(None, ("rows", "depth"), None),
        check_vma=False,
    )
```

profile of v0, /device:TPU:6, one launch (start us, length us, event | category | flops | bytes accessed | tf_op | source)
XLA Modules:
  0.0 205.6 jit_solution(18162330912781502355)
XLA Ops:
  2.6 3.7 %collective-permute-start.1 = (f32[1,128,512]{2,1,0:T(8,128)S(1)}, f32[1,128,512]{2,1,0:T(8,128)}, u32[]{:S(2)}, u32[]{:S(2)}) collective-permute-start(f32[1,128,512]{2,1,0:T(8,128)S(1)} %get-tuple-element.65), channel_id=1, source_target_pairs={{0,4},{4,8},{8,12},{12,16},{16,20},{20,24},{24,28},{28,32},{32,36}... | collective-permute-start | bytes 786440 | tf_op jit(solution)/shard_map/ppermute | solution.py:24
  10.7 2.7 %collective-permute-start.2 = (f32[4,1,512]{2,1,0:T(1,128)S(1)}, f32[4,1,512]{2,1,0:T(1,128)S(1)}, u32[]{:S(2)}, u32[]{:S(2)}) collective-permute-start(f32[4,1,512]{2,1,0:T(1,128)S(1)} %get-tuple-element.17), channel_id=1, source_target_pairs={{1,0},{2,1},{3,2},{5,4},{6,5},{7,6},{9,8},{10,9},{11,10},{13,12},{... | collective-permute-start | bytes 24584 | tf_op jit(solution)/shard_map/ppermute | solution.py:26
  15.4 3.6 %collective-permute-done.3 = f32[4,1,512]{2,1,0:T(1,128)S(1)} collective-permute-done((f32[4,1,512]{2,1,0:T(1,128)S(1)}, f32[4,1,512]{2,1,0:T(1,128)S(1)}, u32[]{:S(2)}, u32[]{:S(2)}) %collective-permute-start.3) | collective-permute-done | bytes 8224 | tf_op jit(solution)/shard_map/ppermute | solution.py:24
  19.0 1.8 multiply_add_fusion.4
  22.4 3.0 %collective-permute-start.5 = (f32[1,128,512]{2,1,0:T(8,128)S(1)}, f32[1,128,512]{2,1,0:T(8,128)S(1)}, u32[]{:S(2)}, u32[]{:S(2)}) collective-permute-start(f32[1,128,512]{2,1,0:T(8,128)S(1)} %get-tuple-element.52), channel_id=1, source_target_pairs={{0,4},{4,8},{8,12},{12,16},{16,20},{20,24},{24,28},{28,32},{32,36}... | collective-permute-start | bytes 786440 | tf_op jit(solution)/shard_map/ppermute | solution.py:24
  26.6 6.3 %collective-permute-start.6 = (f32[4,1,512]{2,1,0:T(1,128)S(1)}, f32[4,1,512]{2,1,0:T(1,128)S(1)}, u32[]{:S(2)}, u32[]{:S(2)}) collective-permute-start(f32[4,1,512]{2,1,0:T(1,128)S(1)} %get-tuple-element.15), channel_id=1, source_target_pairs={{1,0},{2,1},{3,2},{5,4},{6,5},{7,6},{9,8},{10,9},{11,10},{13,12},{... | collective-permute-start | bytes 24584 | tf_op jit(solution)/shard_map/ppermute | solution.py:26
  34.3 4.1 %collective-permute-done.7 = f32[4,1,512]{2,1,0:T(1,128)S(1)} collective-permute-done((f32[4,1,512]{2,1,0:T(1,128)S(1)}, f32[4,1,512]{2,1,0:T(1,128)S(1)}, u32[]{:S(2)}, u32[]{:S(2)}) %collective-permute-start.7) | collective-permute-done | bytes 8224 | tf_op jit(solution)/shard_map/ppermute | solution.py:24
  40.8 5.0 %collective-permute-start.9 = (f32[1,128,512]{2,1,0:T(8,128)S(1)}, f32[1,128,512]{2,1,0:T(8,128)S(1)}, u32[]{:S(2)}, u32[]{:S(2)}) collective-permute-start(f32[1,128,512]{2,1,0:T(8,128)S(1)} %get-tuple-element.40), channel_id=1, source_target_pairs={{0,4},{4,8},{8,12},{12,16},{16,20},{20,24},{24,28},{28,32},{32,36}... | collective-permute-start | bytes 786440 | tf_op jit(solution)/shard_map/ppermute | solution.py:24
  47.0 3.6 %collective-permute-start.10 = (f32[4,1,512]{2,1,0:T(1,128)S(1)}, f32[4,1,512]{2,1,0:T(1,128)S(1)}, u32[]{:S(2)}, u32[]{:S(2)}) collective-permute-start(f32[4,1,512]{2,1,0:T(1,128)S(1)} %get-tuple-element.13), channel_id=1, source_target_pairs={{1,0},{2,1},{3,2},{5,4},{6,5},{7,6},{9,8},{10,9},{11,10},{13,12},{... | collective-permute-start | bytes 24584 | tf_op jit(solution)/shard_map/ppermute | solution.py:26
  52.0 4.1 %collective-permute-done.11 = f32[4,1,512]{2,1,0:T(1,128)S(1)} collective-permute-done((f32[4,1,512]{2,1,0:T(1,128)S(1)}, f32[4,1,512]{2,1,0:T(1,128)S(1)}, u32[]{:S(2)}, u32[]{:S(2)}) %collective-permute-start.11) | collective-permute-done | bytes 8224 | tf_op jit(solution)/shard_map/ppermute | solution.py:24
  56.2 12.8 %exponential_subtract_fusion = (f32[2,128,512]{2,1,0:T(8,128)S(1)}, f32[2,128,512]{2,1,0:T(8,128)S(1)}) fusion(f32[]{:T(128)} %bitcast.15, f32[]{:T(128)} %bitcast.14, f32[]{:T(128)} %bitcast.13, f32[]{:T(128)} %bitcast.12, f32[]{:T(128)} %bitcast.11, f32[]{:T(128)} %bitcast.10, f32[]{:T(128)} %bitcast.9, f32[]{:T(128)} %bitcast.8, f32[]{:T(128)} %bitcast.7, ...), kind=kLoop, calls=%fused_computation.37 | loop fusion | flops 17694720 | bytes 4718656 | tf_op jit(solution)/shard_map/sub | solution.py:62
  71.1 7.9 %collective-permute-start.13 = (f32[1,128,512]{2,1,0:T(8,128)S(1)}, f32[1,128,512]{2,1,0:T(8,128)}, u32[]{:S(2)}, u32[]{:S(2)}) collective-permute-start(f32[1,128,512]{2,1,0:T(8,128)S(1)} %get-tuple-element.28), channel_id=1, source_target_pairs={{0,4},{4,8},{8,12},{12,16},{16,20},{20,24},{24,28},{28,32},{32,36}... | collective-permute-start | bytes 786440 | tf_op jit(solution)/shard_map/ppermute | solution.py:24
  82.3 2.2 %collective-permute-start.14 = (f32[4,1,512]{2,1,0:T(1,128)S(1)}, f32[4,1,512]{2,1,0:T(1,128)S(1)}, u32[]{:S(2)}, u32[]{:S(2)}) collective-permute-start(f32[4,1,512]{2,1,0:T(1,128)S(1)} %get-tuple-element.11), channel_id=1, source_target_pairs={{1,0},{2,1},{3,2},{5,4},{6,5},{7,6},{9,8},{10,9},{11,10},{13,12},{... | collective-permute-start | bytes 24584 | tf_op jit(solution)/shard_map/ppermute | solution.py:26
  84.5 1.5 collective-permute-start.15
  86.1 4.0 %collective-permute-done.15 = f32[4,1,512]{2,1,0:T(1,128)S(1)} collective-permute-done((f32[4,1,512]{2,1,0:T(1,128)S(1)}, f32[4,1,512]{2,1,0:T(1,128)S(1)}, u32[]{:S(2)}, u32[]{:S(2)}) %collective-permute-start.15) | collective-permute-done | bytes 8224 | tf_op jit(solution)/shard_map/ppermute | solution.py:24
  90.1 12.0 %multiply_bitcast_fusion.2 = (f32[1,2,128,512]{3,2,1,0:T(8,128)S(1)}, f32[2,128,512]{2,1,0:T(8,128)S(1)}) fusion(f32[]{:T(128)} %bitcast.31, f32[]{:T(128)} %bitcast.30, f32[]{:T(128)} %bitcast.29, f32[]{:T(128)} %bitcast.28, f32[]{:T(128)} %bitcast.27, f32[]{:T(128)} %bitcast.26, f32[]{:T(128)} %bitcast.25, f32[]{:T(128)} %bitcast.24, f32[]{:T(128)} %bitcast.23, ...), kind=kLoop, calls=%fused_computation.35 | loop fusion | flops 16121856 | bytes 4718656 | tf_op jit(solution)/shard_map/stack | solution.py:63
  102.0 11.8 %multiply_bitcast_fusion.1 = f32[1,2,128,512]{3,2,1,0:T(8,128)S(1)} fusion(f32[2,128,512]{2,1,0:T(8,128)S(1)} %get-tuple-element.6, f32[]{:T(128)} %bitcast.48, f32[]{:T(128)} %bitcast.47, f32[]{:T(128)} %bitcast.46, f32[]{:T(128)} %bitcast.45, f32[]{:T(128)} %bitcast.44, f32[]{:T(128)} %bitcast.43, f32[]{:T(128)} %bitcast.42, f32[]{:T(128)} %bitcast.41, ...), kind=kLoop, calls=%fused_computation.34 | loop fusion | flops 12582912 | bytes 1572928 | tf_op jit(solution)/shard_map/stack | solution.py:63
  113.8 11.7 %multiply_bitcast_fusion = f32[1,2,128,512]{3,2,1,0:T(8,128)S(1)} fusion(f32[2,128,512]{2,1,0:T(8,128)S(1)} %get-tuple-element.6, f32[]{:T(128)} %bitcast.65, f32[]{:T(128)} %bitcast.64, f32[]{:T(128)} %bitcast.63, f32[]{:T(128)} %bitcast.62, f32[]{:T(128)} %bitcast.61, f32[]{:T(128)} %bitcast.60, f32[]{:T(128)} %bitcast.59, f32[]{:T(128)} %bitcast.58, ...), kind=kLoop, calls=%fused_computation.33 | loop fusion | flops 12582912 | bytes 1572928 | tf_op jit(solution)/shard_map/stack | solution.py:63
  128.2 4.2 %collective-permute-start.16 = (f32[4,64,1,512]{3,1,0,2:T(8,128)S(1)}, f32[4,64,1,512]{3,1,0,2:T(8,128)S(1)}, u32[]{:S(2)}, u32[]{:S(2)}) collective-permute-start(f32[4,64,1,512]{3,1,0,2:T(8,128)S(1)} %select_bitcast_fusion), channel_id=1, source_target_pairs={{0,4},{4,0},{8,12},{12,8},{16,20},{20,16},{24,28},{28,24},{32,36},... | collective-permute-start | bytes 1572872 | tf_op jit(solution)/shard_map/ppermute | solution.py:36
  132.4 1.5 collective-permute-done.16
  134.7 6.2 %collective-permute-start.17 = (f32[4,32,1,512]{3,0,1,2:T(4,128)S(1)}, f32[4,32,1,512]{3,0,1,2:T(4,128)S(1)}, u32[]{:S(2)}, u32[]{:S(2)}) collective-permute-start(f32[4,32,1,512]{3,0,1,2:T(4,128)S(1)} %select_bitcast_fusion.1), channel_id=1, source_target_pairs={{0,8},{4,12},{8,0},{12,4},{16,24},{20,28},{24,16},{28,20},{32,40},... | collective-permute-start | bytes 786440 | tf_op jit(solution)/shard_map/ppermute | solution.py:36
  140.9 6.6 %collective-permute-done.17 = f32[4,32,1,512]{3,0,1,2:T(4,128)S(1)} collective-permute-done((f32[4,32,1,512]{3,0,1,2:T(4,128)S(1)}, f32[4,32,1,512]{3,0,1,2:T(4,128)S(1)}, u32[]{:S(2)}, u32[]{:S(2)}) %collective-permute-start.17) | collective-permute-done | bytes 262176 | tf_op jit(solution)/shard_map/ppermute | solution.py:36
  147.9 3.5 %collective-permute-start.18 = (f32[4,16,1,512]{3,0,1,2:T(4,128)S(1)}, f32[4,16,1,512]{3,0,1,2:T(4,128)S(1)}, u32[]{:S(2)}, u32[]{:S(2)}) collective-permute-start(f32[4,16,1,512]{3,0,1,2:T(4,128)S(1)} %select_bitcast_fusion.2), channel_id=1, source_target_pairs={{0,16},{4,20},{8,24},{12,28},{16,0},{20,4},{24,8},{28,12},{32,48},... | collective-permute-start | bytes 393224 | tf_op jit(solution)/shard_map/ppermute | solution.py:36
  151.4 7.1 %collective-permute-done.18 = f32[4,16,1,512]{3,0,1,2:T(4,128)S(1)} collective-permute-done((f32[4,16,1,512]{3,0,1,2:T(4,128)S(1)}, f32[4,16,1,512]{3,0,1,2:T(4,128)S(1)}, u32[]{:S(2)}, u32[]{:S(2)}) %collective-permute-start.18) | collective-permute-done | bytes 131104 | tf_op jit(solution)/shard_map/ppermute | solution.py:36
  158.6 8.3 %collective-permute-start.19 = (f32[4,8,1,512]{3,0,1,2:T(4,128)S(1)}, f32[4,8,1,512]{3,0,1,2:T(4,128)S(1)}, u32[]{:S(2)}, u32[]{:S(2)}) collective-permute-start(f32[4,8,1,512]{3,0,1,2:T(4,128)S(1)} %select_bitcast_fusion.3), channel_id=1, source_target_pairs={{0,32},{4,36},{8,40},{12,44},{16,48},{20,52},{24,56},{28,60},{32,0... | collective-permute-start | bytes 196616 | tf_op jit(solution)/shard_map/ppermute | solution.py:36
  167.0 2.2 %collective-permute-done.19 = f32[4,8,1,512]{3,0,1,2:T(4,128)S(1)} collective-permute-done((f32[4,8,1,512]{3,0,1,2:T(4,128)S(1)}, f32[4,8,1,512]{3,0,1,2:T(4,128)S(1)}, u32[]{:S(2)}, u32[]{:S(2)}) %collective-permute-start.19) | collective-permute-done | bytes 65568 | tf_op jit(solution)/shard_map/ppermute | solution.py:36
  169.3 9.9 %collective-permute-start.20 = (f32[4,4,1,512]{3,0,1,2:T(4,128)S(1)}, f32[4,4,1,512]{3,0,1,2:T(4,128)S(1)}, u32[]{:S(2)}, u32[]{:S(2)}) collective-permute-start(f32[4,4,1,512]{3,0,1,2:T(4,128)S(1)} %select_bitcast_fusion.4), channel_id=1, source_target_pairs={{0,64},{4,68},{8,72},{12,76},{16,80},{20,84},{24,88},{28,92},{32,9... | collective-permute-start | bytes 98312 | tf_op jit(solution)/shard_map/ppermute | solution.py:36
  179.3 1.8 collective-permute-done.20
  181.3 6.2 %collective-permute-start.21 = (f32[4,2,1,512]{3,2,1,0:T(1,128)S(1)}, f32[4,2,1,512]{3,2,1,0:T(1,128)S(1)}, u32[]{:S(2)}, u32[]{:S(2)}) collective-permute-start(f32[4,2,1,512]{3,2,1,0:T(1,128)S(1)} %fusion.11), channel_id=1, source_target_pairs={{0,128},{4,132},{8,136},{12,140},{16,144},{20,148},{24,152},{28,15... | collective-permute-start | bytes 49160 | tf_op jit(solution)/shard_map/ppermute | solution.py:36
  187.5 1.7 collective-permute-done.21
  189.3 14.1 %collective-permute-start.22 = (f32[4,1,1,512]{3,1,2,0:T(1,128)S(1)}, f32[4,1,1,512]{3,1,2,0:T(1,128)S(1)}, u32[]{:S(2)}, u32[]{:S(2)}) collective-permute-start(f32[4,1,1,512]{3,1,2,0:T(1,128)S(1)} %fusion.16), channel_id=1, source_target_pairs={{0,256},{4,260},{8,264},{12,268},{16,272},{20,276},{24,280},{28,28... | collective-permute-start | bytes 24584 | tf_op jit(solution)/shard_map/ppermute | solution.py:36
  203.4 1.6 collective-permute-done.22
  (115 shorter events, 27.9 us)
Async XLA Ops:
  0.0 6.3 %copy-start = (f32[2,128,512]{2,1,0:T(8,128)S(1)}, f32[2,128,512]{2,1,0:T(8,128)}, u32[]{:S(2)}) copy-start(f32[2,128,512]{2,1,0:T(8,128)} %param.2) | copy-start | bytes 1572868
  1.1 8.4 %copy-start.1 = (f32[1,128,512]{2,1,0:T(8,128)}, f32[1,128,512]{2,1,0:T(8,128)S(1)}, u32[]{:S(2)}) copy-start(f32[1,128,512]{2,1,0:T(8,128)S(1)} %get-tuple-element.64) | copy-start | bytes 786436
  1.1 8.4 %copy-start.2 = (f32[1,128,512]{2,1,0:T(8,128)}, f32[1,128,512]{2,1,0:T(8,128)S(1)}, u32[]{:S(2)}) copy-start(f32[1,128,512]{2,1,0:T(8,128)S(1)} %get-tuple-element.65) | copy-start | bytes 786436
  1.1 6.0 %copy-start.5 = (f32[4,16]{1,0:T(4,128)S(1)}, f32[4,16]{1,0:T(4,128)}, u32[]{:S(2)}) copy-start(f32[4,16]{1,0:T(4,128)} %param.3) | copy-start | bytes 772
  1.2 8.4 %collective-permute-start = (f32[1,128,512]{2,1,0:T(8,128)S(1)}, f32[1,128,512]{2,1,0:T(8,128)S(1)}, u32[]{:S(2)}, u32[]{:S(2)}) collective-permute-start(f32[1,128,512]{2,1,0:T(8,128)S(1)} %get-tuple-element.64), channel_id=1, source_target_pairs={{4,0},{8,4},{12,8},{16,12},{20,16},{24,20},{28,24},{32,28},{36,32}... | collective-permute-start | bytes 786440 | tf_op jit(solution)/shard_map/ppermute | solution.py:26
  2.6 6.9 %collective-permute-start.1 = (f32[1,128,512]{2,1,0:T(8,128)S(1)}, f32[1,128,512]{2,1,0:T(8,128)}, u32[]{:S(2)}, u32[]{:S(2)}) collective-permute-start(f32[1,128,512]{2,1,0:T(8,128)S(1)} %get-tuple-element.65), channel_id=1, source_target_pairs={{0,4},{4,8},{8,12},{12,16},{16,20},{20,24},{24,28},{28,32},{32,36}... | collective-permute-start | bytes 786440 | tf_op jit(solution)/shard_map/ppermute | solution.py:24
  10.7 4.7 %collective-permute-start.2 = (f32[4,1,512]{2,1,0:T(1,128)S(1)}, f32[4,1,512]{2,1,0:T(1,128)S(1)}, u32[]{:S(2)}, u32[]{:S(2)}) collective-permute-start(f32[4,1,512]{2,1,0:T(1,128)S(1)} %get-tuple-element.17), channel_id=1, source_target_pairs={{1,0},{2,1},{3,2},{5,4},{6,5},{7,6},{9,8},{10,9},{11,10},{13,12},{... | collective-permute-start | bytes 24584 | tf_op jit(solution)/shard_map/ppermute | solution.py:26
  13.4 5.5 %collective-permute-start.3 = (f32[4,1,512]{2,1,0:T(1,128)S(1)}, f32[4,1,512]{2,1,0:T(1,128)S(1)}, u32[]{:S(2)}, u32[]{:S(2)}) collective-permute-start(f32[4,1,512]{2,1,0:T(1,128)S(1)} %get-tuple-element.18), channel_id=1, source_target_pairs={{0,1},{1,2},{2,3},{4,5},{5,6},{6,7},{8,9},{9,10},{10,11},{12,13},{... | collective-permute-start | bytes 24584 | tf_op jit(solution)/shard_map/ppermute | solution.py:24
  21.1 4.6 %collective-permute-start.4 = (f32[1,128,512]{2,1,0:T(8,128)S(1)}, f32[1,128,512]{2,1,0:T(8,128)S(1)}, u32[]{:S(2)}, u32[]{:S(2)}) collective-permute-start(f32[1,128,512]{2,1,0:T(8,128)S(1)} %get-tuple-element.53), channel_id=1, source_target_pairs={{4,0},{8,4},{12,8},{16,12},{20,16},{24,20},{28,24},{32,28},{36,32}... | collective-permute-start | bytes 786440 | tf_op jit(solution)/shard_map/ppermute | solution.py:26
  22.4 4.2 %collective-permute-start.5 = (f32[1,128,512]{2,1,0:T(8,128)S(1)}, f32[1,128,512]{2,1,0:T(8,128)S(1)}, u32[]{:S(2)}, u32[]{:S(2)}) collective-permute-start(f32[1,128,512]{2,1,0:T(8,128)S(1)} %get-tuple-element.52), channel_id=1, source_target_pairs={{0,4},{4,8},{8,12},{12,16},{16,20},{20,24},{24,28},{28,32},{32,36}... | collective-permute-start | bytes 786440 | tf_op jit(solution)/shard_map/ppermute | solution.py:24
  26.6 7.7 %collective-permute-start.6 = (f32[4,1,512]{2,1,0:T(1,128)S(1)}, f32[4,1,512]{2,1,0:T(1,128)S(1)}, u32[]{:S(2)}, u32[]{:S(2)}) collective-permute-start(f32[4,1,512]{2,1,0:T(1,128)S(1)} %get-tuple-element.15), channel_id=1, source_target_pairs={{1,0},{2,1},{3,2},{5,4},{6,5},{7,6},{9,8},{10,9},{11,10},{13,12},{... | collective-permute-start | bytes 24584 | tf_op jit(solution)/shard_map/ppermute | solution.py:26
  32.9 5.5 %collective-permute-start.7 = (f32[4,1,512]{2,1,0:T(1,128)S(1)}, f32[4,1,512]{2,1,0:T(1,128)S(1)}, u32[]{:S(2)}, u32[]{:S(2)}) collective-permute-start(f32[4,1,512]{2,1,0:T(1,128)S(1)} %get-tuple-element.16), channel_id=1, source_target_pairs={{0,1},{1,2},{2,3},{4,5},{5,6},{6,7},{8,9},{9,10},{10,11},{12,13},{... | collective-permute-start | bytes 24584 | tf_op jit(solution)/shard_map/ppermute | solution.py:24
  39.5 6.6 %collective-permute-start.8 = (f32[1,128,512]{2,1,0:T(8,128)S(1)}, f32[1,128,512]{2,1,0:T(8,128)S(1)}, u32[]{:S(2)}, u32[]{:S(2)}) collective-permute-start(f32[1,128,512]{2,1,0:T(8,128)S(1)} %get-tuple-element.41), channel_id=1, source_target_pairs={{4,0},{8,4},{12,8},{16,12},{20,16},{24,20},{28,24},{32,28},{36,32}... | collective-permute-start | bytes 786440 | tf_op jit(solution)/shard_map/ppermute | solution.py:26
  40.8 6.2 %collective-permute-start.9 = (f32[1,128,512]{2,1,0:T(8,128)S(1)}, f32[1,128,512]{2,1,0:T(8,128)S(1)}, u32[]{:S(2)}, u32[]{:S(2)}) collective-permute-start(f32[1,128,512]{2,1,0:T(8,128)S(1)} %get-tuple-element.40), channel_id=1, source_target_pairs={{0,4},{4,8},{8,12},{12,16},{16,20},{20,24},{24,28},{28,32},{32,36}... | collective-permute-start | bytes 786440 | tf_op jit(solution)/shard_map/ppermute | solution.py:24
  47.0 5.0 %collective-permute-start.10 = (f32[4,1,512]{2,1,0:T(1,128)S(1)}, f32[4,1,512]{2,1,0:T(1,128)S(1)}, u32[]{:S(2)}, u32[]{:S(2)}) collective-permute-start(f32[4,1,512]{2,1,0:T(1,128)S(1)} %get-tuple-element.13), channel_id=1, source_target_pairs={{1,0},{2,1},{3,2},{5,4},{6,5},{7,6},{9,8},{10,9},{11,10},{13,12},{... | collective-permute-start | bytes 24584 | tf_op jit(solution)/shard_map/ppermute | solution.py:26
  50.6 5.5 %collective-permute-start.11 = (f32[4,1,512]{2,1,0:T(1,128)S(1)}, f32[4,1,512]{2,1,0:T(1,128)S(1)}, u32[]{:S(2)}, u32[]{:S(2)}) collective-permute-start(f32[4,1,512]{2,1,0:T(1,128)S(1)} %get-tuple-element.14), channel_id=1, source_target_pairs={{0,1},{1,2},{2,3},{4,5},{5,6},{6,7},{8,9},{9,10},{10,11},{12,13},{... | collective-permute-start | bytes 24584 | tf_op jit(solution)/shard_map/ppermute | solution.py:24
  69.8 11.6 %collective-permute-start.12 = (f32[1,128,512]{2,1,0:T(8,128)S(1)}, f32[1,128,512]{2,1,0:T(8,128)S(1)}, u32[]{:S(2)}, u32[]{:S(2)}) collective-permute-start(f32[1,128,512]{2,1,0:T(8,128)S(1)} %get-tuple-element.29), channel_id=1, source_target_pairs={{4,0},{8,4},{12,8},{16,12},{20,16},{24,20},{28,24},{32,28},{36,32}... | collective-permute-start | bytes 786440 | tf_op jit(solution)/shard_map/ppermute | solution.py:26
  71.1 10.4 %collective-permute-start.13 = (f32[1,128,512]{2,1,0:T(8,128)S(1)}, f32[1,128,512]{2,1,0:T(8,128)}, u32[]{:S(2)}, u32[]{:S(2)}) collective-permute-start(f32[1,128,512]{2,1,0:T(8,128)S(1)} %get-tuple-element.28), channel_id=1, source_target_pairs={{0,4},{4,8},{8,12},{12,16},{16,20},{20,24},{24,28},{28,32},{32,36}... | collective-permute-start | bytes 786440 | tf_op jit(solution)/shard_map/ppermute | solution.py:24
  81.5 8.6 %copy-start.6 = (f32[2,128,1]{2,1,0:T(8,128)S(1)}, f32[2,128,1]{2,1,0:T(8,128)}, u32[]{:S(2)}) copy-start(f32[2,128,1]{2,1,0:T(8,128)} %get-tuple-element.33) | copy-start | bytes 3076
  82.3 3.8 %collective-permute-start.14 = (f32[4,1,512]{2,1,0:T(1,128)S(1)}, f32[4,1,512]{2,1,0:T(1,128)S(1)}, u32[]{:S(2)}, u32[]{:S(2)}) collective-permute-start(f32[4,1,512]{2,1,0:T(1,128)S(1)} %get-tuple-element.11), channel_id=1, source_target_pairs={{1,0},{2,1},{3,2},{5,4},{6,5},{7,6},{9,8},{10,9},{11,10},{13,12},{... | collective-permute-start | bytes 24584 | tf_op jit(solution)/shard_map/ppermute | solution.py:26
  84.5 5.5 %collective-permute-start.15 = (f32[4,1,512]{2,1,0:T(1,128)S(1)}, f32[4,1,512]{2,1,0:T(1,128)S(1)}, u32[]{:S(2)}, u32[]{:S(2)}) collective-permute-start(f32[4,1,512]{2,1,0:T(1,128)S(1)} %get-tuple-element.12), channel_id=1, source_target_pairs={{0,1},{1,2},{2,3},{4,5},{5,6},{6,7},{8,9},{9,10},{10,11},{12,13},{... | collective-permute-start | bytes 24584 | tf_op jit(solution)/shard_map/ppermute | solution.py:24
  125.9 1.9 copy-start.3
  125.9 1.9 copy-start.4
  128.2 5.7 %collective-permute-start.16 = (f32[4,64,1,512]{3,1,0,2:T(8,128)S(1)}, f32[4,64,1,512]{3,1,0,2:T(8,128)S(1)}, u32[]{:S(2)}, u32[]{:S(2)}) collective-permute-start(f32[4,64,1,512]{3,1,0,2:T(8,128)S(1)} %select_bitcast_fusion), channel_id=1, source_target_pairs={{0,4},{4,0},{8,12},{12,8},{16,20},{20,16},{24,28},{28,24},{32,36},... | collective-permute-start | bytes 1572872 | tf_op jit(solution)/shard_map/ppermute | solution.py:36
  134.7 12.8 %collective-permute-start.17 = (f32[4,32,1,512]{3,0,1,2:T(4,128)S(1)}, f32[4,32,1,512]{3,0,1,2:T(4,128)S(1)}, u32[]{:S(2)}, u32[]{:S(2)}) collective-permute-start(f32[4,32,1,512]{3,0,1,2:T(4,128)S(1)} %select_bitcast_fusion.1), channel_id=1, source_target_pairs={{0,8},{4,12},{8,0},{12,4},{16,24},{20,28},{24,16},{28,20},{32,40},... | collective-permute-start | bytes 786440 | tf_op jit(solution)/shard_map/ppermute | solution.py:36
  147.9 10.6 %collective-permute-start.18 = (f32[4,16,1,512]{3,0,1,2:T(4,128)S(1)}, f32[4,16,1,512]{3,0,1,2:T(4,128)S(1)}, u32[]{:S(2)}, u32[]{:S(2)}) collective-permute-start(f32[4,16,1,512]{3,0,1,2:T(4,128)S(1)} %select_bitcast_fusion.2), channel_id=1, source_target_pairs={{0,16},{4,20},{8,24},{12,28},{16,0},{20,4},{24,8},{28,12},{32,48},... | collective-permute-start | bytes 393224 | tf_op jit(solution)/shard_map/ppermute | solution.py:36
  158.6 10.5 %collective-permute-start.19 = (f32[4,8,1,512]{3,0,1,2:T(4,128)S(1)}, f32[4,8,1,512]{3,0,1,2:T(4,128)S(1)}, u32[]{:S(2)}, u32[]{:S(2)}) collective-permute-start(f32[4,8,1,512]{3,0,1,2:T(4,128)S(1)} %select_bitcast_fusion.3), channel_id=1, source_target_pairs={{0,32},{4,36},{8,40},{12,44},{16,48},{20,52},{24,56},{28,60},{32,0... | collective-permute-start | bytes 196616 | tf_op jit(solution)/shard_map/ppermute | solution.py:36
  169.3 11.8 %collective-permute-start.20 = (f32[4,4,1,512]{3,0,1,2:T(4,128)S(1)}, f32[4,4,1,512]{3,0,1,2:T(4,128)S(1)}, u32[]{:S(2)}, u32[]{:S(2)}) collective-permute-start(f32[4,4,1,512]{3,0,1,2:T(4,128)S(1)} %select_bitcast_fusion.4), channel_id=1, source_target_pairs={{0,64},{4,68},{8,72},{12,76},{16,80},{20,84},{24,88},{28,92},{32,9... | collective-permute-start | bytes 98312 | tf_op jit(solution)/shard_map/ppermute | solution.py:36
  181.3 7.9 %collective-permute-start.21 = (f32[4,2,1,512]{3,2,1,0:T(1,128)S(1)}, f32[4,2,1,512]{3,2,1,0:T(1,128)S(1)}, u32[]{:S(2)}, u32[]{:S(2)}) collective-permute-start(f32[4,2,1,512]{3,2,1,0:T(1,128)S(1)} %fusion.11), channel_id=1, source_target_pairs={{0,128},{4,132},{8,136},{12,140},{16,144},{20,148},{24,152},{28,15... | collective-permute-start | bytes 49160 | tf_op jit(solution)/shard_map/ppermute | solution.py:36
  189.3 15.7 %collective-permute-start.22 = (f32[4,1,1,512]{3,1,2,0:T(1,128)S(1)}, f32[4,1,1,512]{3,1,2,0:T(1,128)S(1)}, u32[]{:S(2)}, u32[]{:S(2)}) collective-permute-start(f32[4,1,1,512]{3,1,2,0:T(1,128)S(1)} %fusion.16), channel_id=1, source_target_pairs={{0,256},{4,260},{8,264},{12,268},{16,272},{20,276},{24,280},{28,28... | collective-permute-start | bytes 24584 | tf_op jit(solution)/shard_map/ppermute | solution.py:36
where the time goes:
time: 207 us; the launch traced here: 206 us
  starting transfers between devices  97.5 us (47%)
  other arithmetic  55.5 us (27%)
  waiting for transfers between devices  40.1 us (19%)
  local copies, waits for them, and re-layouts  11.6 us (6%)
    ppermute x7, starting transfers between devices, partner(): return lax.ppermute(value, axis, pairs)  52.3 us
    another operation x4, other arithmetic, appearance(): jnp.stack([mixed[0] * shading, mixed[1] * shading, mixed[2] * shading])  35.6 us
    ppermute x8, starting transfers between devices, extended(): lax.ppermute(tail, axis, [(i, (i + 1) % count) for i in range(ends)])  25.1 us
    ppermute x7, waiting for transfers between devices, partner(): return lax.ppermute(value, axis, pairs)  22.5 us
    ppermute x8, starting transfers between devices, extended(): lax.ppermute(head, axis, [((i + 1) % count, i) for i in range(ends)])  20.2 us
    ppermute x8, waiting for transfers between devices, extended(): lax.ppermute(tail, axis, [(i, (i + 1) % count) for i in range(ends)])  17.6 us
    sub x1, other arithmetic, appearance(): opacity = 1.0 - jnp.exp(-mixed[3] * (OPTICAL_DEPTH / depth_count))  12.8 us
  transfers between devices with their start and end apart: 23, of which 13 were waited for; matrix products, arithmetic and copies ran while one was open for 3% of the time, Pallas kernels for 0%

commit v1 on v0

v1 whole, which is shorter than its diff:
```python
import jax
import jax.numpy as jnp
from jax import lax
from jax.experimental import pallas as pl
from jax.experimental.pallas import tpu as pltpu
from jax.sharding import PartitionSpec as P


PASSES = 3
KNOTS = 16
TIME_STEP = 0.15
OPTICAL_DEPTH = 3.0
UPPER_DENSITY = 6.0
AMBIENT = 0.35

GROUP = 16
BLOCKS = 8
HALO = 4
BAND = 128
COLS = 512
TILE = COLS // GROUP
WIDE = TILE + 2 * HALO
SEGS = 3
SEG_ROWS = 48
PLANES = 2
DEEP = GROUP * PLANES
LANES = 128
VMEM = pltpu.VMEM


def lane_index(shape):
    return lax.broadcasted_iota(jnp.int32, shape, 1)


def pack_kernel(own, above, below, out, ext):
    band = lax.axis_index("rows")
    bands = lax.axis_size("rows")
    for p in range(PLANES):
        ext[p, HALO : HALO + BAND, :] = own[p]
        ext[p, HALO + BAND :, :] = jnp.zeros((SEGS * SEG_ROWS - HALO - BAND, COLS), jnp.float32)

    @pl.when(band > 0)
    def _():
        for p in range(PLANES):
            ext[p, 0:HALO, :] = above[p, 8 - HALO : 8, :]

    @pl.when(band == 0)
    def _():
        for p in range(PLANES):
            for i in range(HALO):
                ext[p, HALO - 1 - i : HALO - i, :] = own[p, i : i + 1, :]

    @pl.when(band < bands - 1)
    def _():
        for p in range(PLANES):
            ext[p, HALO + BAND : 2 * HALO + BAND, :] = below[p, 0:HALO, :]

    @pl.when(band == bands - 1)
    def _():
        for p in range(PLANES):
            for i in range(HALO):
                row = HALO + BAND + i
                ext[p, row : row + 1, :] = own[p, BAND - 1 - i : BAND - i, :]

    lane = lane_index((8, LANES))

    def step(it, carry):
        p = it // 6
        j = it - 6 * p
        tiles = []
        for k in range(SEGS):
            start = pl.multiple_of(SEG_ROWS * k + 8 * j, 8)
            tiles.append([ext[p, pl.ds(start, 8), LANES * q : LANES * (q + 1)] for q in range(4)])
        for t in range(GROUP):
            q, m = divmod(t, 4)
            parts = []
            for k in range(SEGS):
                x = tiles[k][q]
                if m == 0 and q > 0:
                    x = jnp.where(lane >= LANES - HALO, tiles[k][q - 1], x)
                if m == 3 and q < 3:
                    x = jnp.where(lane < HALO, tiles[k][q + 1], x)
                parts.append(pltpu.roll(x, (WIDE * k - TILE * m + HALO) % LANES, 1))
            value = jnp.where(lane < WIDE, parts[0], jnp.where(lane < 2 * WIDE, parts[1], parts[2]))
            out[t, p, pl.ds(pl.multiple_of(8 * j, 8), 8), :] = value
        return carry

    lax.fori_loop(0, PLANES * 6, step, 0)


def next_row(f, lane):
    moved = pltpu.roll(f, SEG_ROWS - 1, 0)
    last = moved[SEG_ROWS - 8 :]
    row = lax.broadcasted_iota(jnp.int32, (8, LANES), 0)
    last = jnp.where(row == 7, pltpu.roll(last, LANES - WIDE, 1), last)
    return jnp.concatenate([moved[: SEG_ROWS - 8], last], axis=0)


def prev_row(f, lane):
    moved = pltpu.roll(f, 1, 0)
    first = moved[:8]
    row = lax.broadcasted_iota(jnp.int32, (8, LANES), 0)
    first = jnp.where(row == 0, pltpu.roll(first, WIDE, 1), first)
    return jnp.concatenate([first, moved[8:]], axis=0)


def flux(change):
    return change / (1.0 + change * change)


def render_kernel(mine, before, after, table, out, fa, fb):
    block = lax.axis_index("depth") // GROUP
    tile = lax.axis_index("depth") % GROUP
    lane = lane_index((SEG_ROWS, LANES))
    column = lane % WIDE
    first_tile = tile == 0
    last_tile = tile == GROUP - 1
    at_first = jnp.logical_and(column == HALO, first_tile)
    at_last = jnp.logical_and(column == HALO + TILE - 1, last_tile)
    open_face = jnp.where(
        jnp.logical_or(at_last, jnp.logical_and(column == HALO - 1, first_tile)), 0.0, 1.0
    )

    for i in range(GROUP):
        for p in range(PLANES):
            fa[HALO + PLANES * i + p] = mine[i, p]

    @pl.when(block > 0)
    def _():
        for i in range(HALO):
            fa[i] = before[i // 2, i % 2]

    @pl.when(block == 0)
    def _():
        for i in range(HALO):
            fa[HALO - 1 - i] = mine[i // 2, i % 2]

    @pl.when(block < BLOCKS - 1)
    def _():
        for i in range(HALO):
            fa[HALO + DEEP + i] = after[i // 2, i % 2]

    @pl.when(block == BLOCKS - 1)
    def _():
        for i in range(HALO):
            d = DEEP - 1 - i
            fa[HALO + DEEP + i] = mine[d // 2, d % 2]

    src, dst = fa, fb
    for sweep in range(PASSES):
        lo, hi = sweep + 1, DEEP + 2 * HALO - 1 - sweep

        def step(p, flux_nearer, src=src, dst=dst):
            f = src[p]
            flux_deeper = flux(src[p + 1] - f)
            row = flux(next_row(f, lane) - f)
            col = flux((pltpu.roll(f, LANES - 1, 1) - f) * open_face)
            total = flux_deeper - flux_nearer
            total = total + (row - prev_row(row, lane))
            total = total + (col - pltpu.roll(col, 1, 1))
            dst[p] = f + TIME_STEP * total
            return flux_deeper

        lax.fori_loop(lo, hi, step, flux(src[lo] - src[lo - 1]))
        src, dst = dst, src

    base = [jnp.broadcast_to(table[c : c + 1, :], (8, LANES)) for c in range(4)]
    slope = [pltpu.roll(base[c], LANES - 1, 1) - base[c] for c in range(4)]

    def lookup(k, part):
        return jnp.concatenate(
            [
                jnp.take_along_axis(part, k[8 * j : 8 * j + 8], axis=1)
                for j in range(SEG_ROWS // 8)
            ],
            axis=0,
        )

    def shade(p, carry):
        red, green, blue, remaining = carry
        f = src[p]
        grad_depth = (src[p + 1] - src[p - 1]) * 0.5
        grad_row = (next_row(f, lane) - prev_row(f, lane)) * 0.5
        right = jnp.where(at_last, f, pltpu.roll(f, LANES - 1, 1))
        left = jnp.where(at_first, f, pltpu.roll(f, 1, 1))
        grad_col = (right - left) * 0.5
        square = grad_depth * grad_depth + grad_row * grad_row + grad_col * grad_col + 0.25
        along = jnp.abs(0.64 * grad_depth + 0.6 * grad_row + 0.48 * grad_col)
        shading = AMBIENT + (1.0 - AMBIENT) * along * lax.rsqrt(square)
        position = f * ((KNOTS - 1) / UPPER_DENSITY) + 1.0
        position = jnp.clip(position, 0.0, KNOTS + 1.0)
        whole = jnp.minimum(jnp.floor(position), float(KNOTS))
        frac = position - whole
        k = whole.astype(jnp.int32)
        mixed = [lookup(k, base[c]) + frac * lookup(k, slope[c]) for c in range(4)]
        kept = jnp.exp(mixed[3] * (-OPTICAL_DEPTH / (DEEP * BLOCKS)))
        weight = remaining * (1.0 - kept) * shading
        return (
            red + weight * mixed[0],
            green + weight * mixed[1],
            blue + weight * mixed[2],
            remaining * kept,
        )

    zero = jnp.zeros((SEG_ROWS, LANES), jnp.float32)
    sums = lax.fori_loop(
        HALO, HALO + DEEP, shade, (zero, zero, zero, jnp.ones_like(zero))
    )
    lanes = lane_index((SEG_ROWS, LANES))
    for k in range(SEGS):
        value = None
        for c in range(4):
            moved = pltpu.roll(sums[c], (TILE * c - WIDE * k - HALO) % LANES, 1)
            value = moved if value is None else jnp.where(lanes >= TILE * c, moved, value)
        first = SEG_ROWS * k - HALO
        lo, hi = max(first, 0), min(first + SEG_ROWS, BAND)
        out[lo:hi, :] = value[lo - first : hi - first]


def gather_kernel(parts, out):
    lane = lane_index((GROUP, LANES))
    total = jnp.zeros((GROUP, LANES), jnp.float32)
    remaining = jnp.ones((GROUP, LANES), jnp.float32)
    for b in range(BLOCKS):
        v = parts[GROUP * b : GROUP * (b + 1)]
        kept = v
        for c in range(3):
            kept = jnp.where(
                jnp.logical_and(lane >= TILE * c, lane < TILE * (c + 1)),
                pltpu.roll(v, TILE * (c + 1), 1),
                kept,
            )
        total = total + remaining * v
        remaining = remaining * kept
    total = jnp.where(lane >= 3 * TILE, 1.0 - remaining, total)
    turned = [total] + [pltpu.roll(total, TILE * s, 1) for s in range(1, 4)]
    for c in range(4):
        for t in range(GROUP):
            m = t % 4
            out[c, :, TILE * t : TILE * (t + 1)] = turned[(m - c) % 4][
                t : t + 1, TILE * m : TILE * (m + 1)
            ]


def call(kernel, shape, scratch, *operands):
    spec = pl.BlockSpec(memory_space=VMEM)
    return pl.pallas_call(
        kernel,
        out_shape=jax.ShapeDtypeStruct(shape, jnp.float32),
        in_specs=[spec] * len(operands),
        out_specs=spec,
        scratch_shapes=scratch,
        name=kernel.__name__,
    )(*operands)


def shifted(value, axis, by):
    size = lax.axis_size(axis)
    pairs = [(i, i + by) for i in range(size) if 0 <= i + by < size]
    return lax.ppermute(value, axis, pairs)


def per_device(density, transfer_table):
    above = shifted(density[:, BAND - 8 :], "rows", 1)
    below = shifted(density[:, :8], "rows", -1)
    rows = SEGS * SEG_ROWS
    sent = call(
        pack_kernel,
        (GROUP, PLANES, SEG_ROWS, LANES),
        [VMEM((PLANES, rows, COLS), jnp.float32)],
        density,
        above,
        below,
    )
    groups = [[GROUP * b + i for i in range(GROUP)] for b in range(BLOCKS)]
    mine = lax.all_to_all(sent, "depth", 0, 0, axis_index_groups=groups, tiled=True)
    near = HALO // PLANES
    before = shifted(mine[GROUP - near :], "depth", GROUP)
    after = shifted(mine[:near], "depth", -GROUP)
    table = jnp.pad(transfer_table, ((0, 4), (1, LANES - KNOTS - 1)))
    field = VMEM((DEEP + 2 * HALO, SEG_ROWS, LANES), jnp.float32)
    partial = call(
        render_kernel, (BAND, LANES), [field, field], mine, before, after, table
    )
    parts = lax.all_to_all(partial, "depth", 0, 0, tiled=True)
    return call(gather_kernel, (4, 1, COLS), [], parts)


def solution(mesh):
    placed = (P("depth", "rows", None), P())
    return jax.shard_map(
        per_device,
        mesh=mesh,
        in_specs=placed,
        out_specs=P(None, ("rows", "depth"), None),
        check_vma=False,
    )
```

time: 207 us -> 110 us (0.53)
  the two profiles are of different devices: /device:TPU:6 before, /device:TPU:1 now
where the time goes in v1:
time: 110 us; the launch traced here: 109 us
  blocking collectives  55.4 us (50%)
  Pallas kernels  31.7 us (29%)
  starting transfers between devices  10.6 us (10%)
  waiting for transfers between devices  8.62 us (8%)
  local copies, waits for them, and re-layouts  2.71 us (2%)
    all_to_all x1, blocking collectives, per_device(): lax.all_to_all(sent, 'depth', 0, 0, axis_index_groups=groups, tiled=True)  32 us
    pallas_call x3, Pallas kernels, call(): pl.pallas_call(kernel, out_shape=jax.ShapeDtypeStruct(shape, jnp.float32)...  31.7 us
    all_to_all x1, blocking collectives, per_device(): parts = lax.all_to_all(partial, 'depth', 0, 0, tiled=True)  23.3 us
    ppermute x4, starting transfers between devices, shifted(): return lax.ppermute(value, axis, pairs)  10.6 us
    ppermute x4, waiting for transfers between devices, shifted(): return lax.ppermute(value, axis, pairs)  8.62 us
  transfers between devices with their start and end apart: 4, of which 3 were waited for; matrix products, arithmetic and copies ran while one was open for 1% of the time, Pallas kernels for 0%

profile of v1, /device:TPU:1, one launch (start us, length us, event | category | flops | bytes accessed | tf_op | source)
XLA Modules:
  0.0 109.1 jit_solution(9820185499248891637)
XLA Ops:
  0.0 0.8 fusion.1
  0.8 3.9 %collective-permute-start = (f32[2,8,512]{2,1,0:T(8,128)S(1)}, f32[2,8,512]{2,1,0:T(8,128)S(1)}, u32[]{:S(2)}, u32[]{:S(2)}) collective-permute-start(f32[2,8,512]{2,1,0:T(8,128)S(1)} %get-tuple-element.8), channel_id=1, source_target_pairs={{0,1},{1,2},{2,3},{4,5},{5,6},{6,7},{8,9},{9,10},{10,11},{12,13},{... | collective-permute-start | bytes 98312 | tf_op jit(solution)/shard_map/ppermute | solution.py:260
  4.7 1.3 %collective-permute-start.1 = (f32[2,8,512]{2,1,0:T(8,128)S(1)}, f32[2,8,512]{2,1,0:T(8,128)S(1)}, u32[]{:S(2)}, u32[]{:S(2)}) collective-permute-start(f32[2,8,512]{2,1,0:T(8,128)S(1)} %get-tuple-element.7), channel_id=1, source_target_pairs={{1,0},{2,1},{3,2},{5,4},{6,5},{7,6},{9,8},{10,9},{11,10},{13,12},{... | collective-permute-start | bytes 98312 | tf_op jit(solution)/shard_map/ppermute | solution.py:260
  6.0 0.0 collective-permute-done.above
  6.0 0.0 copy-start.3
  6.0 3.3 %collective-permute-done.1.below = f32[2,8,512]{2,1,0:T(8,128)S(1)} collective-permute-done((f32[2,8,512]{2,1,0:T(8,128)S(1)}, f32[2,8,512]{2,1,0:T(8,128)S(1)}, u32[]{:S(2)}, u32[]{:S(2)}) %collective-permute-start.1) | collective-permute-done | bytes 32800 | tf_op jit(solution)/shard_map/ppermute | solution.py:260
  9.4 0.0 copy-done.3
  9.4 0.0 copy-start.4
  9.4 0.6 copy-done.4
  10.0 3.5 %pack_kernel.1 = f32[16,2,48,128]{3,2,1,0:T(8,128)} custom-call(f32[2,128,512]{2,1,0:T(8,128)} %own.1, f32[2,8,512]{2,1,0:T(8,128)} %copy-done.3, f32[2,8,512]{2,1,0:T(8,128)} %copy-done.4), custom_call_target="tpu_custom_call" | custom-call | tf_op jit(solution)/shard_map/pack_kernel/pallas_call | solution.py:247
  13.5 32.0 %all_to_all.16.mine = f32[16,2,48,128]{3,2,1,0:T(8,128)S(1)} all-to-all(f32[16,2,48,128]{3,2,1,0:T(8,128)} %pack_kernel.1), channel_id=1, replica_groups={{0,4,8,12,16,20,24,28,32,36,40,44,48,52,56,60},{64,68,72,76,80,84,88,92..., dimensions={0} | all-to-all | bytes 1572864 | tf_op jit(solution)/shard_map/all_to_all | solution.py:276
  45.5 0.0 copy-start
  45.6 0.0 copy-start.5
  45.6 4.1 %collective-permute-start.2 = (f32[2,2,48,128]{3,2,1,0:T(8,128)S(1)}, f32[2,2,48,128]{3,2,1,0:T(8,128)S(1)}, u32[]{:S(2)}, u32[]{:S(2)}) collective-permute-start(f32[2,2,48,128]{3,2,1,0:T(8,128)S(1)} %get-tuple-element.6), channel_id=1, source_target_pairs={{0,64},{4,68},{8,72},{12,76},{16,80},{20,84},{24,88},{28,92},{32,9... | collective-permute-start | bytes 294920 | tf_op jit(solution)/shard_map/ppermute | solution.py:260
  49.7 1.3 %collective-permute-start.3 = (f32[2,2,48,128]{3,2,1,0:T(8,128)S(1)}, f32[2,2,48,128]{3,2,1,0:T(8,128)S(1)}, u32[]{:S(2)}, u32[]{:S(2)}) collective-permute-start(f32[2,2,48,128]{3,2,1,0:T(8,128)S(1)} %get-tuple-element.5), channel_id=1, source_target_pairs={{64,0},{68,4},{72,8},{76,12},{80,16},{84,20},{88,24},{92,28},{96,3... | collective-permute-start | bytes 294920 | tf_op jit(solution)/shard_map/ppermute | solution.py:260
  51.0 0.0 copy-done.5
  51.0 0.7 pad.4.table
  51.7 0.5 collective-permute-done.2.before
  52.2 0.0 copy-start.1
  52.2 4.8 %collective-permute-done.3.after = f32[2,2,48,128]{3,2,1,0:T(8,128)S(1)} collective-permute-done((f32[2,2,48,128]{3,2,1,0:T(8,128)S(1)}, f32[2,2,48,128]{3,2,1,0:T(8,128)S(1)}, u32[]{:S(2)}, u32[]{:S(2)}) %collective-permute-start.3) | collective-permute-done | bytes 98336 | tf_op jit(solution)/shard_map/ppermute | solution.py:260
  57.0 0.0 copy-done
  57.0 0.0 copy-done.1
  57.0 0.0 copy-start.2
  57.0 0.6 copy-done.2
  57.6 26.5 %render_kernel.1 = f32[128,128]{1,0:T(8,128)} custom-call(f32[16,2,48,128]{3,2,1,0:T(8,128)} %copy-done, f32[2,2,48,128]{3,2,1,0:T(8,128)} %copy-done.1, f32[2,2,48,128]{3,2,1,0:T(8,128)} %copy-done.2, f32[8,128]{1,0:T(8,128)} %pad.4.table), custom_call_target="tpu_custom_call" | custom-call | tf_op jit(solution)/shard_map/render_kernel/pallas_call | solution.py:247
  84.1 23.3 %all_to_all.17 = f32[128,1,128]{2,1,0:T(1,128)} all-to-all(f32[128,1,128]{2,1,0:T(1,128)} %bitcast.4), channel_id=1, replica_groups=mesh['depth'=128,'rows'=4] {'depth'}, dimensions={0} | all-to-all | bytes 131072 | tf_op jit(solution)/shard_map/all_to_all | solution.py:285
  107.5 1.6 %gather_kernel.1 = f32[4,1,512]{2,1,0:T(1,128)} custom-call(f32[128,128]{1,0:T(8,128)} %bitcast.5), custom_call_target="tpu_custom_call" | custom-call | tf_op jit(solution)/shard_map/gather_kernel/pallas_call | solution.py:247
  (1 shorter events, 0.0 us)
Async XLA Ops:
  0.8 5.2 %collective-permute-start = (f32[2,8,512]{2,1,0:T(8,128)S(1)}, f32[2,8,512]{2,1,0:T(8,128)S(1)}, u32[]{:S(2)}, u32[]{:S(2)}) collective-permute-start(f32[2,8,512]{2,1,0:T(8,128)S(1)} %get-tuple-element.8), channel_id=1, source_target_pairs={{0,1},{1,2},{2,3},{4,5},{5,6},{6,7},{8,9},{9,10},{10,11},{12,13},{... | collective-permute-start | bytes 98312 | tf_op jit(solution)/shard_map/ppermute | solution.py:260
  4.7 4.7 %collective-permute-start.1 = (f32[2,8,512]{2,1,0:T(8,128)S(1)}, f32[2,8,512]{2,1,0:T(8,128)S(1)}, u32[]{:S(2)}, u32[]{:S(2)}) collective-permute-start(f32[2,8,512]{2,1,0:T(8,128)S(1)} %get-tuple-element.7), channel_id=1, source_target_pairs={{1,0},{2,1},{3,2},{5,4},{6,5},{7,6},{9,8},{10,9},{11,10},{13,12},{... | collective-permute-start | bytes 98312 | tf_op jit(solution)/shard_map/ppermute | solution.py:260
  6.0 3.4 %copy-start.3 = (f32[2,8,512]{2,1,0:T(8,128)}, f32[2,8,512]{2,1,0:T(8,128)S(1)}, u32[]{:S(2)}) copy-start(f32[2,8,512]{2,1,0:T(8,128)S(1)} %collective-permute-done.above) | copy-start | bytes 98308
  9.4 0.6 copy-start.4
  45.5 11.4 %copy-start = (f32[16,2,48,128]{3,2,1,0:T(8,128)}, f32[16,2,48,128]{3,2,1,0:T(8,128)S(1)}, u32[]{:S(2)}) copy-start(f32[16,2,48,128]{3,2,1,0:T(8,128)S(1)} %all_to_all.16.mine) | copy-start | bytes 2359300
  45.6 5.5 %copy-start.5 = (f32[4,16]{1,0:T(4,128)S(1)}, f32[4,16]{1,0:T(4,128)}, u32[]{:S(2)}) copy-start(f32[4,16]{1,0:T(4,128)} %param.3) | copy-start | bytes 772
  45.6 6.6 %collective-permute-start.2 = (f32[2,2,48,128]{3,2,1,0:T(8,128)S(1)}, f32[2,2,48,128]{3,2,1,0:T(8,128)S(1)}, u32[]{:S(2)}, u32[]{:S(2)}) collective-permute-start(f32[2,2,48,128]{3,2,1,0:T(8,128)S(1)} %get-tuple-element.6), channel_id=1, source_target_pairs={{0,64},{4,68},{8,72},{12,76},{16,80},{20,84},{24,88},{28,92},{32,9... | collective-permute-start | bytes 294920 | tf_op jit(solution)/shard_map/ppermute | solution.py:260
  49.7 7.3 %collective-permute-start.3 = (f32[2,2,48,128]{3,2,1,0:T(8,128)S(1)}, f32[2,2,48,128]{3,2,1,0:T(8,128)S(1)}, u32[]{:S(2)}, u32[]{:S(2)}) collective-permute-start(f32[2,2,48,128]{3,2,1,0:T(8,128)S(1)} %get-tuple-element.5), channel_id=1, source_target_pairs={{64,0},{68,4},{72,8},{76,12},{80,16},{84,20},{88,24},{92,28},{96,3... | collective-permute-start | bytes 294920 | tf_op jit(solution)/shard_map/ppermute | solution.py:260
  52.2 4.8 %copy-start.1 = (f32[2,2,48,128]{3,2,1,0:T(8,128)}, f32[2,2,48,128]{3,2,1,0:T(8,128)S(1)}, u32[]{:S(2)}) copy-start(f32[2,2,48,128]{3,2,1,0:T(8,128)S(1)} %collective-permute-done.2.before) | copy-start | bytes 294916
  57.0 0.6 copy-start.2

commit v2 on v1

v2 whole, which is shorter than its diff:
```python
import jax
import jax.numpy as jnp
from jax import lax
from jax.experimental import pallas as pl
from jax.experimental.pallas import tpu as pltpu
from jax.sharding import PartitionSpec as P


PASSES = 3
KNOTS = 16
TIME_STEP = 0.15
OPTICAL_DEPTH = 3.0
UPPER_DENSITY = 6.0
AMBIENT = 0.35

GROUP = 16
BLOCKS = 8
HALO = 4
BAND = 128
COLS = 512
TILE = COLS // GROUP
WIDE = TILE + 2 * HALO
SEGS = 3
SEG_ROWS = 48
TILES = SEG_ROWS // 8
PLANES = 2
DEEP = GROUP * PLANES
LANES = 128
TOP = 8
TALL = SEG_ROWS + 2 * TOP
EDGE = 4
VMEM = pltpu.VMEM


def lane_index(rows=8):
    return lax.broadcasted_iota(jnp.int32, (rows, LANES), 1)


def pack_kernel(own, above, below, out, ext):
    band = lax.axis_index("rows")
    bands = lax.axis_size("rows")
    rows = SEGS * SEG_ROWS
    for p in range(PLANES):
        ext[p, HALO : HALO + BAND, :] = own[p]
        ext[p, rows - 8 :, :] = jnp.zeros((8, COLS), jnp.float32)

    @pl.when(band > 0)
    def _():
        for p in range(PLANES):
            ext[p, 0:HALO, :] = above[p, 8 - HALO : 8, :]

    @pl.when(band == 0)
    def _():
        for p in range(PLANES):
            for i in range(HALO):
                ext[p, HALO - 1 - i : HALO - i, :] = own[p, i : i + 1, :]

    @pl.when(band < bands - 1)
    def _():
        for p in range(PLANES):
            ext[p, HALO + BAND : 2 * HALO + BAND, :] = below[p, 0:HALO, :]

    @pl.when(band == bands - 1)
    def _():
        for p in range(PLANES):
            for i in range(HALO):
                row = HALO + BAND + i
                ext[p, row : row + 1, :] = own[p, BAND - 1 - i : BAND - i, :]

    lane = lane_index()
    segment, left, right = [], [], []
    for m in range(4):
        local = (lane - (TILE * m - HALO)) % LANES
        segment.append((local < WIDE, local < 2 * WIDE))
        column = local % WIDE
        left.append(column < HALO)
        right.append(column >= WIDE - HALO)

    def step(it, carry):
        p = it // TILES
        j = it - TILES * p
        rolled = []
        for k in range(SEGS):
            start = pl.multiple_of(SEG_ROWS * k + 8 * j, 8)
            row = [ext[p, pl.ds(start, 8), LANES * q : LANES * (q + 1)] for q in range(4)]
            rolled.append([pltpu.roll(x, WIDE * k, 1) if k else x for x in row])

        def joined(q, m):
            first, second = segment[m]
            return jnp.where(
                first, rolled[0][q], jnp.where(second, rolled[1][q], rolled[2][q])
            )

        for t in range(GROUP):
            q, m = divmod(t, 4)
            value = joined(q, m)
            if m == 0 and q > 0:
                value = jnp.where(left[m], joined(q - 1, m), value)
            if m == 3 and q < 3:
                value = jnp.where(right[m], joined(q + 1, m), value)
            out[t, p, pl.ds(pl.multiple_of(8 * j, 8), 8), :] = value
        return carry

    lax.fori_loop(0, PLANES * TILES, step, 0)


def flux(change):
    return change / (1.0 + change * change)


def rows_at(j, by=0):
    return slice(TOP + 8 * j + by, TOP + 8 * j + by + 8)


def put(ref, p, tiles):
    for j in range(TILES):
        ref[p, rows_at(j), :] = tiles[j]
    ref[p, TOP - 1 : TOP, :] = pltpu.roll(tiles[-1], WIDE, 1)[7:8]
    ref[p, TOP + SEG_ROWS : TOP + SEG_ROWS + 1, :] = pltpu.roll(tiles[0], LANES - WIDE, 1)[0:1]


def take(ref, p, by=0):
    return [ref[p, rows_at(j, by), :] for j in range(TILES)]


class Tile:
    def __init__(self):
        self.block = lax.axis_index("depth") // GROUP
        tile = lax.axis_index("depth") % GROUP
        self.start = TILE * (tile % 4) - HALO
        local = (lane_index() - self.start + LANES) % LANES
        column = local % WIDE
        first, last = tile == 0, tile == GROUP - 1
        self.at_first = jnp.logical_and(column == HALO, first)
        self.at_last = jnp.logical_and(column == HALO + TILE - 1, last)
        self.open_face = jnp.where(
            jnp.logical_or(self.at_last, jnp.logical_and(column == HALO - 1, first)), 0.0, 1.0
        )


def diffuse(src, p, dst, to, fluxes, slot, flux_nearer, tile):
    f = take(src, p)
    below = take(src, p, 1)
    deeper = take(src, p + 1)
    flux_deeper = [flux(deeper[j] - f[j]) for j in range(TILES)]
    row = [flux(below[j] - f[j]) for j in range(TILES)]
    for j in range(TILES):
        fluxes[slot, rows_at(j), :] = row[j]
    fluxes[slot, TOP - 1 : TOP, :] = pltpu.roll(row[-1], WIDE, 1)[7:8]
    row_prev = take(fluxes, slot, -1)
    new = []
    for j in range(TILES):
        col = flux((pltpu.roll(f[j], LANES - 1, 1) - f[j]) * tile.open_face)
        total = flux_deeper[j] - flux_nearer[j]
        total = total + (row[j] - row_prev[j])
        total = total + (col - pltpu.roll(col, 1, 1))
        new.append(f[j] + TIME_STEP * total)
    put(dst, to, new)
    return flux_deeper


def first_flux(src, p):
    here, deeper = take(src, p), take(src, p + 1)
    return [flux(deeper[j] - here[j]) for j in range(TILES)]


def tables(transfer, table):
    table[...] = jnp.zeros((8, LANES), jnp.float32)
    table[0:4, 1 : 1 + KNOTS] = transfer[...]
    base = [jnp.broadcast_to(table[c : c + 1, :], (8, LANES)) for c in range(4)]
    return base, [pltpu.roll(base[c], LANES - 1, 1) - base[c] for c in range(4)]


def shade(src, p, j, carry, lookup, tile):
    red, green, blue, remaining = carry
    base, slope = lookup
    f = src[p, rows_at(j), :]
    depth = src[p + 1, rows_at(j), :] - src[p - 1, rows_at(j), :]
    row = src[p, rows_at(j, 1), :] - src[p, rows_at(j, -1), :]
    right = jnp.where(tile.at_last, f, pltpu.roll(f, LANES - 1, 1))
    left = jnp.where(tile.at_first, f, pltpu.roll(f, 1, 1))
    col = right - left
    square = depth * depth + row * row + col * col + 1.0
    gain = 1.0 - AMBIENT
    along = jnp.abs(0.64 * gain * depth + 0.6 * gain * row + 0.48 * gain * col)
    shading = AMBIENT + along * lax.rsqrt(square)
    position = f * ((KNOTS - 1) / UPPER_DENSITY) + 1.0
    k = position.astype(jnp.int32)
    frac = position - k.astype(jnp.float32)
    mixed = [
        jnp.take_along_axis(base[c], k, axis=1)
        + frac * jnp.take_along_axis(slope[c], k, axis=1)
        for c in range(4)
    ]
    kept = jnp.exp(mixed[3] * (-OPTICAL_DEPTH / (DEEP * BLOCKS)))
    weight = remaining * (1.0 - kept) * shading
    return (
        red + weight * mixed[0],
        green + weight * mixed[1],
        blue + weight * mixed[2],
        remaining * kept,
    )


def inner_kernel(mine, transfer, out, fa, fb, fluxes, table):
    tile = Tile()
    zero = jnp.zeros((8, LANES), jnp.float32)

    def fill(i, carry):
        for p in range(PLANES):
            tiles = [mine[i, p, 8 * j : 8 * j + 8, :] for j in range(TILES)]
            put(fa, PLANES * i + p, tiles)
        return carry

    lax.fori_loop(0, GROUP, fill, 0)
    src, dst = fa, fb
    for sweep in range(PASSES):
        lo, hi = sweep + 1, DEEP - 1 - sweep

        def step(i, carry, src=src, dst=dst, lo=lo):
            for u in range(2):
                p = lo + 2 * i + u
                carry = diffuse(src, p, dst, p, fluxes, u, carry, tile)
            return carry

        lax.fori_loop(0, (hi - lo) // 2, step, first_flux(src, lo - 1))
        kept = (lo, lo + 1, hi - 2, hi - 1)
        for i in range(EDGE):
            for j in range(TILES):
                out[EDGE * sweep + i, 8 * j : 8 * j + 8, :] = dst[kept[i], rows_at(j), :]
        src, dst = dst, src

    lookup = tables(transfer, table)
    for j in range(TILES):

        def planes(i, carry, j=j):
            for u in range(4):
                carry = shade(src, HALO + 4 * i + u, j, carry, lookup, tile)
            return carry

        sums = lax.fori_loop(0, (DEEP - 2 * HALO) // 4, planes, (zero, zero, zero, zero + 1.0))
        for c in range(4):
            out[EDGE * PASSES + c, 8 * j : 8 * j + 8, :] = sums[c]


def outer_kernel(head, tail, before, after, inner, transfer, out, fa, fb, fluxes, table):
    tile = Tile()
    zero = jnp.zeros((8, LANES), jnp.float32)
    lookup = tables(transfer, table)

    def plane_of(ref, i):
        return [ref[i // 2, i % 2, 8 * j : 8 * j + 8, :] for j in range(TILES)]

    def inner_of(i):
        return [inner[i, 8 * j : 8 * j + 8, :] for j in range(TILES)]

    def side(front):
        inside = tile.block > 0 if front else tile.block < BLOCKS - 1
        own = 4 if front else 0
        halo = 0 if front else 2
        for i in range(2):
            put(fa, own + i, plane_of(head if front else tail, i if front else 2 + i))

        @pl.when(inside)
        def _():
            for i in range(HALO):
                put(fa, halo + i, plane_of(before if front else after, i))

        @pl.when(jnp.logical_not(inside))
        def _():
            for i in range(HALO):
                put(fa, halo + i, plane_of(head if front else tail, HALO - 1 - i))

        src, dst = fa, fb
        for sweep in range(PASSES):
            carry = first_flux(src, 0)
            for i in range(4):
                to = i if front else 2 + i
                carry = diffuse(src, i + 1, dst, to, fluxes, i, carry, tile)
            for i in range(2):
                put(dst, own + i, inner_of(EDGE * sweep + (i if front else 2 + i)))
            src, dst = dst, src
        return src

    src = side(True)
    sums = []
    for j in range(TILES):
        carry = (zero, zero, zero, zero + 1.0)
        for i in range(4):
            carry = shade(src, i + 1, j, carry, lookup, tile)
        mid = [inner[EDGE * PASSES + c, 8 * j : 8 * j + 8, :] for c in range(4)]
        remaining = carry[3]
        sums.append([carry[c] + remaining * mid[c] for c in range(3)] + [remaining * mid[3]])
    src = side(False)
    lane = lane_index()
    for j in range(TILES):
        carry = sums[j]
        for i in range(4):
            carry = shade(src, i + 1, j, carry, lookup, tile)
        for k in range(SEGS):
            value = None
            for c in range(4):
                by = TILE * c - WIDE * k - HALO - tile.start + LANES * 2
                moved = pltpu.roll(carry[c], lax.rem(by, LANES), 1)
                value = moved if value is None else jnp.where(lane >= TILE * c, moved, value)
            first = SEG_ROWS * k + 8 * j - HALO
            lo, hi = max(first, 0), min(first + 8, BAND)
            if lo < hi:
                out[lo:hi, :] = value[lo - first : hi - first]


def gather_kernel(parts, out):
    lane = lane_index(GROUP)
    total = jnp.zeros((GROUP, LANES), jnp.float32)
    remaining = jnp.ones((GROUP, LANES), jnp.float32)
    for b in range(BLOCKS):
        v = parts[GROUP * b : GROUP * (b + 1)]
        kept = v
        for c in range(3):
            kept = jnp.where(
                jnp.logical_and(lane >= TILE * c, lane < TILE * (c + 1)),
                pltpu.roll(v, TILE * (c + 1), 1),
                kept,
            )
        total = total + remaining * v
        remaining = remaining * kept
    total = jnp.where(lane >= 3 * TILE, 1.0 - remaining, total)
    turned = [total] + [pltpu.roll(total, TILE * s, 1) for s in range(1, 4)]
    for c in range(4):
        for t in range(GROUP):
            m = t % 4
            out[c, :, TILE * t : TILE * (t + 1)] = turned[(m - c) % 4][
                t : t + 1, TILE * m : TILE * (m + 1)
            ]


def call(kernel, shape, scratch, *operands):
    spec = pl.BlockSpec(memory_space=VMEM)
    return pl.pallas_call(
        kernel,
        out_shape=jax.ShapeDtypeStruct(shape, jnp.float32),
        in_specs=[spec] * len(operands),
        out_specs=spec,
        scratch_shapes=[VMEM(s, jnp.float32) for s in scratch],
        name=kernel.__name__,
    )(*operands)


def shifted(value, axis, by):
    size = lax.axis_size(axis)
    pairs = [(i, i + by) for i in range(size) if 0 <= i + by < size]
    return lax.ppermute(value, axis, pairs)


def per_device(density, transfer_table):
    above = shifted(density[:, BAND - 8 :], "rows", 1)
    below = shifted(density[:, :8], "rows", -1)
    sent = call(
        pack_kernel,
        (GROUP, PLANES, SEG_ROWS, LANES),
        [(PLANES, SEGS * SEG_ROWS, COLS)],
        density,
        above,
        below,
    )
    groups = [[GROUP * b + i for i in range(GROUP)] for b in range(BLOCKS)]
    mine = lax.all_to_all(sent, "depth", 0, 0, axis_index_groups=groups, tiled=True)
    near = HALO // PLANES
    head, tail = mine[:near], mine[GROUP - near :]
    before = shifted(tail, "depth", GROUP)
    after = shifted(head, "depth", -GROUP)
    field = (DEEP, TALL, LANES)
    inner = call(
        inner_kernel,
        (EDGE * PASSES + 4, SEG_ROWS, LANES),
        [field, field, (2, TALL, LANES), (8, LANES)],
        mine,
        transfer_table,
    )
    few = (6, TALL, LANES)
    partial = call(
        outer_kernel,
        (BAND, LANES),
        [few, few, (4, TALL, LANES), (8, LANES)],
        head,
        tail,
        before,
        after,
        inner,
        transfer_table,
    )
    parts = lax.all_to_all(partial, "depth", 0, 0, tiled=True)
    return call(gather_kernel, (4, 1, COLS), [], parts)


def solution(mesh):
    placed = (P("depth", "rows", None), P())
    return jax.shard_map(
        per_device,
        mesh=mesh,
        in_specs=placed,
        out_specs=P(None, ("rows", "depth"), None),
        check_vma=False,
    )
```

time: 110 us -> 100 us (0.909)
  waiting for transfers between devices: 8.62 us -> 0.99 us
  Pallas kernels: 31.7 us -> 26.2 us
  blocking collectives: 55.4 us -> 60.1 us
  starting transfers between devices: 10.6 us -> 9.19 us
    ppermute x4, waiting for transfers between devices: 8.62 us -> 0.99 us  [shifted(): return lax.ppermute(value, axis, pairs)]
    pallas_call x3 -> x4, Pallas kernels: 31.7 us -> 26.2 us  [call(): pl.pallas_call(kernel, out_shape=jax.ShapeDtypeStruct(shape, jnp.float32)...]
    all_to_all x1, blocking collectives: 23.3 us -> 26.2 us  [per_device(): parts = lax.all_to_all(partial, 'depth', 0, 0, tiled=True)]
    all_to_all x1, blocking collectives: 32 us -> 33.9 us  [per_device(): lax.all_to_all(sent, 'depth', 0, 0, axis_index_groups=groups, tiled=True)]
    ppermute x4, starting transfers between devices: 10.6 us -> 9.19 us  [shifted(): return lax.ppermute(value, axis, pairs)]
  transfers between devices with their start and end apart: 4 -> 4, of which waited for: 3 -> 1; matrix products, arithmetic and copies ran while one was open for 1% -> 0% of each run, Pallas kernels for 0% -> 18%
where the time goes in v2:
time: 100 us; the launch traced here: 99.3 us
  blocking collectives  60.1 us (60%)
  Pallas kernels  26.2 us (26%)
  starting transfers between devices  9.19 us (9%)
  local copies, waits for them, and re-layouts  2.68 us (3%)
    all_to_all x1, blocking collectives, per_device(): lax.all_to_all(sent, 'depth', 0, 0, axis_index_groups=groups, tiled=True)  33.9 us
    all_to_all x1, blocking collectives, per_device(): parts = lax.all_to_all(partial, 'depth', 0, 0, tiled=True)  26.2 us
    pallas_call x4, Pallas kernels, call(): pl.pallas_call(kernel, out_shape=jax.ShapeDtypeStruct(shape, jnp.float32)...  26.2 us
    ppermute x4, starting transfers between devices, shifted(): return lax.ppermute(value, axis, pairs)  9.19 us
  transfers between devices with their start and end apart: 4, of which 1 were waited for; matrix products, arithmetic and copies ran while one was open for 0% of the time, Pallas kernels for 18%

profile of v2, /device:TPU:1, one launch (start us, length us, event | category | flops | bytes accessed | tf_op | source)
XLA Modules:
  0.0 99.3 jit_solution(9814940399222192204)
XLA Ops:
  0.0 0.8 fusion.1
  0.8 1.3 %collective-permute-start.1 = (f32[2,8,512]{2,1,0:T(8,128)S(1)}, f32[2,8,512]{2,1,0:T(8,128)S(1)}, u32[]{:S(2)}, u32[]{:S(2)}) collective-permute-start(f32[2,8,512]{2,1,0:T(8,128)S(1)} %get-tuple-element.7), channel_id=1, source_target_pairs={{1,0},{2,1},{3,2},{5,4},{6,5},{7,6},{9,8},{10,9},{11,10},{13,12},{... | collective-permute-start | bytes 98312 | tf_op jit(solution)/shard_map/ppermute | solution.py:352
  2.1 4.6 %collective-permute-start = (f32[2,8,512]{2,1,0:T(8,128)S(1)}, f32[2,8,512]{2,1,0:T(8,128)S(1)}, u32[]{:S(2)}, u32[]{:S(2)}) collective-permute-start(f32[2,8,512]{2,1,0:T(8,128)S(1)} %get-tuple-element.8), channel_id=1, source_target_pairs={{0,1},{1,2},{2,3},{4,5},{5,6},{6,7},{8,9},{9,10},{10,11},{12,13},{... | collective-permute-start | bytes 98312 | tf_op jit(solution)/shard_map/ppermute | solution.py:352
  6.6 0.0 collective-permute-done.1.below
  6.7 0.0 copy-start.5
  6.7 1.0 collective-permute-done.above
  7.6 0.0 copy-done.5
  7.6 0.0 copy-start.6
  7.6 0.6 copy-done.6
  8.3 3.0 %pack_kernel.1 = f32[16,2,48,128]{3,2,1,0:T(8,128)} custom-call(f32[2,128,512]{2,1,0:T(8,128)} %own.1, f32[2,8,512]{2,1,0:T(8,128)} %copy-done.6, f32[2,8,512]{2,1,0:T(8,128)} %copy-done.5), custom_call_target="tpu_custom_call" | custom-call | tf_op jit(solution)/shard_map/pack_kernel/pallas_call | solution.py:339
  11.3 33.9 %all_to_all.16.mine = f32[16,2,48,128]{3,2,1,0:T(8,128)S(1)} all-to-all(f32[16,2,48,128]{3,2,1,0:T(8,128)} %pack_kernel.1), channel_id=1, replica_groups={{0,4,8,12,16,20,24,28,32,36,40,44,48,52,56,60},{64,68,72,76,80,84,88,92..., dimensions={0} | all-to-all | bytes 1572864 | tf_op jit(solution)/shard_map/all_to_all | solution.py:367
  45.2 0.0 copy-start
  45.2 0.0 copy-start.1
  45.2 0.0 copy-start.2
  45.2 2.1 %collective-permute-start.2 = (f32[2,2,48,128]{3,2,1,0:T(8,128)S(1)}, f32[2,2,48,128]{3,2,1,0:T(8,128)S(1)}, u32[]{:S(2)}, u32[]{:S(2)}) collective-permute-start(f32[2,2,48,128]{3,2,1,0:T(8,128)S(1)} %get-tuple-element.5.tail), channel_id=1, source_target_pairs={{0,64},{4,68},{8,72},{12,76},{16,80},{20,84},{24,88},{28,92},{32,9... | collective-permute-start | bytes 294920 | tf_op jit(solution)/shard_map/ppermute | solution.py:352
  47.3 1.3 %collective-permute-start.3 = (f32[2,2,48,128]{3,2,1,0:T(8,128)S(1)}, f32[2,2,48,128]{3,2,1,0:T(8,128)S(1)}, u32[]{:S(2)}, u32[]{:S(2)}) collective-permute-start(f32[2,2,48,128]{3,2,1,0:T(8,128)S(1)} %get-tuple-element.6.head), channel_id=1, source_target_pairs={{64,0},{68,4},{72,8},{76,12},{80,16},{84,20},{88,24},{92,28},{96,3... | collective-permute-start | bytes 294920 | tf_op jit(solution)/shard_map/ppermute | solution.py:352
  48.6 0.0 copy-done
  48.6 17.5 %inner_kernel.1.inner = f32[16,48,128]{2,1,0:T(8,128)} custom-call(f32[16,2,48,128]{3,2,1,0:T(8,128)} %copy-done, f32[4,16]{1,0:T(4,128)} %transfer.3), custom_call_target="tpu_custom_call" | custom-call | tf_op jit(solution)/shard_map/inner_kernel/pallas_call | solution.py:339
  66.1 0.0 copy-done.1
  66.1 0.0 copy-done.2
  66.1 0.0 collective-permute-done.2.before
  66.1 0.0 copy-start.3
  66.1 0.0 collective-permute-done.3.after
  66.1 0.6 copy-done.3
  66.7 0.0 copy-start.4
  66.7 0.6 copy-done.4
  67.4 4.0 %outer_kernel.1 = f32[128,128]{1,0:T(8,128)} custom-call(f32[2,2,48,128]{3,2,1,0:T(8,128)} %copy-done.2, f32[2,2,48,128]{3,2,1,0:T(8,128)} %copy-done.1, f32[2,2,48,128]{3,2,1,0:T(8,128)} %copy-done.3, f32[2,2,48,128]{3,2,1,0:T(8,128)} %copy-done.4, f32[16,48,128]{2,1,0:T(8,128)} %inner_kernel.1.inner, f32[4,16]{1,0:T(4,128)} %transfer.3), custom_call_target="tpu_custom_call" | custom-call | tf_op jit(solution)/shard_map/outer_kernel/pallas_call | solution.py:339
  71.4 26.2 %all_to_all.17 = f32[128,1,128]{2,1,0:T(1,128)} all-to-all(f32[128,1,128]{2,1,0:T(1,128)} %bitcast.5), channel_id=1, replica_groups=mesh['depth'=128,'rows'=4] {'depth'}, dimensions={0} | all-to-all | bytes 131072 | tf_op jit(solution)/shard_map/all_to_all | solution.py:392
  97.6 1.6 %gather_kernel.1 = f32[4,1,512]{2,1,0:T(1,128)} custom-call(f32[128,128]{1,0:T(8,128)} %bitcast.4), custom_call_target="tpu_custom_call" | custom-call | tf_op jit(solution)/shard_map/gather_kernel/pallas_call | solution.py:339
  (1 shorter events, 0.0 us)
Async XLA Ops:
  0.8 5.9 %collective-permute-start.1 = (f32[2,8,512]{2,1,0:T(8,128)S(1)}, f32[2,8,512]{2,1,0:T(8,128)S(1)}, u32[]{:S(2)}, u32[]{:S(2)}) collective-permute-start(f32[2,8,512]{2,1,0:T(8,128)S(1)} %get-tuple-element.7), channel_id=1, source_target_pairs={{1,0},{2,1},{3,2},{5,4},{6,5},{7,6},{9,8},{10,9},{11,10},{13,12},{... | collective-permute-start | bytes 98312 | tf_op jit(solution)/shard_map/ppermute | solution.py:352
  2.1 5.6 %collective-permute-start = (f32[2,8,512]{2,1,0:T(8,128)S(1)}, f32[2,8,512]{2,1,0:T(8,128)S(1)}, u32[]{:S(2)}, u32[]{:S(2)}) collective-permute-start(f32[2,8,512]{2,1,0:T(8,128)S(1)} %get-tuple-element.8), channel_id=1, source_target_pairs={{0,1},{1,2},{2,3},{4,5},{5,6},{6,7},{8,9},{9,10},{10,11},{12,13},{... | collective-permute-start | bytes 98312 | tf_op jit(solution)/shard_map/ppermute | solution.py:352
  6.7 1.0 %copy-start.5 = (f32[2,8,512]{2,1,0:T(8,128)}, f32[2,8,512]{2,1,0:T(8,128)S(1)}, u32[]{:S(2)}) copy-start(f32[2,8,512]{2,1,0:T(8,128)S(1)} %collective-permute-done.1.below) | copy-start | bytes 98308
  7.6 0.6 copy-start.6
  45.2 3.4 %copy-start = (f32[16,2,48,128]{3,2,1,0:T(8,128)}, f32[16,2,48,128]{3,2,1,0:T(8,128)S(1)}, u32[]{:S(2)}) copy-start(f32[16,2,48,128]{3,2,1,0:T(8,128)S(1)} %all_to_all.16.mine) | copy-start | bytes 2359300
  45.2 20.9 %copy-start.1 = (f32[2,2,48,128]{3,2,1,0:T(8,128)}, f32[2,2,48,128]{3,2,1,0:T(8,128)S(1)}, u32[]{:S(2)}) copy-start(f32[2,2,48,128]{3,2,1,0:T(8,128)S(1)} %get-tuple-element.5.tail) | copy-start | bytes 294916
  45.2 20.9 %copy-start.2 = (f32[2,2,48,128]{3,2,1,0:T(8,128)}, f32[2,2,48,128]{3,2,1,0:T(8,128)S(1)}, u32[]{:S(2)}) copy-start(f32[2,2,48,128]{3,2,1,0:T(8,128)S(1)} %get-tuple-element.6.head) | copy-start | bytes 294916
  45.2 20.9 %collective-permute-start.2 = (f32[2,2,48,128]{3,2,1,0:T(8,128)S(1)}, f32[2,2,48,128]{3,2,1,0:T(8,128)S(1)}, u32[]{:S(2)}, u32[]{:S(2)}) collective-permute-start(f32[2,2,48,128]{3,2,1,0:T(8,128)S(1)} %get-tuple-element.5.tail), channel_id=1, source_target_pairs={{0,64},{4,68},{8,72},{12,76},{16,80},{20,84},{24,88},{28,92},{32,9... | collective-permute-start | bytes 294920 | tf_op jit(solution)/shard_map/ppermute | solution.py:352
  47.3 18.8 %collective-permute-start.3 = (f32[2,2,48,128]{3,2,1,0:T(8,128)S(1)}, f32[2,2,48,128]{3,2,1,0:T(8,128)S(1)}, u32[]{:S(2)}, u32[]{:S(2)}) collective-permute-start(f32[2,2,48,128]{3,2,1,0:T(8,128)S(1)} %get-tuple-element.6.head), channel_id=1, source_target_pairs={{64,0},{68,4},{72,8},{76,12},{80,16},{84,20},{88,24},{92,28},{96,3... | collective-permute-start | bytes 294920 | tf_op jit(solution)/shard_map/ppermute | solution.py:352
  66.1 0.6 copy-start.3
  66.7 0.6 copy-start.4

commit v3 on v2

--- a/solution.py
+++ b/solution.py
@@ -29,6 +29,8 @@
 TOP = 8
 TALL = SEG_ROWS + 2 * TOP
 EDGE = 4
+UNROLL = 7
+SHADED = 8
 VMEM = pltpu.VMEM
 
 
@@ -109,7 +111,9 @@
 
 
 def rows_at(j, by=0):
-    return slice(TOP + 8 * j + by, TOP + 8 * j + by + 8)
+    if isinstance(j, int):
+        return slice(TOP + 8 * j + by, TOP + 8 * j + by + 8)
+    return pl.ds(pl.multiple_of(8 * j, 8) + TOP + by, 8)
 
 
 def put(ref, p, tiles):
@@ -164,11 +168,35 @@
     return [flux(deeper[j] - here[j]) for j in range(TILES)]
 
 
-def tables(transfer, table):
-    table[...] = jnp.zeros((8, LANES), jnp.float32)
-    table[0:4, 1 : 1 + KNOTS] = transfer[...]
-    base = [jnp.broadcast_to(table[c : c + 1, :], (8, LANES)) for c in range(4)]
-    return base, [pltpu.roll(base[c], LANES - 1, 1) - base[c] for c in range(4)]
+ALONG_ROWS = lax.GatherDimensionNumbers(
+    offset_dims=(),
+    collapsed_slice_dims=(0,),
+    start_index_map=(0,),
+    operand_batching_dims=(1,),
+    start_indices_batching_dims=(1,),
+)
+
+
+def along_rows(x, k):
+    return lax.gather(
+        x, k[..., None], ALONG_ROWS, (1, 1), mode=lax.GatherScatterMode.PROMISE_IN_BOUNDS
+    )
+
+
+def pick(parts, k, high):
+    return jnp.where(high, along_rows(parts[1], k), along_rows(parts[0], k))
+
+
+def tables(transfer):
+    base, slope = [], []
+    for c in range(4):
+        knots = jnp.broadcast_to(transfer[:, c : c + 1], (KNOTS, LANES))
+        row = lax.broadcasted_iota(jnp.int32, (KNOTS, LANES), 0)
+        after = jnp.where(row == KNOTS - 1, 0.0, pltpu.roll(knots, KNOTS - 1, 0))
+        step = after - knots
+        base.append((knots[:8], knots[8:]))
+        slope.append((step[:8], step[8:]))
+    return base, slope
 
 
 def shade(src, p, j, carry, lookup, tile):
@@ -184,14 +212,12 @@
     gain = 1.0 - AMBIENT
     along = jnp.abs(0.64 * gain * depth + 0.6 * gain * row + 0.48 * gain * col)
     shading = AMBIENT + along * lax.rsqrt(square)
-    position = f * ((KNOTS - 1) / UPPER_DENSITY) + 1.0
+    position = f * ((KNOTS - 1) / UPPER_DENSITY)
     k = position.astype(jnp.int32)
     frac = position - k.astype(jnp.float32)
-    mixed = [
-        jnp.take_along_axis(base[c], k, axis=1)
-        + frac * jnp.take_along_axis(slope[c], k, axis=1)
-        for c in range(4)
-    ]
+    high = k >= 8
+    k = jnp.bitwise_and(k, 7)
+    mixed = [pick(base[c], k, high) + frac * pick(slope[c], k, high) for c in range(4)]
     kept = jnp.exp(mixed[3] * (-OPTICAL_DEPTH / (DEEP * BLOCKS)))
     weight = remaining * (1.0 - kept) * shading
     return (
@@ -202,106 +228,116 @@
     )
 
 
-def inner_kernel(mine, transfer, out, fa, fb, fluxes, table):
+def inner_kernel(mine, knots, out, fa, fb, fluxes):
     tile = Tile()
     zero = jnp.zeros((8, LANES), jnp.float32)
 
     def fill(i, carry):
         for p in range(PLANES):
-            tiles = [mine[i, p, 8 * j : 8 * j + 8, :] for j in range(TILES)]
-            put(fa, PLANES * i + p, tiles)
+            put(fa, PLANES * i + p, [mine[i, p, 8 * j : 8 * j + 8, :] for j in range(TILES)])
         return carry
 
     lax.fori_loop(0, GROUP, fill, 0)
     src, dst = fa, fb
     for sweep in range(PASSES):
         lo, hi = sweep + 1, DEEP - 1 - sweep
-
-        def step(i, carry, src=src, dst=dst, lo=lo):
-            for u in range(2):
-                p = lo + 2 * i + u
+        count = hi - lo
+        unroll = 6 if count % 6 == 0 else UNROLL
+
+        def step(i, carry, src=src, dst=dst, lo=lo, unroll=unroll):
+            for u in range(unroll):
+                p = lo + unroll * i + u
                 carry = diffuse(src, p, dst, p, fluxes, u, carry, tile)
             return carry
 
-        lax.fori_loop(0, (hi - lo) // 2, step, first_flux(src, lo - 1))
+        whole = count // unroll
+        carry = lax.fori_loop(0, whole, step, first_flux(src, lo - 1))
+        for u in range(count - unroll * whole):
+            p = lo + unroll * whole + u
+            carry = diffuse(src, p, dst, p, fluxes, u, carry, tile)
         kept = (lo, lo + 1, hi - 2, hi - 1)
         for i in range(EDGE):
             for j in range(TILES):
                 out[EDGE * sweep + i, 8 * j : 8 * j + 8, :] = dst[kept[i], rows_at(j), :]
         src, dst = dst, src
 
-    lookup = tables(transfer, table)
-    for j in range(TILES):
-
-        def planes(i, carry, j=j):
-            for u in range(4):
-                carry = shade(src, HALO + 4 * i + u, j, carry, lookup, tile)
+    lookup = tables(knots)
+    first = (zero, zero, zero, zero + 1.0)
+
+    def shaded(j, unused):
+        def planes(i, carry):
+            for u in range(SHADED):
+                carry = shade(src, HALO + SHADED * i + u, j, carry, lookup, tile)
             return carry
 
-        sums = lax.fori_loop(0, (DEEP - 2 * HALO) // 4, planes, (zero, zero, zero, zero + 1.0))
+        sums = lax.fori_loop(0, (DEEP - 2 * HALO) // SHADED, planes, first)
         for c in range(4):
-            out[EDGE * PASSES + c, 8 * j : 8 * j + 8, :] = sums[c]
-
-
-def outer_kernel(head, tail, before, after, inner, transfer, out, fa, fb, fluxes, table):
+            out[EDGE * PASSES + c, pl.ds(pl.multiple_of(8 * j, 8), 8), :] = sums[c]
+        return unused
+
+    lax.fori_loop(0, TILES, shaded, 0)
+
+
+def outer_kernel(head, tail, before, after, inner, knots, out, fa, fb, ga, gb, fluxes):
     tile = Tile()
     zero = jnp.zeros((8, LANES), jnp.float32)
-    lookup = tables(transfer, table)
-
-    def plane_of(ref, i):
-        return [ref[i // 2, i % 2, 8 * j : 8 * j + 8, :] for j in range(TILES)]
-
-    def inner_of(i):
-        return [inner[i, 8 * j : 8 * j + 8, :] for j in range(TILES)]
-
-    def side(front):
-        inside = tile.block > 0 if front else tile.block < BLOCKS - 1
-        own = 4 if front else 0
-        halo = 0 if front else 2
-        for i in range(2):
-            put(fa, own + i, plane_of(head if front else tail, i if front else 2 + i))
-
-        @pl.when(inside)
-        def _():
-            for i in range(HALO):
-                put(fa, halo + i, plane_of(before if front else after, i))
-
-        @pl.when(jnp.logical_not(inside))
-        def _():
-            for i in range(HALO):
-                put(fa, halo + i, plane_of(head if front else tail, HALO - 1 - i))
-
-        src, dst = fa, fb
-        for sweep in range(PASSES):
+    lookup = tables(knots)
+
+    def fill(ref, to, source, i):
+        put(ref, to, [source[i // 2, i % 2, 8 * j : 8 * j + 8, :] for j in range(TILES)])
+
+    for i in range(2):
+        fill(fa, 4 + i, head, i)
+        fill(ga, i, tail, 2 + i)
+
+    @pl.when(tile.block > 0)
+    def _():
+        for i in range(HALO):
+            fill(fa, i, before, i)
+
+    @pl.when(tile.block == 0)
+    def _():
+        for i in range(HALO):
+            fill(fa, i, head, HALO - 1 - i)
+
+    @pl.when(tile.block < BLOCKS - 1)
+    def _():
+        for i in range(HALO):
+            fill(ga, 2 + i, after, i)
+
+    @pl.when(tile.block == BLOCKS - 1)
+    def _():
+        for i in range(HALO):
+            fill(ga, 2 + i, tail, HALO - 1 - i)
+
+    front, back = (fa, fb), (ga, gb)
+    for sweep in range(PASSES):
+        for (src, dst), at in ((front, 0), (back, 2)):
             carry = first_flux(src, 0)
             for i in range(4):
-                to = i if front else 2 + i
-                carry = diffuse(src, i + 1, dst, to, fluxes, i, carry, tile)
-            for i in range(2):
-                put(dst, own + i, inner_of(EDGE * sweep + (i if front else 2 + i)))
-            src, dst = dst, src
-        return src
-
-    src = side(True)
-    sums = []
+                carry = diffuse(src, i + 1, dst, at + i, fluxes, at // 2 * 4 + i, carry, tile)
+        for i in range(2):
+            for ref, to, k in ((front[1], 4 + i, i), (back[1], i, 2 + i)):
+                k += EDGE * sweep
+                put(ref, to, [inner[k, 8 * j : 8 * j + 8, :] for j in range(TILES)])
+        front, back = front[::-1], back[::-1]
+
+    lane = lane_index()
     for j in range(TILES):
         carry = (zero, zero, zero, zero + 1.0)
         for i in range(4):
-            carry = shade(src, i + 1, j, carry, lookup, tile)
+            carry = shade(front[0], i + 1, j, carry, lookup, tile)
         mid = [inner[EDGE * PASSES + c, 8 * j : 8 * j + 8, :] for c in range(4)]
-        remaining = carry[3]
-        sums.append([carry[c] + remaining * mid[c] for c in range(3)] + [remaining * mid[3]])
-    src = side(False)
-    lane = lane_index()
-    for j in range(TILES):
-        carry = sums[j]
+        end = (zero, zero, zero, zero + 1.0)
         for i in range(4):
-            carry = shade(src, i + 1, j, carry, lookup, tile)
+            end = shade(back[0], i + 1, j, end, lookup, tile)
+        sums = [carry[c] + carry[3] * (mid[c] + mid[3] * end[c]) for c in range(3)]
+        sums.append(carry[3] * mid[3] * end[3])
         for k in range(SEGS):
             value = None
             for c in range(4):
                 by = TILE * c - WIDE * k - HALO - tile.start + LANES * 2
-                moved = pltpu.roll(carry[c], lax.rem(by, LANES), 1)
+                moved = pltpu.roll(sums[c], lax.rem(by, LANES), 1)
                 value = moved if value is None else jnp.where(lane >= TILE * c, moved, value)
             first = SEG_ROWS * k + 8 * j - HALO
             lo, hi = max(first, 0), min(first + 8, BAND)
@@ -336,9 +372,10 @@
 
 def call(kernel, shape, scratch, *operands):
     spec = pl.BlockSpec(memory_space=VMEM)
+    operands = [pltpu.with_memory_space_constraint(x, VMEM) for x in operands]
     return pl.pallas_call(
         kernel,
-        out_shape=jax.ShapeDtypeStruct(shape, jnp.float32),
+        out_shape=VMEM(shape, jnp.float32),
         in_specs=[spec] * len(operands),
         out_specs=spec,
         scratch_shapes=[VMEM(s, jnp.float32) for s in scratch],
@@ -369,25 +406,26 @@
     head, tail = mine[:near], mine[GROUP - near :]
     before = shifted(tail, "depth", GROUP)
     after = shifted(head, "depth", -GROUP)
+    knots = transfer_table.T
     field = (DEEP, TALL, LANES)
     inner = call(
         inner_kernel,
         (EDGE * PASSES + 4, SEG_ROWS, LANES),
-        [field, field, (2, TALL, LANES), (8, LANES)],
+        [field, field, (UNROLL, TALL, LANES)],
         mine,
-        transfer_table,
+        knots,
     )
     few = (6, TALL, LANES)
     partial = call(
         outer_kernel,
         (BAND, LANES),
-        [few, few, (4, TALL, LANES), (8, LANES)],
+        [few, few, few, few, (8, TALL, LANES)],
         head,
         tail,
         before,
         after,
         inner,
-        transfer_table,
+        knots,
     )
     parts = lax.all_to_all(partial, "depth", 0, 0, tiled=True)
     return call(gather_kernel, (4, 1, COLS), [], parts)

time: 100 us -> 84.3 us (0.84)
  Pallas kernels: 26.2 us -> 9.87 us
  blocking collectives: 60.1 us -> 57.6 us
  waiting for transfers between devices: 0.99 us -> 3.36 us
  starting transfers between devices: 9.19 us -> 10.5 us
    pallas_call x4, Pallas kernels: 26.2 us -> 9.87 us  [call(): pl.pallas_call(kernel, out_shape=VMEM(shape, jnp.float32), in_specs=[spec...]
    ppermute x4, waiting for transfers between devices: 0.99 us -> 3.36 us  [shifted(): return lax.ppermute(value, axis, pairs)]
    all_to_all x1, blocking collectives: 33.9 us -> 31.8 us  [per_device(): lax.all_to_all(sent, 'depth', 0, 0, axis_index_groups=groups, tiled=True)]
    ppermute x4, starting transfers between devices: 9.19 us -> 10.5 us  [shifted(): return lax.ppermute(value, axis, pairs)]
  transfers between devices with their start and end apart: 4 -> 4, of which waited for: 1 -> 1; matrix products, arithmetic and copies ran while one was open for 0% -> 0% of each run, Pallas kernels for 18% -> 7%
where the time goes in v3:
time: 84.3 us; the launch traced here: 84 us
  blocking collectives  57.6 us (68%)
  starting transfers between devices  10.5 us (12%)
  Pallas kernels  9.87 us (12%)
  waiting for transfers between devices  3.36 us (4%)
  local copies, waits for them, and re-layouts  2.53 us (3%)
    all_to_all x1, blocking collectives, per_device(): lax.all_to_all(sent, 'depth', 0, 0, axis_index_groups=groups, tiled=True)  31.8 us
    all_to_all x1, blocking collectives, per_device(): parts = lax.all_to_all(partial, 'depth', 0, 0, tiled=True)  25.8 us
    ppermute x4, starting transfers between devices, shifted(): return lax.ppermute(value, axis, pairs)  10.5 us
    pallas_call x4, Pallas kernels, call(): pl.pallas_call(kernel, out_shape=VMEM(shape, jnp.float32), in_specs=[spec...  9.87 us
    ppermute x4, waiting for transfers between devices, shifted(): return lax.ppermute(value, axis, pairs)  3.36 us
    unnamed x6, local copies, waits for them, and re-layouts  1.73 us
  transfers between devices with their start and end apart: 4, of which 1 were waited for; matrix products, arithmetic and copies ran while one was open for 0% of the time, Pallas kernels for 7%

profile of v3, /device:TPU:1, one launch (start us, length us, event | category | flops | bytes accessed | tf_op | source)
XLA Modules:
  0.0 84.0 jit_solution(9643427258291547460)
XLA Ops:
  0.0 0.8 fusion.1
  0.8 3.9 %collective-permute-start = (f32[2,8,512]{2,1,0:T(8,128)S(1)}, f32[2,8,512]{2,1,0:T(8,128)S(1)}, u32[]{:S(2)}, u32[]{:S(2)}) collective-permute-start(f32[2,8,512]{2,1,0:T(8,128)S(1)} %get-tuple-element.8), channel_id=1, source_target_pairs={{0,1},{1,2},{2,3},{4,5},{5,6},{6,7},{8,9},{9,10},{10,11},{12,13},{... | collective-permute-start | bytes 98312 | tf_op jit(solution)/shard_map/ppermute | solution.py:389
  4.7 1.3 %collective-permute-start.1 = (f32[2,8,512]{2,1,0:T(8,128)S(1)}, f32[2,8,512]{2,1,0:T(8,128)S(1)}, u32[]{:S(2)}, u32[]{:S(2)}) collective-permute-start(f32[2,8,512]{2,1,0:T(8,128)S(1)} %get-tuple-element.7), channel_id=1, source_target_pairs={{1,0},{2,1},{3,2},{5,4},{6,5},{7,6},{9,8},{10,9},{11,10},{13,12},{... | collective-permute-start | bytes 98312 | tf_op jit(solution)/shard_map/ppermute | solution.py:389
  6.0 0.0 collective-permute-done.above
  6.0 3.3 %collective-permute-done.1.below = f32[2,8,512]{2,1,0:T(8,128)S(1)} collective-permute-done((f32[2,8,512]{2,1,0:T(8,128)S(1)}, f32[2,8,512]{2,1,0:T(8,128)S(1)}, u32[]{:S(2)}, u32[]{:S(2)}) %collective-permute-start.1) | collective-permute-done | bytes 32800 | tf_op jit(solution)/shard_map/ppermute | solution.py:389
  9.4 0.0 copy-start
  9.4 1.0 %copy-done = f32[2,128,512]{2,1,0:T(8,128)S(1)} copy-done((f32[2,128,512]{2,1,0:T(8,128)S(1)}, f32[2,128,512]{2,1,0:T(8,128)}, u32[]{:S(2)}) %copy-start) | copy-done | bytes 524312
  10.4 1.0 %pack_kernel.1 = f32[16,2,48,128]{3,2,1,0:T(8,128)S(1)} custom-call(f32[2,128,512]{2,1,0:T(8,128)S(1)} %copy-done, f32[2,8,512]{2,1,0:T(8,128)S(1)} %collective-permute-done.above, f32[2,8,512]{2,1,0:T(8,128)S(1)} %collective-permute-done.1.below), custom_call_target="tpu_custom_call" | custom-call | tf_op jit(solution)/shard_map/pack_kernel/pallas_call | solution.py:376
  11.4 31.8 %all_to_all.16.mine = f32[16,2,48,128]{3,2,1,0:T(8,128)S(1)} all-to-all(f32[16,2,48,128]{3,2,1,0:T(8,128)S(1)} %pack_kernel.1), channel_id=1, replica_groups={{0,4,8,12,16,20,24,28,32,36,40,44,48,52,56,60},{64,68,72,76,80,84,88,92..., dimensions={0} | all-to-all | bytes 1572864 | tf_op jit(solution)/shard_map/all_to_all | solution.py:404
  43.3 0.0 copy-start.1
  43.3 4.0 %collective-permute-start.2 = (f32[2,2,48,128]{3,2,1,0:T(8,128)S(1)}, f32[2,2,48,128]{3,2,1,0:T(8,128)S(1)}, u32[]{:S(2)}, u32[]{:S(2)}) collective-permute-start(f32[2,2,48,128]{3,2,1,0:T(8,128)S(1)} %get-tuple-element.5.tail), channel_id=1, source_target_pairs={{0,64},{4,68},{8,72},{12,76},{16,80},{20,84},{24,88},{28,92},{32,9... | collective-permute-start | bytes 294920 | tf_op jit(solution)/shard_map/ppermute | solution.py:389
  47.3 1.3 %collective-permute-start.3 = (f32[2,2,48,128]{3,2,1,0:T(8,128)S(1)}, f32[2,2,48,128]{3,2,1,0:T(8,128)S(1)}, u32[]{:S(2)}, u32[]{:S(2)}) collective-permute-start(f32[2,2,48,128]{3,2,1,0:T(8,128)S(1)} %get-tuple-element.6.head), channel_id=1, source_target_pairs={{64,0},{68,4},{72,8},{76,12},{80,16},{84,20},{88,24},{92,28},{96,3... | collective-permute-start | bytes 294920 | tf_op jit(solution)/shard_map/ppermute | solution.py:389
  48.6 0.0 copy-done.1
  48.6 0.1 copy.4
  48.7 6.3 %inner_kernel.1.inner = f32[16,48,128]{2,1,0:T(8,128)S(1)} custom-call(f32[16,2,48,128]{3,2,1,0:T(8,128)S(1)} %all_to_all.16.mine, f32[16,4]{1,0:T(8,128)S(1)} %bitcast.7), custom_call_target="tpu_custom_call" | custom-call | tf_op jit(solution)/shard_map/inner_kernel/pallas_call | solution.py:376
  55.0 0.0 collective-permute-done.2.before
  55.0 0.0 collective-permute-done.3.after
  55.0 2.4 %outer_kernel.1 = f32[128,128]{1,0:T(8,128)S(1)} custom-call(f32[2,2,48,128]{3,2,1,0:T(8,128)S(1)} %get-tuple-element.6.head, f32[2,2,48,128]{3,2,1,0:T(8,128)S(1)} %get-tuple-element.5.tail, f32[2,2,48,128]{3,2,1,0:T(8,128)S(1)} %collective-permute-done.2.before, f32[2,2,48,128]{3,2,1,0:T(8,128)S(1)} %collective-permute-done.3.after, ...), custom_call_target="tpu_custom_call" | custom-call | tf_op jit(solution)/shard_map/outer_kernel/pallas_call | solution.py:376
  57.4 25.8 %all_to_all.17 = f32[128,1,128]{2,1,0:T(1,128)S(1)} all-to-all(f32[128,1,128]{2,1,0:T(1,128)S(1)} %bitcast.6), channel_id=1, replica_groups=mesh['depth'=128,'rows'=4] {'depth'}, dimensions={0} | all-to-all | bytes 131072 | tf_op jit(solution)/shard_map/all_to_all | solution.py:430
  83.1 0.2 gather_kernel.1
  83.3 0.6 copy.6
  (1 shorter events, 0.0 us)
Async XLA Ops:
  0.8 5.2 %collective-permute-start = (f32[2,8,512]{2,1,0:T(8,128)S(1)}, f32[2,8,512]{2,1,0:T(8,128)S(1)}, u32[]{:S(2)}, u32[]{:S(2)}) collective-permute-start(f32[2,8,512]{2,1,0:T(8,128)S(1)} %get-tuple-element.8), channel_id=1, source_target_pairs={{0,1},{1,2},{2,3},{4,5},{5,6},{6,7},{8,9},{9,10},{10,11},{12,13},{... | collective-permute-start | bytes 98312 | tf_op jit(solution)/shard_map/ppermute | solution.py:389
  4.7 4.7 %collective-permute-start.1 = (f32[2,8,512]{2,1,0:T(8,128)S(1)}, f32[2,8,512]{2,1,0:T(8,128)S(1)}, u32[]{:S(2)}, u32[]{:S(2)}) collective-permute-start(f32[2,8,512]{2,1,0:T(8,128)S(1)} %get-tuple-element.7), channel_id=1, source_target_pairs={{1,0},{2,1},{3,2},{5,4},{6,5},{7,6},{9,8},{10,9},{11,10},{13,12},{... | collective-permute-start | bytes 98312 | tf_op jit(solution)/shard_map/ppermute | solution.py:389
  9.4 1.0 %copy-start = (f32[2,128,512]{2,1,0:T(8,128)S(1)}, f32[2,128,512]{2,1,0:T(8,128)}, u32[]{:S(2)}) copy-start(f32[2,128,512]{2,1,0:T(8,128)} %own.1) | copy-start | bytes 1572868
  43.3 5.3 %copy-start.1 = (f32[4,16]{1,0:T(4,128)S(1)}, f32[4,16]{1,0:T(4,128)}, u32[]{:S(2)}) copy-start(f32[4,16]{1,0:T(4,128)} %param.3) | copy-start | bytes 772
  43.3 11.7 %collective-permute-start.2 = (f32[2,2,48,128]{3,2,1,0:T(8,128)S(1)}, f32[2,2,48,128]{3,2,1,0:T(8,128)S(1)}, u32[]{:S(2)}, u32[]{:S(2)}) collective-permute-start(f32[2,2,48,128]{3,2,1,0:T(8,128)S(1)} %get-tuple-element.5.tail), channel_id=1, source_target_pairs={{0,64},{4,68},{8,72},{12,76},{16,80},{20,84},{24,88},{28,92},{32,9... | collective-permute-start | bytes 294920 | tf_op jit(solution)/shard_map/ppermute | solution.py:389
  47.3 7.7 %collective-permute-start.3 = (f32[2,2,48,128]{3,2,1,0:T(8,128)S(1)}, f32[2,2,48,128]{3,2,1,0:T(8,128)S(1)}, u32[]{:S(2)}, u32[]{:S(2)}) collective-permute-start(f32[2,2,48,128]{3,2,1,0:T(8,128)S(1)} %get-tuple-element.6.head), channel_id=1, source_target_pairs={{64,0},{68,4},{72,8},{76,12},{80,16},{84,20},{88,24},{92,28},{96,3... | collective-permute-start | bytes 294920 | tf_op jit(solution)/shard_map/ppermute | solution.py:389

commit v4 on v3

--- a/solution.py
+++ b/solution.py
@@ -28,7 +28,7 @@
 LANES = 128
 TOP = 8
 TALL = SEG_ROWS + 2 * TOP
-EDGE = 4
+FRONT = HALO
 UNROLL = 7
 SHADED = 8
 VMEM = pltpu.VMEM
@@ -38,72 +38,101 @@
     return lax.broadcasted_iota(jnp.int32, (rows, LANES), 1)
 
 
-def pack_kernel(own, above, below, out, ext):
-    band = lax.axis_index("rows")
-    bands = lax.axis_size("rows")
-    rows = SEGS * SEG_ROWS
-    for p in range(PLANES):
-        ext[p, HALO : HALO + BAND, :] = own[p]
-        ext[p, rows - 8 :, :] = jnp.zeros((8, COLS), jnp.float32)
-
-    @pl.when(band > 0)
-    def _():
-        for p in range(PLANES):
-            ext[p, 0:HALO, :] = above[p, 8 - HALO : 8, :]
-
-    @pl.when(band == 0)
-    def _():
-        for p in range(PLANES):
-            for i in range(HALO):
-                ext[p, HALO - 1 - i : HALO - i, :] = own[p, i : i + 1, :]
-
-    @pl.when(band < bands - 1)
-    def _():
-        for p in range(PLANES):
-            ext[p, HALO + BAND : 2 * HALO + BAND, :] = below[p, 0:HALO, :]
-
-    @pl.when(band == bands - 1)
-    def _():
-        for p in range(PLANES):
-            for i in range(HALO):
-                row = HALO + BAND + i
-                ext[p, row : row + 1, :] = own[p, BAND - 1 - i : BAND - i, :]
-
+def window_masks():
     lane = lane_index()
     segment, left, right = [], [], []
     for m in range(4):
         local = (lane - (TILE * m - HALO)) % LANES
-        segment.append((local < WIDE, local < 2 * WIDE))
+        segment.append([(local >= WIDE * k) & (local < WIDE * (k + 1)) for k in range(SEGS)])
         column = local % WIDE
         left.append(column < HALO)
         right.append(column >= WIDE - HALO)
+    return segment, left, right
+
+
+def windows(tiles, joined, left, right):
+    for t in range(GROUP):
+        q, m = divmod(t, 4)
+        value = joined(tiles, q, m)
+        if m == 0 and q > 0:
+            value = jnp.where(left[m], joined(tiles, q - 1, m), value)
+        if m == 3 and q < 3:
+            value = jnp.where(right[m], joined(tiles, q + 1, m), value)
+        yield t, m, value
+
+
+def pack_kernel(density, out, own, ext, sem):
+    copy = pltpu.make_async_copy(density, own, sem)
+    copy.start()
+    rows = SEGS * SEG_ROWS
+    for p in range(PLANES):
+        ext[p, :8, :] = jnp.zeros((8, COLS), jnp.float32)
+        ext[p, rows - 16 :, :] = jnp.zeros((16, COLS), jnp.float32)
+    segment, left, right = window_masks()
+    copy.wait()
+    for p in range(PLANES):
+        ext[p, HALO : HALO + BAND, :] = own[p]
+
+    def joined(rolled, q, m):
+        rest = jnp.where(segment[m][1], rolled[1][q], rolled[2][q])
+        return jnp.where(segment[m][0], rolled[0][q], rest)
 
     def step(it, carry):
         p = it // TILES
         j = it - TILES * p
+        row = pl.multiple_of(8 * j, 8)
         rolled = []
         for k in range(SEGS):
-            start = pl.multiple_of(SEG_ROWS * k + 8 * j, 8)
-            row = [ext[p, pl.ds(start, 8), LANES * q : LANES * (q + 1)] for q in range(4)]
-            rolled.append([pltpu.roll(x, WIDE * k, 1) if k else x for x in row])
-
-        def joined(q, m):
-            first, second = segment[m]
-            return jnp.where(
-                first, rolled[0][q], jnp.where(second, rolled[1][q], rolled[2][q])
-            )
-
-        for t in range(GROUP):
-            q, m = divmod(t, 4)
-            value = joined(q, m)
-            if m == 0 and q > 0:
-                value = jnp.where(left[m], joined(q - 1, m), value)
-            if m == 3 and q < 3:
-                value = jnp.where(right[m], joined(q + 1, m), value)
-            out[t, p, pl.ds(pl.multiple_of(8 * j, 8), 8), :] = value
+            start = pl.multiple_of(row + SEG_ROWS * k, 8)
+            tiles = [ext[p, pl.ds(start, 8), LANES * q : LANES * (q + 1)] for q in range(4)]
+            rolled.append([pltpu.roll(x, WIDE * k, 1) if k else x for x in tiles])
+        for t, m, value in windows(rolled, joined, left, right):
+            out[t, p, pl.ds(row, 8), :] = value
         return carry
 
     lax.fori_loop(0, PLANES * TILES, step, 0)
+
+
+def halo_kernel(sent, first, last, above, below, out, edge):
+    band = lax.axis_index("rows")
+    bands = lax.axis_size("rows")
+
+    @pl.when(band > 0)
+    def _():
+        for p in range(PLANES):
+            edge[p, 0:HALO, :] = above[p, 8 - HALO : 8, :]
+
+    @pl.when(band == 0)
+    def _():
+        for p in range(PLANES):
+            for i in range(HALO):
+                edge[p, HALO - 1 - i : HALO - i, :] = first[p, i : i + 1, :]
+
+    @pl.when(band < bands - 1)
+    def _():
+        for p in range(PLANES):
+            edge[p, HALO : 2 * HALO, :] = below[p, 0:HALO, :]
+
+    @pl.when(band == bands - 1)
+    def _():
+        for p in range(PLANES):
+            for i in range(HALO):
+                edge[p, HALO + i : HALO + i + 1, :] = last[p, 7 - i : 8 - i, :]
+
+    segment, left, right = window_masks()
+    row = lax.broadcasted_iota(jnp.int32, (8, LANES), 0)
+    places = ((0, 0, row < HALO), (2, SEG_ROWS - 16, row >= HALO))
+
+    def joined(rolled, q, m):
+        return rolled[q]
+
+    for p in range(PLANES):
+        tiles = [edge[p, :, LANES * q : LANES * (q + 1)] for q in range(4)]
+        for k, at, rows in places:
+            rolled = [pltpu.roll(x, WIDE * k, 1) for x in tiles] if k else tiles
+            for t, m, value in windows(rolled, joined, left, right):
+                here = sent[t, p, at : at + 8, :]
+                out[t, p, at : at + 8, :] = jnp.where(rows & segment[m][k], value, here)
 
 
 def flux(change):
@@ -228,19 +257,37 @@
     )
 
 
-def inner_kernel(mine, knots, out, fa, fb, fluxes):
+def inner_kernel(mine, knots, out, fa, fb, fluxes, sums):
     tile = Tile()
     zero = jnp.zeros((8, LANES), jnp.float32)
+    is_first = tile.block == 0
+
+    def plane_of(i, p):
+        return [mine[i, p, 8 * j : 8 * j + 8, :] for j in range(TILES)]
 
     def fill(i, carry):
         for p in range(PLANES):
-            put(fa, PLANES * i + p, [mine[i, p, 8 * j : 8 * j + 8, :] for j in range(TILES)])
+            put(fa, FRONT + PLANES * i + p, plane_of(i, p))
         return carry
 
     lax.fori_loop(0, GROUP, fill, 0)
+
+    @pl.when(is_first)
+    def _():
+        for i in range(HALO):
+            put(fa, FRONT - 1 - i, plane_of(i // 2, i % 2))
+
     src, dst = fa, fb
     for sweep in range(PASSES):
-        lo, hi = sweep + 1, DEEP - 1 - sweep
+        lo, hi = FRONT + sweep + 1, FRONT + DEEP - 1 - sweep
+
+        @pl.when(is_first)
+        def _(src=src, dst=dst, lo=lo):
+            carry = first_flux(src, lo - 5)
+            for u in range(4):
+                p = lo - 4 + u
+                carry = diffuse(src, p, dst, p, fluxes, u, carry, tile)
+
         count = hi - lo
         unroll = 6 if count % 6 == 0 else UNROLL
 
@@ -255,84 +302,91 @@
         for u in range(count - unroll * whole):
             p = lo + unroll * whole + u
             carry = diffuse(src, p, dst, p, fluxes, u, carry, tile)
-        kept = (lo, lo + 1, hi - 2, hi - 1)
-        for i in range(EDGE):
+        for i in range(2):
             for j in range(TILES):
-                out[EDGE * sweep + i, 8 * j : 8 * j + 8, :] = dst[kept[i], rows_at(j), :]
+                out[2 * sweep + i, 8 * j : 8 * j + 8, :] = dst[hi - 2 + i, rows_at(j), :]
         src, dst = dst, src
 
     lookup = tables(knots)
-    first = (zero, zero, zero, zero + 1.0)
+    start = (zero, zero, zero, zero + 1.0)
+
+    def rows(j):
+        return pl.ds(pl.multiple_of(8 * j, 8), 8)
+
+    @pl.when(is_first)
+    def _():
+        def shaded(j, unused):
+            carry = start
+            for u in range(HALO):
+                carry = shade(src, FRONT + u, j, carry, lookup, tile)
+            for c in range(4):
+                sums[c, rows(j), :] = carry[c]
+            return unused
+
+        lax.fori_loop(0, TILES, shaded, 0)
+
+    @pl.when(jnp.logical_not(is_first))
+    def _():
+        for c in range(4):
+            for j in range(TILES):
+                sums[c, 8 * j : 8 * j + 8, :] = start[c]
 
     def shaded(j, unused):
         def planes(i, carry):
             for u in range(SHADED):
-                carry = shade(src, HALO + SHADED * i + u, j, carry, lookup, tile)
+                p = FRONT + HALO + SHADED * i + u
+                carry = shade(src, p, j, carry, lookup, tile)
             return carry
 
-        sums = lax.fori_loop(0, (DEEP - 2 * HALO) // SHADED, planes, first)
+        carry = tuple(sums[c, rows(j), :] for c in range(4))
+        carry = lax.fori_loop(0, (DEEP - 2 * HALO) // SHADED, planes, carry)
         for c in range(4):
-            out[EDGE * PASSES + c, pl.ds(pl.multiple_of(8 * j, 8), 8), :] = sums[c]
+            out[2 * PASSES + c, rows(j), :] = carry[c]
         return unused
 
     lax.fori_loop(0, TILES, shaded, 0)
 
 
-def outer_kernel(head, tail, before, after, inner, knots, out, fa, fb, ga, gb, fluxes):
+def outer_kernel(tail, after, inner, knots, out, fa, fb, fluxes):
     tile = Tile()
-    zero = jnp.zeros((8, LANES), jnp.float32)
     lookup = tables(knots)
-
-    def fill(ref, to, source, i):
-        put(ref, to, [source[i // 2, i % 2, 8 * j : 8 * j + 8, :] for j in range(TILES)])
-
+    is_last = tile.block == BLOCKS - 1
+
+    def fill(to, source, i):
+        put(fa, to, [source[i // 2, i % 2, 8 * j : 8 * j + 8, :] for j in range(TILES)])
+
+    near = HALO // PLANES
     for i in range(2):
-        fill(fa, 4 + i, head, i)
-        fill(ga, i, tail, 2 + i)
-
-    @pl.when(tile.block > 0)
-    def _():
-        for i in range(HALO):
-            fill(fa, i, before, i)
-
-    @pl.when(tile.block == 0)
-    def _():
-        for i in range(HALO):
-            fill(fa, i, head, HALO - 1 - i)
-
-    @pl.when(tile.block < BLOCKS - 1)
-    def _():
-        for i in range(HALO):
-            fill(ga, 2 + i, after, i)
-
-    @pl.when(tile.block == BLOCKS - 1)
-    def _():
-        for i in range(HALO):
-            fill(ga, 2 + i, tail, HALO - 1 - i)
-
-    front, back = (fa, fb), (ga, gb)
+        fill(i, tail, 2 * near - 2 + i)
+
+    @pl.when(jnp.logical_not(is_last))
+    def _():
+        for i in range(2 * HALO):
+            fill(2 + i, after, i)
+
+    @pl.when(is_last)
+    def _():
+        for i in range(2 * HALO):
+            fill(2 + i, tail, max(HALO - 1 - i, 0))
+
+    src, dst = fa, fb
     for sweep in range(PASSES):
-        for (src, dst), at in ((front, 0), (back, 2)):
-            carry = first_flux(src, 0)
-            for i in range(4):
-                carry = diffuse(src, i + 1, dst, at + i, fluxes, at // 2 * 4 + i, carry, tile)
+        carry = first_flux(src, 0)
+        for i in range(2 * HALO):
+            carry = diffuse(src, i + 1, dst, i + 2, fluxes, i, carry, tile)
         for i in range(2):
-            for ref, to, k in ((front[1], 4 + i, i), (back[1], i, 2 + i)):
-                k += EDGE * sweep
-                put(ref, to, [inner[k, 8 * j : 8 * j + 8, :] for j in range(TILES)])
-        front, back = front[::-1], back[::-1]
+            rest = [inner[2 * sweep + i, 8 * j : 8 * j + 8, :] for j in range(TILES)]
+            put(dst, i, rest)
+        src, dst = dst, src
 
     lane = lane_index()
     for j in range(TILES):
-        carry = (zero, zero, zero, zero + 1.0)
-        for i in range(4):
-            carry = shade(front[0], i + 1, j, carry, lookup, tile)
-        mid = [inner[EDGE * PASSES + c, 8 * j : 8 * j + 8, :] for c in range(4)]
-        end = (zero, zero, zero, zero + 1.0)
-        for i in range(4):
-            end = shade(back[0], i + 1, j, end, lookup, tile)
-        sums = [carry[c] + carry[3] * (mid[c] + mid[3] * end[c]) for c in range(3)]
-        sums.append(carry[3] * mid[3] * end[3])
+        sums = tuple(inner[2 * PASSES + c, 8 * j : 8 * j + 8, :] for c in range(4))
+        for i in range(2 * HALO):
+            if i == HALO:
+                own = sums
+            sums = shade(src, i + 1, j, sums, lookup, tile)
+        sums = [jnp.where(is_last, own[c], sums[c]) for c in range(4)]
         for k in range(SEGS):
             value = None
             for c in range(4):
@@ -370,7 +424,7 @@
             ]
 
 
-def call(kernel, shape, scratch, *operands):
+def call(kernel, shape, scratch, *operands, **options):
     spec = pl.BlockSpec(memory_space=VMEM)
     operands = [pltpu.with_memory_space_constraint(x, VMEM) for x in operands]
     return pl.pallas_call(
@@ -380,6 +434,7 @@
         out_specs=spec,
         scratch_shapes=[VMEM(s, jnp.float32) for s in scratch],
         name=kernel.__name__,
+        **options,
     )(*operands)
 
 
@@ -390,39 +445,53 @@
 
 
 def per_device(density, transfer_table):
-    above = shifted(density[:, BAND - 8 :], "rows", 1)
-    below = shifted(density[:, :8], "rows", -1)
+    first, last = density[:, :8], density[:, BAND - 8 :]
+    above = shifted(last, "rows", 1)
+    below = shifted(first, "rows", -1)
+    chunks = (GROUP, PLANES, SEG_ROWS, LANES)
+    cut = pl.pallas_call(
+        pack_kernel,
+        out_shape=VMEM(chunks, jnp.float32),
+        in_specs=[pl.BlockSpec(memory_space=pl.ANY)],
+        out_specs=pl.BlockSpec(memory_space=VMEM),
+        scratch_shapes=[
+            VMEM((PLANES, BAND, COLS), jnp.float32),
+            VMEM((PLANES, SEGS * SEG_ROWS, COLS), jnp.float32),
+            pltpu.SemaphoreType.DMA,
+        ],
+        name="pack_kernel",
+    )(density)
     sent = call(
-        pack_kernel,
-        (GROUP, PLANES, SEG_ROWS, LANES),
-        [(PLANES, SEGS * SEG_ROWS, COLS)],
-        density,
+        halo_kernel,
+        chunks,
+        [(PLANES, 8, COLS)],
+        cut,
+        first,
+        last,
         above,
         below,
+        input_output_aliases={0: 0},
     )
     groups = [[GROUP * b + i for i in range(GROUP)] for b in range(BLOCKS)]
     mine = lax.all_to_all(sent, "depth", 0, 0, axis_index_groups=groups, tiled=True)
     near = HALO // PLANES
-    head, tail = mine[:near], mine[GROUP - near :]
-    before = shifted(tail, "depth", GROUP)
-    after = shifted(head, "depth", -GROUP)
+    tail = mine[GROUP - near :]
+    after = shifted(mine[: 2 * near], "depth", -GROUP)
     knots = transfer_table.T
-    field = (DEEP, TALL, LANES)
+    field = (FRONT + DEEP, TALL, LANES)
     inner = call(
         inner_kernel,
-        (EDGE * PASSES + 4, SEG_ROWS, LANES),
-        [field, field, (UNROLL, TALL, LANES)],
+        (2 * PASSES + 4, SEG_ROWS, LANES),
+        [field, field, (UNROLL, TALL, LANES), (4, SEG_ROWS, LANES)],
         mine,
         knots,
     )
-    few = (6, TALL, LANES)
+    few = (2 * HALO + 2, TALL, LANES)
     partial = call(
         outer_kernel,
         (BAND, LANES),
-        [few, few, few, few, (8, TALL, LANES)],
-        head,
+        [few, few, (2 * HALO, TALL, LANES)],
         tail,
-        before,
         after,
         inner,
         knots,

time: 84.3 us -> 77.4 us (0.918)
  starting transfers between devices: 10.5 us -> 6.51 us
  waiting for transfers between devices: 3.36 us -> 1.33 us
  Pallas kernels: 9.87 us -> 11.8 us
  blocking collectives: 57.6 us -> 55.8 us
  local copies, waits for them, and re-layouts: 2.53 us -> 1.49 us
    ppermute x4 -> x3, starting transfers between devices: 10.5 us -> 6.51 us  [shifted(): return lax.ppermute(value, axis, pairs)]
    pallas_call x0 -> x1, Pallas kernels: none -> 2.14 us  [per_device(): pl.pallas_call(pack_kernel, out_shape=VMEM(chunks, jnp.float32), in_specs...]
    ppermute x4 -> x3, waiting for transfers between devices: 3.36 us -> 1.33 us  [shifted(): return lax.ppermute(value, axis, pairs)]
    all_to_all x1, blocking collectives: 25.8 us -> 24 us  [per_device(): parts = lax.all_to_all(partial, 'depth', 0, 0, tiled=True)]
    unnamed x6 -> x4, local copies, waits for them, and re-layouts: 1.73 us -> 0.69 us
  transfers between devices with their start and end apart: 4 -> 3, of which waited for: 1 -> 2; matrix products, arithmetic and copies ran while one was open for 0% -> 0% of each run, Pallas kernels for 7% -> 13%
where the time goes in v4:
time: 77.4 us; the launch traced here: 77 us
  blocking collectives  55.8 us (72%)
  Pallas kernels  11.8 us (15%)
  starting transfers between devices  6.51 us (8%)
  local copies, waits for them, and re-layouts  1.49 us (2%)
  waiting for transfers between devices  1.33 us (2%)
    all_to_all x1, blocking collectives, per_device(): lax.all_to_all(sent, 'depth', 0, 0, axis_index_groups=groups, tiled=True)  31.8 us
    all_to_all x1, blocking collectives, per_device(): parts = lax.all_to_all(partial, 'depth', 0, 0, tiled=True)  24 us
    pallas_call x4, Pallas kernels, call(): pl.pallas_call(kernel, out_shape=VMEM(shape, jnp.float32), in_specs=[spec...  9.67 us
    ppermute x3, starting transfers between devices, shifted(): return lax.ppermute(value, axis, pairs)  6.51 us
    pallas_call x1, Pallas kernels, per_device(): pl.pallas_call(pack_kernel, out_shape=VMEM(chunks, jnp.float32), in_specs...  2.14 us
  transfers between devices with their start and end apart: 3, of which 2 were waited for; matrix products, arithmetic and copies ran while one was open for 0% of the time, Pallas kernels for 13%

profile of v4, /device:TPU:1, one launch (start us, length us, event | category | flops | bytes accessed | tf_op | source)
XLA Modules:
  0.0 77.0 jit_solution(17447447423357360844)
XLA Ops:
  0.0 0.8 %fusion = (f32[2,8,512]{2,1,0:T(8,128)S(1)}, f32[2,8,512]{2,1,0:T(8,128)S(1)}) fusion(f32[2,128,512]{2,1,0:T(8,128)} %density.1), kind=kLoop, calls=%fused_computation | loop fusion | bytes 131072 | tf_op jit(solution)/shard_map/slice | solution.py:448
  0.8 3.9 %collective-permute-start = (f32[2,8,512]{2,1,0:T(8,128)S(1)}, f32[2,8,512]{2,1,0:T(8,128)S(1)}, u32[]{:S(2)}, u32[]{:S(2)}) collective-permute-start(f32[2,8,512]{2,1,0:T(8,128)S(1)} %get-tuple-element.5.last), channel_id=1, source_target_pairs={{0,1},{1,2},{2,3},{4,5},{5,6},{6,7},{8,9},{9,10},{10,11},{12,13},{... | collective-permute-start | bytes 98312 | tf_op jit(solution)/shard_map/ppermute | solution.py:444
  4.7 1.3 %collective-permute-start.1 = (f32[2,8,512]{2,1,0:T(8,128)S(1)}, f32[2,8,512]{2,1,0:T(8,128)S(1)}, u32[]{:S(2)}, u32[]{:S(2)}) collective-permute-start(f32[2,8,512]{2,1,0:T(8,128)S(1)} %get-tuple-element.6.first), channel_id=1, source_target_pairs={{1,0},{2,1},{3,2},{5,4},{6,5},{7,6},{9,8},{10,9},{11,10},{13,12},{... | collective-permute-start | bytes 98312 | tf_op jit(solution)/shard_map/ppermute | solution.py:444
  6.0 2.1 %pack_kernel.1.sent = f32[16,2,48,128]{3,2,1,0:T(8,128)S(1)} custom-call(f32[2,128,512]{2,1,0:T(8,128)} %density.1), custom_call_target="tpu_custom_call" | custom-call | tf_op jit(solution)/shard_map/pack_kernel/pallas_call | solution.py:452
  8.2 0.0 collective-permute-done.above
  8.2 1.2 %collective-permute-done.1.below = f32[2,8,512]{2,1,0:T(8,128)S(1)} collective-permute-done((f32[2,8,512]{2,1,0:T(8,128)S(1)}, f32[2,8,512]{2,1,0:T(8,128)S(1)}, u32[]{:S(2)}, u32[]{:S(2)}) %collective-permute-start.1) | collective-permute-done | bytes 32800 | tf_op jit(solution)/shard_map/ppermute | solution.py:444
  9.4 0.1 halo_kernel.1
  9.5 31.8 %all_to_all.16.mine = f32[16,2,48,128]{3,2,1,0:T(8,128)S(1)} all-to-all(f32[16,2,48,128]{3,2,1,0:T(8,128)S(1)} %halo_kernel.1), channel_id=1, replica_groups={{0,4,8,12,16,20,24,28,32,36,40,44,48,52,56,60},{64,68,72,76,80,84,88,92..., dimensions={0} | all-to-all | bytes 1572864 | tf_op jit(solution)/shard_map/all_to_all | solution.py:476
  41.3 0.0 copy-start
  41.3 1.3 %collective-permute-start.2 = (f32[4,2,48,128]{3,2,1,0:T(8,128)S(1)}, f32[4,2,48,128]{3,2,1,0:T(8,128)S(1)}, u32[]{:S(2)}, u32[]{:S(2)}) collective-permute-start(f32[4,2,48,128]{3,2,1,0:T(8,128)S(1)} %slice.17), channel_id=1, source_target_pairs={{64,0},{68,4},{72,8},{76,12},{80,16},{84,20},{88,24},{92,28},{96,3... | collective-permute-start | bytes 589832 | tf_op jit(solution)/shard_map/ppermute | solution.py:444
  42.6 0.0 copy-done
  42.6 0.1 copy.5
  42.7 7.5 %inner_kernel.1.inner = f32[10,48,128]{2,1,0:T(8,128)S(1)} custom-call(f32[16,2,48,128]{3,2,1,0:T(8,128)S(1)} %all_to_all.16.mine, f32[16,4]{1,0:T(8,128)S(1)} %bitcast.7), custom_call_target="tpu_custom_call" | custom-call | tf_op jit(solution)/shard_map/inner_kernel/pallas_call | solution.py:430
  50.3 0.1 collective-permute-done.2.after
  50.4 1.8 %outer_kernel.1 = f32[128,128]{1,0:T(8,128)S(1)} custom-call(f32[2,2,48,128]{3,2,1,0:T(8,128)S(1)} %slice.16.tail, f32[4,2,48,128]{3,2,1,0:T(8,128)S(1)} %collective-permute-done.2.after, f32[10,48,128]{2,1,0:T(8,128)S(1)} %inner_kernel.1.inner, f32[16,4]{1,0:T(8,128)S(1)} %bitcast.8), custom_call_target="tpu_custom_call" | custom-call | tf_op jit(solution)/shard_map/outer_kernel/pallas_call | solution.py:430
  52.2 24.0 %all_to_all.17 = f32[128,1,128]{2,1,0:T(1,128)S(1)} all-to-all(f32[128,1,128]{2,1,0:T(1,128)S(1)} %bitcast.5), channel_id=1, replica_groups=mesh['depth'=128,'rows'=4] {'depth'}, dimensions={0} | all-to-all | bytes 131072 | tf_op jit(solution)/shard_map/all_to_all | solution.py:499
  76.2 0.2 gather_kernel.1
  76.4 0.6 copy.8
  (2 shorter events, 0.0 us)
Async XLA Ops:
  0.8 7.4 %collective-permute-start = (f32[2,8,512]{2,1,0:T(8,128)S(1)}, f32[2,8,512]{2,1,0:T(8,128)S(1)}, u32[]{:S(2)}, u32[]{:S(2)}) collective-permute-start(f32[2,8,512]{2,1,0:T(8,128)S(1)} %get-tuple-element.5.last), channel_id=1, source_target_pairs={{0,1},{1,2},{2,3},{4,5},{5,6},{6,7},{8,9},{9,10},{10,11},{12,13},{... | collective-permute-start | bytes 98312 | tf_op jit(solution)/shard_map/ppermute | solution.py:444
  4.7 4.7 %collective-permute-start.1 = (f32[2,8,512]{2,1,0:T(8,128)S(1)}, f32[2,8,512]{2,1,0:T(8,128)S(1)}, u32[]{:S(2)}, u32[]{:S(2)}) collective-permute-start(f32[2,8,512]{2,1,0:T(8,128)S(1)} %get-tuple-element.6.first), channel_id=1, source_target_pairs={{1,0},{2,1},{3,2},{5,4},{6,5},{7,6},{9,8},{10,9},{11,10},{13,12},{... | collective-permute-start | bytes 98312 | tf_op jit(solution)/shard_map/ppermute | solution.py:444
  41.3 1.3 %copy-start = (f32[4,16]{1,0:T(4,128)S(1)}, f32[4,16]{1,0:T(4,128)}, u32[]{:S(2)}) copy-start(f32[4,16]{1,0:T(4,128)} %param.3) | copy-start | bytes 772
  41.3 9.1 %collective-permute-start.2 = (f32[4,2,48,128]{3,2,1,0:T(8,128)S(1)}, f32[4,2,48,128]{3,2,1,0:T(8,128)S(1)}, u32[]{:S(2)}, u32[]{:S(2)}) collective-permute-start(f32[4,2,48,128]{3,2,1,0:T(8,128)S(1)} %slice.17), channel_id=1, source_target_pairs={{64,0},{68,4},{72,8},{76,12},{80,16},{84,20},{88,24},{92,28},{96,3... | collective-permute-start | bytes 589832 | tf_op jit(solution)/shard_map/ppermute | solution.py:444

commit v5 on v4

--- a/solution.py
+++ b/solution.py
@@ -61,15 +61,31 @@
         yield t, m, value
 
 
-def pack_kernel(density, out, own, ext, sem):
-    copy = pltpu.make_async_copy(density, own, sem)
-    copy.start()
+def load_kernel(density, own, first, last, sems):
+    copies = [
+        (density.at[:, pl.ds(0, 8), :], first),
+        (density.at[:, pl.ds(BAND - 8, 8), :], last),
+    ]
+    rows = BAND // 4
+    for p in range(PLANES):
+        for i in range(4):
+            part = pl.ds(rows * i, rows)
+            copies.append((density.at[p, part, :], own.at[p, part, :]))
+    started = [
+        pltpu.make_async_copy(source, to, sems.at[i]) for i, (source, to) in enumerate(copies)
+    ]
+    for copy in started:
+        copy.start()
+    for copy in started:
+        copy.wait()
+
+
+def pack_kernel(own, out, ext):
     rows = SEGS * SEG_ROWS
     for p in range(PLANES):
         ext[p, :8, :] = jnp.zeros((8, COLS), jnp.float32)
         ext[p, rows - 16 :, :] = jnp.zeros((16, COLS), jnp.float32)
     segment, left, right = window_masks()
-    copy.wait()
     for p in range(PLANES):
         ext[p, HALO : HALO + BAND, :] = own[p]
 
@@ -445,22 +461,19 @@
 
 
 def per_device(density, transfer_table):
-    first, last = density[:, :8], density[:, BAND - 8 :]
+    edge = VMEM((PLANES, 8, COLS), jnp.float32)
+    own, first, last = pl.pallas_call(
+        load_kernel,
+        out_shape=[VMEM(density.shape, jnp.float32), edge, edge],
+        in_specs=[pl.BlockSpec(memory_space=pl.ANY)],
+        out_specs=[pl.BlockSpec(memory_space=VMEM)] * 3,
+        scratch_shapes=[pltpu.SemaphoreType.DMA((2 + 4 * PLANES,))],
+        name="load_kernel",
+    )(density)
     above = shifted(last, "rows", 1)
     below = shifted(first, "rows", -1)
     chunks = (GROUP, PLANES, SEG_ROWS, LANES)
-    cut = pl.pallas_call(
-        pack_kernel,
-        out_shape=VMEM(chunks, jnp.float32),
-        in_specs=[pl.BlockSpec(memory_space=pl.ANY)],
-        out_specs=pl.BlockSpec(memory_space=VMEM),
-        scratch_shapes=[
-            VMEM((PLANES, BAND, COLS), jnp.float32),
-            VMEM((PLANES, SEGS * SEG_ROWS, COLS), jnp.float32),
-            pltpu.SemaphoreType.DMA,
-        ],
-        name="pack_kernel",
-    )(density)
+    cut = call(pack_kernel, chunks, [(PLANES, SEGS * SEG_ROWS, COLS)], own)
     sent = call(
         halo_kernel,
         chunks,

time: 77.4 us -> 77.7 us (level)
  waiting for transfers between devices: 1.33 us -> 2.46 us
  local copies, waits for them, and re-layouts: 1.49 us -> 0.71 us
    ppermute x3, waiting for transfers between devices: 1.33 us -> 2.46 us  [shifted(): return lax.ppermute(value, axis, pairs)]
    pallas_call x4 -> x5, Pallas kernels: 9.67 us -> 10.7 us  [call(): pl.pallas_call(kernel, out_shape=VMEM(shape, jnp.float32), in_specs=[spec...]
    pallas_call x1, Pallas kernels: 2.14 us -> 1.18 us  [per_device(): pl.pallas_call(load_kernel, out_shape=[VMEM(density.shape, jnp.float32),...]
    slice x1 -> x0, local copies, waits for them, and re-layouts: 0.78 us -> none  [per_device(): first, last = (density[:, :8], density[:, BAND - 8:])]
  transfers between devices with their start and end apart: 3 -> 3, of which waited for: 2 -> 2; matrix products, arithmetic and copies ran while one was open for 0% -> 0% of each run, Pallas kernels for 13% -> 11%
where the time goes in v5:
time: 77.7 us; the launch traced here: 77.4 us
  blocking collectives  55.8 us (72%)
  Pallas kernels  11.9 us (15%)
  starting transfers between devices  6.52 us (8%)
  waiting for transfers between devices  2.46 us (3%)
    all_to_all x1, blocking collectives, per_device(): lax.all_to_all(sent, 'depth', 0, 0, axis_index_groups=groups, tiled=True)  31.8 us
    all_to_all x1, blocking collectives, per_device(): parts = lax.all_to_all(partial, 'depth', 0, 0, tiled=True)  24 us
    pallas_call x5, Pallas kernels, call(): pl.pallas_call(kernel, out_shape=VMEM(shape, jnp.float32), in_specs=[spec...  10.7 us
    ppermute x3, starting transfers between devices, shifted(): return lax.ppermute(value, axis, pairs)  6.52 us
    ppermute x3, waiting for transfers between devices, shifted(): return lax.ppermute(value, axis, pairs)  2.46 us
  transfers between devices with their start and end apart: 3, of which 2 were waited for; matrix products, arithmetic and copies ran while one was open for 0% of the time, Pallas kernels for 11%

profile of v5, /device:TPU:1, one launch (start us, length us, event | category | flops | bytes accessed | tf_op | source)
XLA Modules:
  0.0 77.4 jit_solution(7175058019333284072)
XLA Ops:
  0.0 1.2 %load_kernel.1 = (f32[2,128,512]{2,1,0:T(8,128)S(1)}, f32[2,8,512]{2,1,0:T(8,128)S(1)}, f32[2,8,512]{2,1,0:T(8,128)S(1)}) custom-call(f32[2,128,512]{2,1,0:T(8,128)} %density.1), custom_call_target="tpu_custom_call" | custom-call | tf_op jit(solution)/shard_map/load_kernel/pallas_call | solution.py:465
  1.2 3.9 %collective-permute-start = (f32[2,8,512]{2,1,0:T(8,128)S(1)}, f32[2,8,512]{2,1,0:T(8,128)S(1)}, u32[]{:S(2)}, u32[]{:S(2)}) collective-permute-start(f32[2,8,512]{2,1,0:T(8,128)S(1)} %get-tuple-element.10.last), channel_id=1, source_target_pairs={{0,1},{1,2},{2,3},{4,5},{5,6},{6,7},{8,9},{9,10},{10,11},{12,13},{... | collective-permute-start | bytes 98312 | tf_op jit(solution)/shard_map/ppermute | solution.py:460
  5.1 1.3 %collective-permute-start.1 = (f32[2,8,512]{2,1,0:T(8,128)S(1)}, f32[2,8,512]{2,1,0:T(8,128)S(1)}, u32[]{:S(2)}, u32[]{:S(2)}) collective-permute-start(f32[2,8,512]{2,1,0:T(8,128)S(1)} %get-tuple-element.9.first), channel_id=1, source_target_pairs={{1,0},{2,1},{3,2},{5,4},{6,5},{7,6},{9,8},{10,9},{11,10},{13,12},{... | collective-permute-start | bytes 98312 | tf_op jit(solution)/shard_map/ppermute | solution.py:460
  6.4 1.0 %pack_kernel.1.sent = f32[16,2,48,128]{3,2,1,0:T(8,128)S(1)} custom-call(f32[2,128,512]{2,1,0:T(8,128)S(1)} %get-tuple-element.8.own), custom_call_target="tpu_custom_call" | custom-call | tf_op jit(solution)/shard_map/pack_kernel/pallas_call | solution.py:446
  7.5 0.0 collective-permute-done.above
  7.5 2.3 %collective-permute-done.1.below = f32[2,8,512]{2,1,0:T(8,128)S(1)} collective-permute-done((f32[2,8,512]{2,1,0:T(8,128)S(1)}, f32[2,8,512]{2,1,0:T(8,128)S(1)}, u32[]{:S(2)}, u32[]{:S(2)}) %collective-permute-start.1) | collective-permute-done | bytes 32800 | tf_op jit(solution)/shard_map/ppermute | solution.py:460
  9.8 0.1 halo_kernel.1
  9.9 31.8 %all_to_all.16.mine = f32[16,2,48,128]{3,2,1,0:T(8,128)S(1)} all-to-all(f32[16,2,48,128]{3,2,1,0:T(8,128)S(1)} %halo_kernel.1), channel_id=1, replica_groups={{0,4,8,12,16,20,24,28,32,36,40,44,48,52,56,60},{64,68,72,76,80,84,88,92..., dimensions={0} | all-to-all | bytes 1572864 | tf_op jit(solution)/shard_map/all_to_all | solution.py:489
  41.7 0.0 copy-start
  41.8 1.3 %collective-permute-start.2 = (f32[4,2,48,128]{3,2,1,0:T(8,128)S(1)}, f32[4,2,48,128]{3,2,1,0:T(8,128)S(1)}, u32[]{:S(2)}, u32[]{:S(2)}) collective-permute-start(f32[4,2,48,128]{3,2,1,0:T(8,128)S(1)} %slice.9), channel_id=1, source_target_pairs={{64,0},{68,4},{72,8},{76,12},{80,16},{84,20},{88,24},{92,28},{96,3... | collective-permute-start | bytes 589832 | tf_op jit(solution)/shard_map/ppermute | solution.py:460
  43.1 0.0 copy-done
  43.1 0.1 copy.5
  43.2 7.5 %inner_kernel.1.inner = f32[10,48,128]{2,1,0:T(8,128)S(1)} custom-call(f32[16,2,48,128]{3,2,1,0:T(8,128)S(1)} %all_to_all.16.mine, f32[16,4]{1,0:T(8,128)S(1)} %bitcast.7), custom_call_target="tpu_custom_call" | custom-call | tf_op jit(solution)/shard_map/inner_kernel/pallas_call | solution.py:446
  50.7 0.1 collective-permute-done.2.after
  50.8 1.8 %outer_kernel.1 = f32[128,128]{1,0:T(8,128)S(1)} custom-call(f32[2,2,48,128]{3,2,1,0:T(8,128)S(1)} %slice.8.tail, f32[4,2,48,128]{3,2,1,0:T(8,128)S(1)} %collective-permute-done.2.after, f32[10,48,128]{2,1,0:T(8,128)S(1)} %inner_kernel.1.inner, f32[16,4]{1,0:T(8,128)S(1)} %bitcast.8), custom_call_target="tpu_custom_call" | custom-call | tf_op jit(solution)/shard_map/outer_kernel/pallas_call | solution.py:446
  52.7 24.0 %all_to_all.17 = f32[128,1,128]{2,1,0:T(1,128)S(1)} all-to-all(f32[128,1,128]{2,1,0:T(1,128)S(1)} %bitcast.5), channel_id=1, replica_groups=mesh['depth'=128,'rows'=4] {'depth'}, dimensions={0} | all-to-all | bytes 131072 | tf_op jit(solution)/shard_map/all_to_all | solution.py:512
  76.6 0.2 gather_kernel.1
  76.8 0.6 copy.8
  (2 shorter events, 0.0 us)
Async XLA Ops:
  1.2 6.3 %collective-permute-start = (f32[2,8,512]{2,1,0:T(8,128)S(1)}, f32[2,8,512]{2,1,0:T(8,128)S(1)}, u32[]{:S(2)}, u32[]{:S(2)}) collective-permute-start(f32[2,8,512]{2,1,0:T(8,128)S(1)} %get-tuple-element.10.last), channel_id=1, source_target_pairs={{0,1},{1,2},{2,3},{4,5},{5,6},{6,7},{8,9},{9,10},{10,11},{12,13},{... | collective-permute-start | bytes 98312 | tf_op jit(solution)/shard_map/ppermute | solution.py:460
  5.1 4.7 %collective-permute-start.1 = (f32[2,8,512]{2,1,0:T(8,128)S(1)}, f32[2,8,512]{2,1,0:T(8,128)S(1)}, u32[]{:S(2)}, u32[]{:S(2)}) collective-permute-start(f32[2,8,512]{2,1,0:T(8,128)S(1)} %get-tuple-element.9.first), channel_id=1, source_target_pairs={{1,0},{2,1},{3,2},{5,4},{6,5},{7,6},{9,8},{10,9},{11,10},{13,12},{... | collective-permute-start | bytes 98312 | tf_op jit(solution)/shard_map/ppermute | solution.py:460
  41.7 1.3 %copy-start = (f32[4,16]{1,0:T(4,128)S(1)}, f32[4,16]{1,0:T(4,128)}, u32[]{:S(2)}) copy-start(f32[4,16]{1,0:T(4,128)} %param.3) | copy-start | bytes 772
  41.8 9.1 %collective-permute-start.2 = (f32[4,2,48,128]{3,2,1,0:T(8,128)S(1)}, f32[4,2,48,128]{3,2,1,0:T(8,128)S(1)}, u32[]{:S(2)}, u32[]{:S(2)}) collective-permute-start(f32[4,2,48,128]{3,2,1,0:T(8,128)S(1)} %slice.9), channel_id=1, source_target_pairs={{64,0},{68,4},{72,8},{76,12},{80,16},{84,20},{88,24},{92,28},{96,3... | collective-permute-start | bytes 589832 | tf_op jit(solution)/shard_map/ppermute | solution.py:460

commit v6 on v4

--- a/solution.py
+++ b/solution.py
@@ -29,6 +29,7 @@
 TOP = 8
 TALL = SEG_ROWS + 2 * TOP
 FRONT = HALO
+PARTS = 4
 UNROLL = 7
 SHADED = 8
 VMEM = pltpu.VMEM
@@ -61,25 +62,39 @@
         yield t, m, value
 
 
-def pack_kernel(density, out, own, ext, sem):
-    copy = pltpu.make_async_copy(density, own, sem)
-    copy.start()
+def slice_kernel(density, first, last, sems):
+    copies = [
+        pltpu.make_async_copy(density.at[:, pl.ds(row, 8), :], to, sems.at[i])
+        for i, (row, to) in enumerate(((0, first), (BAND - 8, last)))
+    ]
+    for copy in copies:
+        copy.start()
+    for copy in copies:
+        copy.wait()
+
+
+def pack_kernel(density, out, own, ext, sems):
     rows = SEGS * SEG_ROWS
+    part = BAND // PARTS
+    copies = []
+    for p in range(PLANES):
+        for i in range(PARTS):
+            at = pl.ds(part * i, part)
+            copies.append(
+                pltpu.make_async_copy(density.at[p, at, :], own.at[p, at, :], sems.at[p, i])
+            )
+    for copy in copies:
+        copy.start()
     for p in range(PLANES):
         ext[p, :8, :] = jnp.zeros((8, COLS), jnp.float32)
         ext[p, rows - 16 :, :] = jnp.zeros((16, COLS), jnp.float32)
     segment, left, right = window_masks()
-    copy.wait()
-    for p in range(PLANES):
-        ext[p, HALO : HALO + BAND, :] = own[p]
 
     def joined(rolled, q, m):
         rest = jnp.where(segment[m][1], rolled[1][q], rolled[2][q])
         return jnp.where(segment[m][0], rolled[0][q], rest)
 
-    def step(it, carry):
-        p = it // TILES
-        j = it - TILES * p
+    def step(j, p):
         row = pl.multiple_of(8 * j, 8)
         rolled = []
         for k in range(SEGS):
@@ -88,9 +103,14 @@
             rolled.append([pltpu.roll(x, WIDE * k, 1) if k else x for x in tiles])
         for t, m, value in windows(rolled, joined, left, right):
             out[t, p, pl.ds(row, 8), :] = value
-        return carry
-
-    lax.fori_loop(0, PLANES * TILES, step, 0)
+        return p
+
+    for p in range(PLANES):
+        for copy in copies[PARTS * p : PARTS * (p + 1)]:
+            copy.wait()
+        ext[p, HALO : HALO + BAND, :] = own[p]
+        for j in range(TILES):
+            step(j, p)
 
 
 def halo_kernel(sent, first, last, above, below, out, edge):
@@ -445,7 +465,15 @@
 
 
 def per_device(density, transfer_table):
-    first, last = density[:, :8], density[:, BAND - 8 :]
+    edge = VMEM((PLANES, 8, COLS), jnp.float32)
+    first, last = pl.pallas_call(
+        slice_kernel,
+        out_shape=[edge, edge],
+        in_specs=[pl.BlockSpec(memory_space=pl.ANY)],
+        out_specs=[pl.BlockSpec(memory_space=VMEM)] * 2,
+        scratch_shapes=[pltpu.SemaphoreType.DMA((2,))],
+        name="slice_kernel",
+    )(density)
     above = shifted(last, "rows", 1)
     below = shifted(first, "rows", -1)
     chunks = (GROUP, PLANES, SEG_ROWS, LANES)
@@ -457,7 +485,7 @@
         scratch_shapes=[
             VMEM((PLANES, BAND, COLS), jnp.float32),
             VMEM((PLANES, SEGS * SEG_ROWS, COLS), jnp.float32),
-            pltpu.SemaphoreType.DMA,
+            pltpu.SemaphoreType.DMA((PLANES, PARTS)),
         ],
         name="pack_kernel",
     )(density)

time: 77.4 us -> 77.4 us (level)
  waiting for transfers between devices: 1.33 us -> 2.2 us
  local copies, waits for them, and re-layouts: 1.49 us -> 0.71 us
    pallas_call x1, Pallas kernels: 2.14 us -> 1.27 us  [per_device(): pl.pallas_call(pack_kernel, out_shape=VMEM(chunks, jnp.float32), in_specs...]
    ppermute x3, waiting for transfers between devices: 1.33 us -> 2.2 us  [shifted(): return lax.ppermute(value, axis, pairs)]
    pallas_call x0 -> x1, Pallas kernels: none -> 0.79 us  [per_device(): pl.pallas_call(slice_kernel, out_shape=[edge, edge], in_specs=[pl.BlockSp...]
    slice x1 -> x0, local copies, waits for them, and re-layouts: 0.78 us -> none  [per_device(): first, last = (density[:, :8], density[:, BAND - 8:])]
  transfers between devices with their start and end apart: 3 -> 3, of which waited for: 2 -> 2; matrix products, arithmetic and copies ran while one was open for 0% -> 0% of each run, Pallas kernels for 13% -> 11%
where the time goes in v6:
time: 77.4 us; the launch traced here: 77 us
  blocking collectives  55.8 us (72%)
  Pallas kernels  11.7 us (15%)
  starting transfers between devices  6.52 us (8%)
  waiting for transfers between devices  2.2 us (3%)
    all_to_all x1, blocking collectives, per_device(): lax.all_to_all(sent, 'depth', 0, 0, axis_index_groups=groups, tiled=True)  31.8 us
    all_to_all x1, blocking collectives, per_device(): parts = lax.all_to_all(partial, 'depth', 0, 0, tiled=True)  24 us
    pallas_call x4, Pallas kernels, call(): pl.pallas_call(kernel, out_shape=VMEM(shape, jnp.float32), in_specs=[spec...  9.67 us
    ppermute x3, starting transfers between devices, shifted(): return lax.ppermute(value, axis, pairs)  6.52 us
    ppermute x3, waiting for transfers between devices, shifted(): return lax.ppermute(value, axis, pairs)  2.2 us
  transfers between devices with their start and end apart: 3, of which 2 were waited for; matrix products, arithmetic and copies ran while one was open for 0% of the time, Pallas kernels for 11%

profile of v6, /device:TPU:1, one launch (start us, length us, event | category | flops | bytes accessed | tf_op | source)
XLA Modules:
  0.0 77.0 jit_solution(657697748347917338)
XLA Ops:
  0.0 0.8 %slice_kernel.1 = (f32[2,8,512]{2,1,0:T(8,128)S(1)}, f32[2,8,512]{2,1,0:T(8,128)S(1)}) custom-call(f32[2,128,512]{2,1,0:T(8,128)} %density.3), custom_call_target="tpu_custom_call" | custom-call | tf_op jit(solution)/shard_map/slice_kernel/pallas_call | solution.py:469
  0.8 3.9 %collective-permute-start = (f32[2,8,512]{2,1,0:T(8,128)S(1)}, f32[2,8,512]{2,1,0:T(8,128)S(1)}, u32[]{:S(2)}, u32[]{:S(2)}) collective-permute-start(f32[2,8,512]{2,1,0:T(8,128)S(1)} %get-tuple-element.8.last), channel_id=1, source_target_pairs={{0,1},{1,2},{2,3},{4,5},{5,6},{6,7},{8,9},{9,10},{10,11},{12,13},{... | collective-permute-start | bytes 98312 | tf_op jit(solution)/shard_map/ppermute | solution.py:464
  4.7 1.3 %collective-permute-start.1 = (f32[2,8,512]{2,1,0:T(8,128)S(1)}, f32[2,8,512]{2,1,0:T(8,128)S(1)}, u32[]{:S(2)}, u32[]{:S(2)}) collective-permute-start(f32[2,8,512]{2,1,0:T(8,128)S(1)} %get-tuple-element.7.first), channel_id=1, source_target_pairs={{1,0},{2,1},{3,2},{5,4},{6,5},{7,6},{9,8},{10,9},{11,10},{13,12},{... | collective-permute-start | bytes 98312 | tf_op jit(solution)/shard_map/ppermute | solution.py:464
  6.0 1.3 %pack_kernel.1.sent = f32[16,2,48,128]{3,2,1,0:T(8,128)S(1)} custom-call(f32[2,128,512]{2,1,0:T(8,128)} %density.3), custom_call_target="tpu_custom_call" | custom-call | tf_op jit(solution)/shard_map/pack_kernel/pallas_call | solution.py:480
  7.3 0.0 collective-permute-done.above
  7.3 2.1 %collective-permute-done.1.below = f32[2,8,512]{2,1,0:T(8,128)S(1)} collective-permute-done((f32[2,8,512]{2,1,0:T(8,128)S(1)}, f32[2,8,512]{2,1,0:T(8,128)S(1)}, u32[]{:S(2)}, u32[]{:S(2)}) %collective-permute-start.1) | collective-permute-done | bytes 32800 | tf_op jit(solution)/shard_map/ppermute | solution.py:464
  9.4 0.1 halo_kernel.1
  9.5 31.8 %all_to_all.16.mine = f32[16,2,48,128]{3,2,1,0:T(8,128)S(1)} all-to-all(f32[16,2,48,128]{3,2,1,0:T(8,128)S(1)} %halo_kernel.1), channel_id=1, replica_groups={{0,4,8,12,16,20,24,28,32,36,40,44,48,52,56,60},{64,68,72,76,80,84,88,92..., dimensions={0} | all-to-all | bytes 1572864 | tf_op jit(solution)/shard_map/all_to_all | solution.py:504
  41.3 0.0 copy-start
  41.4 1.3 %collective-permute-start.2 = (f32[4,2,48,128]{3,2,1,0:T(8,128)S(1)}, f32[4,2,48,128]{3,2,1,0:T(8,128)S(1)}, u32[]{:S(2)}, u32[]{:S(2)}) collective-permute-start(f32[4,2,48,128]{3,2,1,0:T(8,128)S(1)} %slice.9), channel_id=1, source_target_pairs={{64,0},{68,4},{72,8},{76,12},{80,16},{84,20},{88,24},{92,28},{96,3... | collective-permute-start | bytes 589832 | tf_op jit(solution)/shard_map/ppermute | solution.py:464
  42.7 0.0 copy-done
  42.7 0.1 copy.5
  42.8 7.5 %inner_kernel.1.inner = f32[10,48,128]{2,1,0:T(8,128)S(1)} custom-call(f32[16,2,48,128]{3,2,1,0:T(8,128)S(1)} %all_to_all.16.mine, f32[16,4]{1,0:T(8,128)S(1)} %bitcast.7), custom_call_target="tpu_custom_call" | custom-call | tf_op jit(solution)/shard_map/inner_kernel/pallas_call | solution.py:450
  50.3 0.1 collective-permute-done.2.after
  50.4 1.8 %outer_kernel.1 = f32[128,128]{1,0:T(8,128)S(1)} custom-call(f32[2,2,48,128]{3,2,1,0:T(8,128)S(1)} %slice.8.tail, f32[4,2,48,128]{3,2,1,0:T(8,128)S(1)} %collective-permute-done.2.after, f32[10,48,128]{2,1,0:T(8,128)S(1)} %inner_kernel.1.inner, f32[16,4]{1,0:T(8,128)S(1)} %bitcast.8), custom_call_target="tpu_custom_call" | custom-call | tf_op jit(solution)/shard_map/outer_kernel/pallas_call | solution.py:450
  52.3 24.0 %all_to_all.17 = f32[128,1,128]{2,1,0:T(1,128)S(1)} all-to-all(f32[128,1,128]{2,1,0:T(1,128)S(1)} %bitcast.5), channel_id=1, replica_groups=mesh['depth'=128,'rows'=4] {'depth'}, dimensions={0} | all-to-all | bytes 131072 | tf_op jit(solution)/shard_map/all_to_all | solution.py:527
  76.2 0.2 gather_kernel.1
  76.4 0.6 copy.8
  (2 shorter events, 0.0 us)
Async XLA Ops:
  0.8 6.5 %collective-permute-start = (f32[2,8,512]{2,1,0:T(8,128)S(1)}, f32[2,8,512]{2,1,0:T(8,128)S(1)}, u32[]{:S(2)}, u32[]{:S(2)}) collective-permute-start(f32[2,8,512]{2,1,0:T(8,128)S(1)} %get-tuple-element.8.last), channel_id=1, source_target_pairs={{0,1},{1,2},{2,3},{4,5},{5,6},{6,7},{8,9},{9,10},{10,11},{12,13},{... | collective-permute-start | bytes 98312 | tf_op jit(solution)/shard_map/ppermute | solution.py:464
  4.7 4.7 %collective-permute-start.1 = (f32[2,8,512]{2,1,0:T(8,128)S(1)}, f32[2,8,512]{2,1,0:T(8,128)S(1)}, u32[]{:S(2)}, u32[]{:S(2)}) collective-permute-start(f32[2,8,512]{2,1,0:T(8,128)S(1)} %get-tuple-element.7.first), channel_id=1, source_target_pairs={{1,0},{2,1},{3,2},{5,4},{6,5},{7,6},{9,8},{10,9},{11,10},{13,12},{... | collective-permute-start | bytes 98312 | tf_op jit(solution)/shard_map/ppermute | solution.py:464
  41.3 1.3 %copy-start = (f32[4,16]{1,0:T(4,128)S(1)}, f32[4,16]{1,0:T(4,128)}, u32[]{:S(2)}) copy-start(f32[4,16]{1,0:T(4,128)} %param.3) | copy-start | bytes 772
  41.4 9.1 %collective-permute-start.2 = (f32[4,2,48,128]{3,2,1,0:T(8,128)S(1)}, f32[4,2,48,128]{3,2,1,0:T(8,128)S(1)}, u32[]{:S(2)}, u32[]{:S(2)}) collective-permute-start(f32[4,2,48,128]{3,2,1,0:T(8,128)S(1)} %slice.9), channel_id=1, source_target_pairs={{64,0},{68,4},{72,8},{76,12},{80,16},{84,20},{88,24},{92,28},{96,3... | collective-permute-start | bytes 589832 | tf_op jit(solution)/shard_map/ppermute | solution.py:464

commit v7 on v6

--- a/solution.py
+++ b/solution.py
@@ -62,11 +62,14 @@
         yield t, m, value
 
 
-def slice_kernel(density, first, last, sems):
-    copies = [
-        pltpu.make_async_copy(density.at[:, pl.ds(row, 8), :], to, sems.at[i])
-        for i, (row, to) in enumerate(((0, first), (BAND - 8, last)))
-    ]
+def slice_kernel(density, out, sems):
+    band = lax.axis_index("rows")
+    copies = []
+    for to in range(out.shape[0]):
+        top = (band > to) | ((band == 0) & (to == 0))
+        row = pl.multiple_of(jnp.where(top, 0, BAND - 8), 8)
+        source = density.at[:, pl.ds(row, 8), :]
+        copies.append(pltpu.make_async_copy(source, out.at[to], sems.at[to]))
     for copy in copies:
         copy.start()
     for copy in copies:
@@ -113,12 +116,13 @@
             step(j, p)
 
 
-def halo_kernel(sent, first, last, above, below, out, edge):
+def halo_kernel(sent, strips, out, edge):
     band = lax.axis_index("rows")
     bands = lax.axis_size("rows")
 
     @pl.when(band > 0)
     def _():
+        above = strips.at[jnp.maximum(band - 1, 0)]
         for p in range(PLANES):
             edge[p, 0:HALO, :] = above[p, 8 - HALO : 8, :]
 
@@ -126,10 +130,11 @@
     def _():
         for p in range(PLANES):
             for i in range(HALO):
-                edge[p, HALO - 1 - i : HALO - i, :] = first[p, i : i + 1, :]
+                edge[p, HALO - 1 - i : HALO - i, :] = strips[0, p, i : i + 1, :]
 
     @pl.when(band < bands - 1)
     def _():
+        below = strips.at[jnp.minimum(band + 1, bands - 1)]
         for p in range(PLANES):
             edge[p, HALO : 2 * HALO, :] = below[p, 0:HALO, :]
 
@@ -137,7 +142,7 @@
     def _():
         for p in range(PLANES):
             for i in range(HALO):
-                edge[p, HALO + i : HALO + i + 1, :] = last[p, 7 - i : 8 - i, :]
+                edge[p, HALO + i : HALO + i + 1, :] = strips[strips.shape[0] - 1, p, 7 - i : 8 - i, :]
 
     segment, left, right = window_masks()
     row = lax.broadcasted_iota(jnp.int32, (8, LANES), 0)
@@ -465,17 +470,16 @@
 
 
 def per_device(density, transfer_table):
-    edge = VMEM((PLANES, 8, COLS), jnp.float32)
-    first, last = pl.pallas_call(
+    bands = lax.axis_size("rows")
+    strips = pl.pallas_call(
         slice_kernel,
-        out_shape=[edge, edge],
+        out_shape=jax.ShapeDtypeStruct((bands, PLANES, 8, COLS), jnp.float32),
         in_specs=[pl.BlockSpec(memory_space=pl.ANY)],
-        out_specs=[pl.BlockSpec(memory_space=VMEM)] * 2,
-        scratch_shapes=[pltpu.SemaphoreType.DMA((2,))],
+        out_specs=pl.BlockSpec(memory_space=pl.ANY),
+        scratch_shapes=[pltpu.SemaphoreType.DMA((bands,))],
         name="slice_kernel",
     )(density)
-    above = shifted(last, "rows", 1)
-    below = shifted(first, "rows", -1)
+    strips = lax.all_to_all(strips, "rows", 0, 0, tiled=True)
     chunks = (GROUP, PLANES, SEG_ROWS, LANES)
     cut = pl.pallas_call(
         pack_kernel,
@@ -494,10 +498,7 @@
         chunks,
         [(PLANES, 8, COLS)],
         cut,
-        first,
-        last,
-        above,
-        below,
+        strips,
         input_output_aliases={0: 0},
     )
     groups = [[GROUP * b + i for i in range(GROUP)] for b in range(BLOCKS)]

time: 77.4 us -> 82.8 us (1.070)
  Pallas kernels: 11.7 us -> 16 us
  waiting for transfers between devices: 2.2 us -> 3.68 us
    ppermute x3 -> x1, starting transfers between devices: 6.52 us -> 1.29 us  [shifted(): return lax.ppermute(value, axis, pairs)]
    all_to_all x0 -> x1, starting transfers between devices: none -> 4.84 us  [per_device(): strips = lax.all_to_all(strips, 'rows', 0, 0, tiled=True)]
    pallas_call x1, Pallas kernels: 0.79 us -> 5.1 us  [per_device(): pl.pallas_call(slice_kernel, out_shape=jax.ShapeDtypeStruct((bands, PLANE...]
    all_to_all x0 -> x1, waiting for transfers between devices: none -> 3.55 us  [per_device(): strips = lax.all_to_all(strips, 'rows', 0, 0, tiled=True)]
    ppermute x3 -> x1, waiting for transfers between devices: 2.2 us -> 0.13 us  [shifted(): return lax.ppermute(value, axis, pairs)]
  transfers between devices with their start and end apart: 3 -> 2, of which waited for: 2 -> 2; matrix products, arithmetic and copies ran while one was open for 0% -> 0% of each run, Pallas kernels for 11% -> 11%
where the time goes in v7:
time: 82.8 us; the launch traced here: 82.4 us
  blocking collectives  55.8 us (67%)
  Pallas kernels  16 us (19%)
  starting transfers between devices  6.13 us (7%)
  waiting for transfers between devices  3.68 us (4%)
    all_to_all x1, blocking collectives, per_device(): lax.all_to_all(sent, 'depth', 0, 0, axis_index_groups=groups, tiled=True)  31.8 us
    all_to_all x1, blocking collectives, per_device(): parts = lax.all_to_all(partial, 'depth', 0, 0, tiled=True)  24 us
    pallas_call x4, Pallas kernels, call(): pl.pallas_call(kernel, out_shape=VMEM(shape, jnp.float32), in_specs=[spec...  9.67 us
    pallas_call x1, Pallas kernels, per_device(): pl.pallas_call(slice_kernel, out_shape=jax.ShapeDtypeStruct((bands, PLANE...  5.1 us
    all_to_all x1, starting transfers between devices, per_device(): strips = lax.all_to_all(strips, 'rows', 0, 0, tiled=True)  4.84 us
    all_to_all x1, waiting for transfers between devices, per_device(): strips = lax.all_to_all(strips, 'rows', 0, 0, tiled=True)  3.55 us
  transfers between devices with their start and end apart: 2, of which 2 were waited for; matrix products, arithmetic and copies ran while one was open for 0% of the time, Pallas kernels for 11%

profile of v7, /device:TPU:1, one launch (start us, length us, event | category | flops | bytes accessed | tf_op | source)
XLA Modules:
  0.0 82.4 jit_solution(15852812032318098167)
XLA Ops:
  0.0 5.1 %slice_kernel.1 = f32[4,2,8,512]{3,2,1,0:T(8,128)} custom-call(f32[2,128,512]{2,1,0:T(8,128)} %density.3), custom_call_target="tpu_custom_call" | custom-call | tf_op jit(solution)/shard_map/slice_kernel/pallas_call | solution.py:474
  5.1 4.8 %all-to-all-start = ((f32[4,2,8,512]{3,2,1,0:T(8,128)}), f32[4,2,8,512]{3,2,1,0:T(8,128)S(1)}, u32[]{:S(2)}, u32[]{:S(2)}) async-start(f32[4,2,8,512]{3,2,1,0:T(8,128)} %slice_kernel.1), calls=%async_computation | async-start | bytes 262144 | tf_op jit(solution)/shard_map/all_to_all | solution.py:482
  10.0 1.3 %pack_kernel.1.sent = f32[16,2,48,128]{3,2,1,0:T(8,128)S(1)} custom-call(f32[2,128,512]{2,1,0:T(8,128)} %density.3), custom_call_target="tpu_custom_call" | custom-call | tf_op jit(solution)/shard_map/pack_kernel/pallas_call | solution.py:484
  11.2 3.6 %all-to-all-done.strips = f32[4,2,8,512]{3,2,1,0:T(8,128)S(1)} async-done(((f32[4,2,8,512]{3,2,1,0:T(8,128)}), f32[4,2,8,512]{3,2,1,0:T(8,128)S(1)}, u32[]{:S(2)}, u32[]{:S(2)}) %all-to-all-start) | async-done | bytes 131104 | tf_op jit(solution)/shard_map/all_to_all | solution.py:482
  14.8 0.1 halo_kernel.1
  14.9 31.8 %all_to_all.21.mine = f32[16,2,48,128]{3,2,1,0:T(8,128)S(1)} all-to-all(f32[16,2,48,128]{3,2,1,0:T(8,128)S(1)} %halo_kernel.1), channel_id=1, replica_groups={{0,4,8,12,16,20,24,28,32,36,40,44,48,52,56,60},{64,68,72,76,80,84,88,92..., dimensions={0} | all-to-all | bytes 1572864 | tf_op jit(solution)/shard_map/all_to_all | solution.py:505
  46.7 0.0 copy-start
  46.8 1.3 %collective-permute-start = (f32[4,2,48,128]{3,2,1,0:T(8,128)S(1)}, f32[4,2,48,128]{3,2,1,0:T(8,128)S(1)}, u32[]{:S(2)}, u32[]{:S(2)}) collective-permute-start(f32[4,2,48,128]{3,2,1,0:T(8,128)S(1)} %slice.9), channel_id=1, source_target_pairs={{64,0},{68,4},{72,8},{76,12},{80,16},{84,20},{88,24},{92,28},{96,3... | collective-permute-start | bytes 589832 | tf_op jit(solution)/shard_map/ppermute | solution.py:469
  48.1 0.0 copy-done
  48.1 0.1 copy.5
  48.2 7.5 %inner_kernel.1.inner = f32[10,48,128]{2,1,0:T(8,128)S(1)} custom-call(f32[16,2,48,128]{3,2,1,0:T(8,128)S(1)} %all_to_all.21.mine, f32[16,4]{1,0:T(8,128)S(1)} %bitcast.7), custom_call_target="tpu_custom_call" | custom-call | tf_op jit(solution)/shard_map/inner_kernel/pallas_call | solution.py:455
  55.7 0.1 collective-permute-done.after
  55.8 1.8 %outer_kernel.1 = f32[128,128]{1,0:T(8,128)S(1)} custom-call(f32[2,2,48,128]{3,2,1,0:T(8,128)S(1)} %slice.8.tail, f32[4,2,48,128]{3,2,1,0:T(8,128)S(1)} %collective-permute-done.after, f32[10,48,128]{2,1,0:T(8,128)S(1)} %inner_kernel.1.inner, f32[16,4]{1,0:T(8,128)S(1)} %bitcast.8), custom_call_target="tpu_custom_call" | custom-call | tf_op jit(solution)/shard_map/outer_kernel/pallas_call | solution.py:455
  57.7 24.0 %all_to_all.22 = f32[128,1,128]{2,1,0:T(1,128)S(1)} all-to-all(f32[128,1,128]{2,1,0:T(1,128)S(1)} %bitcast.5), channel_id=1, replica_groups=mesh['depth'=128,'rows'=4] {'depth'}, dimensions={0} | all-to-all | bytes 131072 | tf_op jit(solution)/shard_map/all_to_all | solution.py:528
  81.6 0.2 gather_kernel.1
  81.8 0.6 copy.8
  (2 shorter events, 0.0 us)
Async XLA Ops:
  5.1 9.7 %all-to-all-start = ((f32[4,2,8,512]{3,2,1,0:T(8,128)}), f32[4,2,8,512]{3,2,1,0:T(8,128)S(1)}, u32[]{:S(2)}, u32[]{:S(2)}) async-start(f32[4,2,8,512]{3,2,1,0:T(8,128)} %slice_kernel.1), calls=%async_computation | async-start | bytes 262144 | tf_op jit(solution)/shard_map/all_to_all | solution.py:482
  46.7 1.3 %copy-start = (f32[4,16]{1,0:T(4,128)S(1)}, f32[4,16]{1,0:T(4,128)}, u32[]{:S(2)}) copy-start(f32[4,16]{1,0:T(4,128)} %param.3) | copy-start | bytes 772
  46.8 9.1 %collective-permute-start = (f32[4,2,48,128]{3,2,1,0:T(8,128)S(1)}, f32[4,2,48,128]{3,2,1,0:T(8,128)S(1)}, u32[]{:S(2)}, u32[]{:S(2)}) collective-permute-start(f32[4,2,48,128]{3,2,1,0:T(8,128)S(1)} %slice.9), channel_id=1, source_target_pairs={{64,0},{68,4},{72,8},{76,12},{80,16},{84,20},{88,24},{92,28},{96,3... | collective-permute-start | bytes 589832 | tf_op jit(solution)/shard_map/ppermute | solution.py:469

commit v8 on v6

--- a/solution.py
+++ b/solution.py
@@ -62,11 +62,13 @@
         yield t, m, value
 
 
-def slice_kernel(density, first, last, sems):
-    copies = [
-        pltpu.make_async_copy(density.at[:, pl.ds(row, 8), :], to, sems.at[i])
-        for i, (row, to) in enumerate(((0, first), (BAND - 8, last)))
-    ]
+def slice_kernel(density, one, two, sems):
+    even = lax.axis_index("rows") % 2 == 0
+    rows = (jnp.where(even, BAND - 8, 0), jnp.where(even, 0, BAND - 8))
+    copies = []
+    for i, (row, to) in enumerate(zip(rows, (one, two))):
+        source = density.at[:, pl.ds(pl.multiple_of(row, 8), 8), :]
+        copies.append(pltpu.make_async_copy(source, to, sems.at[i]))
     for copy in copies:
         copy.start()
     for copy in copies:
@@ -113,31 +115,46 @@
             step(j, p)
 
 
-def halo_kernel(sent, first, last, above, below, out, edge):
+def halo_kernel(sent, two, from_one, from_two, out, edge):
     band = lax.axis_index("rows")
     bands = lax.axis_size("rows")
-
-    @pl.when(band > 0)
-    def _():
+    even = band % 2 == 0
+
+    def above(source):
         for p in range(PLANES):
-            edge[p, 0:HALO, :] = above[p, 8 - HALO : 8, :]
+            edge[p, 0:HALO, :] = source[p, 8 - HALO : 8, :]
+
+    def below(source):
+        for p in range(PLANES):
+            edge[p, HALO : 2 * HALO, :] = source[p, 0:HALO, :]
+
+    @pl.when(even)
+    def _():
+        below(from_one)
+
+    @pl.when(jnp.logical_not(even))
+    def _():
+        above(from_one)
+
+    @pl.when(even & (band > 0))
+    def _():
+        above(from_two)
+
+    @pl.when(jnp.logical_not(even) & (band < bands - 1))
+    def _():
+        below(from_two)
 
     @pl.when(band == 0)
     def _():
         for p in range(PLANES):
             for i in range(HALO):
-                edge[p, HALO - 1 - i : HALO - i, :] = first[p, i : i + 1, :]
-
-    @pl.when(band < bands - 1)
-    def _():
-        for p in range(PLANES):
-            edge[p, HALO : 2 * HALO, :] = below[p, 0:HALO, :]
+                edge[p, HALO - 1 - i : HALO - i, :] = two[p, i : i + 1, :]
 
     @pl.when(band == bands - 1)
     def _():
         for p in range(PLANES):
             for i in range(HALO):
-                edge[p, HALO + i : HALO + i + 1, :] = last[p, 7 - i : 8 - i, :]
+                edge[p, HALO + i : HALO + i + 1, :] = two[p, 7 - i : 8 - i, :]
 
     segment, left, right = window_masks()
     row = lax.broadcasted_iota(jnp.int32, (8, LANES), 0)
@@ -453,7 +470,6 @@
         in_specs=[spec] * len(operands),
         out_specs=spec,
         scratch_shapes=[VMEM(s, jnp.float32) for s in scratch],
-        name=kernel.__name__,
         **options,
     )(*operands)
 
@@ -464,9 +480,10 @@
     return lax.ppermute(value, axis, pairs)
 
 
-def per_device(density, transfer_table):
+def rendered(density, transfer_table):
+    bands = lax.axis_size("rows")
     edge = VMEM((PLANES, 8, COLS), jnp.float32)
-    first, last = pl.pallas_call(
+    one, two = pl.pallas_call(
         slice_kernel,
         out_shape=[edge, edge],
         in_specs=[pl.BlockSpec(memory_space=pl.ANY)],
@@ -474,8 +491,10 @@
         scratch_shapes=[pltpu.SemaphoreType.DMA((2,))],
         name="slice_kernel",
     )(density)
-    above = shifted(last, "rows", 1)
-    below = shifted(first, "rows", -1)
+    pairs = [(i, i + 1) for i in range(0, bands, 2)]
+    from_one = lax.ppermute(one, "rows", pairs + [(b, a) for a, b in pairs])
+    pairs = [(i, i + 1) for i in range(1, bands - 1, 2)]
+    from_two = lax.ppermute(two, "rows", pairs + [(b, a) for a, b in pairs])
     chunks = (GROUP, PLANES, SEG_ROWS, LANES)
     cut = pl.pallas_call(
         pack_kernel,
@@ -494,10 +513,9 @@
         chunks,
         [(PLANES, 8, COLS)],
         cut,
-        first,
-        last,
-        above,
-        below,
+        two,
+        from_one,
+        from_two,
         input_output_aliases={0: 0},
     )
     groups = [[GROUP * b + i for i in range(GROUP)] for b in range(BLOCKS)]
@@ -531,7 +549,7 @@
 def solution(mesh):
     placed = (P("depth", "rows", None), P())
     return jax.shard_map(
-        per_device,
+        rendered,
         mesh=mesh,
         in_specs=placed,
         out_specs=P(None, ("rows", "depth"), None),

time: 77.4 us -> 76.9 us (level)
  waiting for transfers between devices: 2.2 us -> 0.14 us
  starting transfers between devices: 6.52 us -> 8.35 us
    ppermute x0 -> x2, starting transfers between devices: none -> 7.06 us  [the longest x1 6.39 us: rendered(): from_one = lax.ppermute(one, 'rows', pairs + [(b, a) for a, b in pairs])]
    ppermute x3 -> x1, starting transfers between devices: 6.52 us -> 1.29 us  [shifted(): return lax.ppermute(value, axis, pairs)]
    ppermute x3 -> x1, waiting for transfers between devices: 2.2 us -> 0.13 us  [shifted(): return lax.ppermute(value, axis, pairs)]
  transfers between devices with their start and end apart: 3 -> 3, of which waited for: 2 -> 1; matrix products, arithmetic and copies ran while one was open for 0% -> 0% of each run, Pallas kernels for 11% -> 11%
where the time goes in v8:
time: 76.9 us; the launch traced here: 76.5 us
  blocking collectives  55.5 us (72%)
  Pallas kernels  11.8 us (15%)
  starting transfers between devices  8.35 us (11%)
    all_to_all x1, blocking collectives, rendered(): lax.all_to_all(sent, 'depth', 0, 0, axis_index_groups=groups, tiled=True)  31.5 us
    all_to_all x1, blocking collectives, rendered(): parts = lax.all_to_all(partial, 'depth', 0, 0, tiled=True)  24 us
    pallas_call x4, Pallas kernels, call(): pl.pallas_call(kernel, out_shape=VMEM(shape, jnp.float32), in_specs=[spec...  9.7 us
    ppermute x1, starting transfers between devices, rendered(): from_one = lax.ppermute(one, 'rows', pairs + [(b, a) for a, b in pairs])  6.39 us
  transfers between devices with their start and end apart: 3, of which 1 were waited for; matrix products, arithmetic and copies ran while one was open for 0% of the time, Pallas kernels for 11%

profile of v8, /device:TPU:1, one launch (start us, length us, event | category | flops | bytes accessed | tf_op | source)
XLA Modules:
  0.0 76.5 jit_solution(9386636923366893094)
XLA Ops:
  0.0 0.8 %slice_kernel.1 = (f32[2,8,512]{2,1,0:T(8,128)S(1)}, f32[2,8,512]{2,1,0:T(8,128)S(1)}) custom-call(f32[2,128,512]{2,1,0:T(8,128)} %density.3), custom_call_target="tpu_custom_call" | custom-call | tf_op jit(solution)/shard_map/slice_kernel/pallas_call | solution.py:486
  0.8 0.7 collective-permute-start.1
  1.5 6.4 %collective-permute-start = (f32[2,8,512]{2,1,0:T(8,128)S(1)}, f32[2,8,512]{2,1,0:T(8,128)S(1)}, u32[]{:S(2)}, u32[]{:S(2)}) collective-permute-start(f32[2,8,512]{2,1,0:T(8,128)S(1)} %get-tuple-element.8), channel_id=1, source_target_pairs={{0,1},{2,3},{1,0},{3,2},{4,5},{6,7},{5,4},{7,6},{8,9},{10,11},{9,8... | collective-permute-start | bytes 98312 | tf_op jit(solution)/shard_map/ppermute | solution.py:495
  7.9 1.3 %pack_kernel.1.sent = f32[16,2,48,128]{3,2,1,0:T(8,128)S(1)} custom-call(f32[2,128,512]{2,1,0:T(8,128)} %density.3), custom_call_target="tpu_custom_call" | custom-call | tf_op jit(solution)/shard_map/pack_kernel/pallas_call | solution.py:499
  9.2 0.0 collective-permute-done.1.from_two
  9.2 0.0 collective-permute-done.from_one
  9.2 0.1 shard_map.28
  9.3 31.5 %all_to_all.16.mine = f32[16,2,48,128]{3,2,1,0:T(8,128)S(1)} all-to-all(f32[16,2,48,128]{3,2,1,0:T(8,128)S(1)} %shard_map.28), channel_id=1, replica_groups={{0,4,8,12,16,20,24,28,32,36,40,44,48,52,56,60},{64,68,72,76,80,84,88,92..., dimensions={0} | all-to-all | bytes 1572864 | tf_op jit(solution)/shard_map/all_to_all | solution.py:522
  40.8 0.0 copy-start
  40.8 1.3 %collective-permute-start.2 = (f32[4,2,48,128]{3,2,1,0:T(8,128)S(1)}, f32[4,2,48,128]{3,2,1,0:T(8,128)S(1)}, u32[]{:S(2)}, u32[]{:S(2)}) collective-permute-start(f32[4,2,48,128]{3,2,1,0:T(8,128)S(1)} %slice.9), channel_id=1, source_target_pairs={{64,0},{68,4},{72,8},{76,12},{80,16},{84,20},{88,24},{92,28},{96,3... | collective-permute-start | bytes 589832 | tf_op jit(solution)/shard_map/ppermute | solution.py:480
  42.1 0.0 copy-done
  42.2 0.1 copy.5
  42.3 7.5 %shard_map.29.inner = f32[10,48,128]{2,1,0:T(8,128)S(1)} custom-call(f32[16,2,48,128]{3,2,1,0:T(8,128)S(1)} %all_to_all.16.mine, f32[16,4]{1,0:T(8,128)S(1)} %bitcast.7), custom_call_target="tpu_custom_call" | custom-call | tf_op jit(solution)/shard_map/pallas_call | solution.py:467
  49.8 0.1 collective-permute-done.2.after
  49.9 1.8 %shard_map.30 = f32[128,128]{1,0:T(8,128)S(1)} custom-call(f32[2,2,48,128]{3,2,1,0:T(8,128)S(1)} %slice.8.tail, f32[4,2,48,128]{3,2,1,0:T(8,128)S(1)} %collective-permute-done.2.after, f32[10,48,128]{2,1,0:T(8,128)S(1)} %shard_map.29.inner, f32[16,4]{1,0:T(8,128)S(1)} %bitcast.8), custom_call_target="tpu_custom_call" | custom-call | tf_op jit(solution)/shard_map/pallas_call | solution.py:467
  51.8 24.0 %all_to_all.17 = f32[128,1,128]{2,1,0:T(1,128)S(1)} all-to-all(f32[128,1,128]{2,1,0:T(1,128)S(1)} %bitcast.5), channel_id=1, replica_groups=mesh['depth'=128,'rows'=4] {'depth'}, dimensions={0} | all-to-all | bytes 131072 | tf_op jit(solution)/shard_map/all_to_all | solution.py:545
  75.7 0.2 shard_map.31
  75.9 0.6 copy.8
  (2 shorter events, 0.0 us)
Async XLA Ops:
  0.8 8.4 %collective-permute-start.1 = (f32[2,8,512]{2,1,0:T(8,128)S(1)}, f32[2,8,512]{2,1,0:T(8,128)S(1)}, u32[]{:S(2)}, u32[]{:S(2)}) collective-permute-start(f32[2,8,512]{2,1,0:T(8,128)S(1)} %get-tuple-element.7.two), channel_id=1, source_target_pairs={{1,2},{2,1},{5,6},{6,5},{9,10},{10,9},{13,14},{14,13},{17,18},{18,... | collective-permute-start | bytes 98312 | tf_op jit(solution)/shard_map/ppermute | solution.py:497
  1.5 7.7 %collective-permute-start = (f32[2,8,512]{2,1,0:T(8,128)S(1)}, f32[2,8,512]{2,1,0:T(8,128)S(1)}, u32[]{:S(2)}, u32[]{:S(2)}) collective-permute-start(f32[2,8,512]{2,1,0:T(8,128)S(1)} %get-tuple-element.8), channel_id=1, source_target_pairs={{0,1},{2,3},{1,0},{3,2},{4,5},{6,7},{5,4},{7,6},{8,9},{10,11},{9,8... | collective-permute-start | bytes 98312 | tf_op jit(solution)/shard_map/ppermute | solution.py:495
  40.8 1.3 %copy-start = (f32[4,16]{1,0:T(4,128)S(1)}, f32[4,16]{1,0:T(4,128)}, u32[]{:S(2)}) copy-start(f32[4,16]{1,0:T(4,128)} %param.3) | copy-start | bytes 772
  40.8 9.1 %collective-permute-start.2 = (f32[4,2,48,128]{3,2,1,0:T(8,128)S(1)}, f32[4,2,48,128]{3,2,1,0:T(8,128)S(1)}, u32[]{:S(2)}, u32[]{:S(2)}) collective-permute-start(f32[4,2,48,128]{3,2,1,0:T(8,128)S(1)} %slice.9), channel_id=1, source_target_pairs={{64,0},{68,4},{72,8},{76,12},{80,16},{84,20},{88,24},{92,28},{96,3... | collective-permute-start | bytes 589832 | tf_op jit(solution)/shard_map/ppermute | solution.py:480

commit v9 on v8

--- a/solution.py
+++ b/solution.py
@@ -62,17 +62,21 @@
         yield t, m, value
 
 
-def slice_kernel(density, one, two, sems):
+def slice_kernel(density, one, two, ends, sems):
     even = lax.axis_index("rows") % 2 == 0
-    rows = (jnp.where(even, BAND - 8, 0), jnp.where(even, 0, BAND - 8))
     copies = []
-    for i, (row, to) in enumerate(zip(rows, (one, two))):
-        source = density.at[:, pl.ds(pl.multiple_of(row, 8), 8), :]
-        copies.append(pltpu.make_async_copy(source, to, sems.at[i]))
+    for i, row in enumerate((0, BAND - 8)):
+        source = density.at[:, pl.ds(row, 8), :]
+        copies.append(pltpu.make_async_copy(source, ends.at[i], sems.at[i]))
     for copy in copies:
         copy.start()
     for copy in copies:
         copy.wait()
+    for p in range(PLANES):
+        first = ends[0, p, 0:HALO, :]
+        last = ends[1, p, 8 - HALO : 8, :]
+        one[p] = jnp.where(even, last, first)
+        two[p] = jnp.where(even, first, last)
 
 
 def pack_kernel(density, out, own, ext, sems):
@@ -122,11 +126,11 @@
 
     def above(source):
         for p in range(PLANES):
-            edge[p, 0:HALO, :] = source[p, 8 - HALO : 8, :]
+            edge[p, 0:HALO, :] = source[p]
 
     def below(source):
         for p in range(PLANES):
-            edge[p, HALO : 2 * HALO, :] = source[p, 0:HALO, :]
+            edge[p, HALO : 2 * HALO, :] = source[p]
 
     @pl.when(even)
     def _():
@@ -154,7 +158,7 @@
     def _():
         for p in range(PLANES):
             for i in range(HALO):
-                edge[p, HALO + i : HALO + i + 1, :] = two[p, 7 - i : 8 - i, :]
+                edge[p, HALO + i : HALO + i + 1, :] = two[p, HALO - 1 - i : HALO - i, :]
 
     segment, left, right = window_masks()
     row = lax.broadcasted_iota(jnp.int32, (8, LANES), 0)
@@ -303,11 +307,13 @@
         return [mine[i, p, 8 * j : 8 * j + 8, :] for j in range(TILES)]
 
     def fill(i, carry):
-        for p in range(PLANES):
-            put(fa, FRONT + PLANES * i + p, plane_of(i, p))
+        for u in range(4):
+            for p in range(PLANES):
+                k = 4 * i + u
+                put(fa, FRONT + PLANES * k + p, plane_of(k, p))
         return carry
 
-    lax.fori_loop(0, GROUP, fill, 0)
+    lax.fori_loop(0, GROUP // 4, fill, 0)
 
     @pl.when(is_first)
     def _():
@@ -482,13 +488,16 @@
 
 def rendered(density, transfer_table):
     bands = lax.axis_size("rows")
-    edge = VMEM((PLANES, 8, COLS), jnp.float32)
+    edge = VMEM((PLANES, HALO, COLS), jnp.float32)
     one, two = pl.pallas_call(
         slice_kernel,
         out_shape=[edge, edge],
         in_specs=[pl.BlockSpec(memory_space=pl.ANY)],
         out_specs=[pl.BlockSpec(memory_space=VMEM)] * 2,
-        scratch_shapes=[pltpu.SemaphoreType.DMA((2,))],
+        scratch_shapes=[
+            VMEM((2, PLANES, 8, COLS), jnp.float32),
+            pltpu.SemaphoreType.DMA((2,)),
+        ],
         name="slice_kernel",
     )(density)
     pairs = [(i, i + 1) for i in range(0, bands, 2)]
@@ -543,7 +552,14 @@
         knots,
     )
     parts = lax.all_to_all(partial, "depth", 0, 0, tiled=True)
-    return call(gather_kernel, (4, 1, COLS), [], parts)
+    spec = pl.BlockSpec(memory_space=VMEM)
+    return pl.pallas_call(
+        gather_kernel,
+        out_shape=jax.ShapeDtypeStruct((4, 1, COLS), jnp.float32),
+        in_specs=[spec],
+        out_specs=spec,
+        name="gather_kernel",
+    )(pltpu.with_memory_space_constraint(parts, VMEM))
 
 
 def solution(mesh):

time: 76.9 us -> 76.6 us (level)
  waiting for transfers between devices: 0.14 us -> 0.93 us
    pallas_call x4 -> x3, Pallas kernels: 9.7 us -> 8.71 us  [call(): pl.pallas_call(kernel, out_shape=VMEM(shape, jnp.float32), in_specs=[spec...]
    pallas_call x0 -> x1, Pallas kernels: none -> 0.8 us  [rendered(): pl.pallas_call(gather_kernel, out_shape=jax.ShapeDtypeStruct((4, 1, COLS)...]
    ppermute x1, waiting for transfers between devices: 0.13 us -> 0.92 us  [shifted(): return lax.ppermute(value, axis, pairs)]
  transfers between devices with their start and end apart: 3 -> 3, of which waited for: 1 -> 1; matrix products, arithmetic and copies ran while one was open for 0% -> 0% of each run, Pallas kernels for 11% -> 10%
where the time goes in v9:
time: 76.6 us; the launch traced here: 76.2 us
  blocking collectives  55.2 us (72%)
  Pallas kernels  11.6 us (15%)
  starting transfers between devices  8.35 us (11%)
  waiting for transfers between devices  0.93 us (1%)
    all_to_all x1, blocking collectives, rendered(): lax.all_to_all(sent, 'depth', 0, 0, axis_index_groups=groups, tiled=True)  31.3 us
    all_to_all x1, blocking collectives, rendered(): parts = lax.all_to_all(partial, 'depth', 0, 0, tiled=True)  23.8 us
    pallas_call x3, Pallas kernels, call(): pl.pallas_call(kernel, out_shape=VMEM(shape, jnp.float32), in_specs=[spec...  8.71 us
    ppermute x1, starting transfers between devices, rendered(): from_one = lax.ppermute(one, 'rows', pairs + [(b, a) for a, b in pairs])  6.39 us
  transfers between devices with their start and end apart: 3, of which 1 were waited for; matrix products, arithmetic and copies ran while one was open for 0% of the time, Pallas kernels for 10%

profile of v9, /device:TPU:1, one launch (start us, length us, event | category | flops | bytes accessed | tf_op | source)
XLA Modules:
  0.0 76.2 jit_solution(10476098277119210482)
XLA Ops:
  0.0 0.8 %slice_kernel.1 = (f32[2,4,512]{2,1,0:T(4,128)S(1)}, f32[2,4,512]{2,1,0:T(4,128)S(1)}) custom-call(f32[2,128,512]{2,1,0:T(8,128)} %density.3), custom_call_target="tpu_custom_call" | custom-call | tf_op jit(solution)/shard_map/slice_kernel/pallas_call | solution.py:492
  0.8 0.7 collective-permute-start.1
  1.5 6.4 %collective-permute-start = (f32[2,4,512]{2,1,0:T(4,128)S(1)}, f32[2,4,512]{2,1,0:T(4,128)S(1)}, u32[]{:S(2)}, u32[]{:S(2)}) collective-permute-start(f32[2,4,512]{2,1,0:T(4,128)S(1)} %get-tuple-element.8), channel_id=1, source_target_pairs={{0,1},{2,3},{1,0},{3,2},{4,5},{6,7},{5,4},{7,6},{8,9},{10,11},{9,8... | collective-permute-start | bytes 49160 | tf_op jit(solution)/shard_map/ppermute | solution.py:504
  7.9 1.3 %pack_kernel.1.sent = f32[16,2,48,128]{3,2,1,0:T(8,128)S(1)} custom-call(f32[2,128,512]{2,1,0:T(8,128)} %density.3), custom_call_target="tpu_custom_call" | custom-call | tf_op jit(solution)/shard_map/pack_kernel/pallas_call | solution.py:508
  9.2 0.0 collective-permute-done.1.from_two
  9.2 0.0 collective-permute-done.from_one
  9.2 0.1 shard_map.28
  9.3 31.3 %all_to_all.16.mine = f32[16,2,48,128]{3,2,1,0:T(8,128)S(1)} all-to-all(f32[16,2,48,128]{3,2,1,0:T(8,128)S(1)} %shard_map.28), channel_id=1, replica_groups={{0,4,8,12,16,20,24,28,32,36,40,44,48,52,56,60},{64,68,72,76,80,84,88,92..., dimensions={0} | all-to-all | bytes 1572864 | tf_op jit(solution)/shard_map/all_to_all | solution.py:531
  40.7 0.0 copy-start
  40.7 1.3 %collective-permute-start.2 = (f32[4,2,48,128]{3,2,1,0:T(8,128)S(1)}, f32[4,2,48,128]{3,2,1,0:T(8,128)S(1)}, u32[]{:S(2)}, u32[]{:S(2)}) collective-permute-start(f32[4,2,48,128]{3,2,1,0:T(8,128)S(1)} %slice.9), channel_id=1, source_target_pairs={{64,0},{68,4},{72,8},{76,12},{80,16},{84,20},{88,24},{92,28},{96,3... | collective-permute-start | bytes 589832 | tf_op jit(solution)/shard_map/ppermute | solution.py:486
  42.0 0.0 copy-done
  42.0 0.1 copy.5
  42.1 6.7 %shard_map.29.inner = f32[10,48,128]{2,1,0:T(8,128)S(1)} custom-call(f32[16,2,48,128]{3,2,1,0:T(8,128)S(1)} %all_to_all.16.mine, f32[16,4]{1,0:T(8,128)S(1)} %bitcast.7), custom_call_target="tpu_custom_call" | custom-call | tf_op jit(solution)/shard_map/pallas_call | solution.py:473
  48.8 0.9 %collective-permute-done.2.after = f32[4,2,48,128]{3,2,1,0:T(8,128)S(1)} collective-permute-done((f32[4,2,48,128]{3,2,1,0:T(8,128)S(1)}, f32[4,2,48,128]{3,2,1,0:T(8,128)S(1)}, u32[]{:S(2)}, u32[]{:S(2)}) %collective-permute-start.2) | collective-permute-done | bytes 196640 | tf_op jit(solution)/shard_map/ppermute | solution.py:486
  49.7 1.8 %shard_map.30 = f32[128,128]{1,0:T(8,128)S(1)} custom-call(f32[2,2,48,128]{3,2,1,0:T(8,128)S(1)} %slice.8.tail, f32[4,2,48,128]{3,2,1,0:T(8,128)S(1)} %collective-permute-done.2.after, f32[10,48,128]{2,1,0:T(8,128)S(1)} %shard_map.29.inner, f32[16,4]{1,0:T(8,128)S(1)} %bitcast.8), custom_call_target="tpu_custom_call" | custom-call | tf_op jit(solution)/shard_map/pallas_call | solution.py:473
  51.6 23.8 %all_to_all.17 = f32[128,1,128]{2,1,0:T(1,128)S(1)} all-to-all(f32[128,1,128]{2,1,0:T(1,128)S(1)} %bitcast.5), channel_id=1, replica_groups=mesh['depth'=128,'rows'=4] {'depth'}, dimensions={0} | all-to-all | bytes 131072 | tf_op jit(solution)/shard_map/all_to_all | solution.py:554
  75.4 0.8 %gather_kernel.1 = f32[4,1,512]{2,1,0:T(1,128)} custom-call(f32[128,128]{1,0:T(8,128)S(1)} %bitcast.6), custom_call_target="tpu_custom_call" | custom-call | tf_op jit(solution)/shard_map/gather_kernel/pallas_call | solution.py:556
  (2 shorter events, 0.0 us)
Async XLA Ops:
  0.8 8.4 %collective-permute-start.1 = (f32[2,4,512]{2,1,0:T(4,128)S(1)}, f32[2,4,512]{2,1,0:T(4,128)S(1)}, u32[]{:S(2)}, u32[]{:S(2)}) collective-permute-start(f32[2,4,512]{2,1,0:T(4,128)S(1)} %get-tuple-element.7.two), channel_id=1, source_target_pairs={{1,2},{2,1},{5,6},{6,5},{9,10},{10,9},{13,14},{14,13},{17,18},{18,... | collective-permute-start | bytes 49160 | tf_op jit(solution)/shard_map/ppermute | solution.py:506
  1.5 7.7 %collective-permute-start = (f32[2,4,512]{2,1,0:T(4,128)S(1)}, f32[2,4,512]{2,1,0:T(4,128)S(1)}, u32[]{:S(2)}, u32[]{:S(2)}) collective-permute-start(f32[2,4,512]{2,1,0:T(4,128)S(1)} %get-tuple-element.8), channel_id=1, source_target_pairs={{0,1},{2,3},{1,0},{3,2},{4,5},{6,7},{5,4},{7,6},{8,9},{10,11},{9,8... | collective-permute-start | bytes 49160 | tf_op jit(solution)/shard_map/ppermute | solution.py:504
  40.7 1.3 %copy-start = (f32[4,16]{1,0:T(4,128)S(1)}, f32[4,16]{1,0:T(4,128)}, u32[]{:S(2)}) copy-start(f32[4,16]{1,0:T(4,128)} %param.3) | copy-start | bytes 772
  40.7 9.1 %collective-permute-start.2 = (f32[4,2,48,128]{3,2,1,0:T(8,128)S(1)}, f32[4,2,48,128]{3,2,1,0:T(8,128)S(1)}, u32[]{:S(2)}, u32[]{:S(2)}) collective-permute-start(f32[4,2,48,128]{3,2,1,0:T(8,128)S(1)} %slice.9), channel_id=1, source_target_pairs={{64,0},{68,4},{72,8},{76,12},{80,16},{84,20},{88,24},{92,28},{96,3... | collective-permute-start | bytes 589832 | tf_op jit(solution)/shard_map/ppermute | solution.py:486

commit v10 on v9

--- a/solution.py
+++ b/solution.py
@@ -21,14 +21,19 @@
 TILE = COLS // GROUP
 WIDE = TILE + 2 * HALO
 SEGS = 3
-SEG_ROWS = 48
-TILES = SEG_ROWS // 8
+SEG_ROWS = 46
+RAW_ROWS = 43
+TILES = 6
+LINES = 8 * TILES
 PLANES = 2
 DEEP = GROUP * PLANES
 LANES = 128
 TOP = 8
-TALL = SEG_ROWS + 2 * TOP
+TALL = 64
 FRONT = HALO
+CHUNK = 2 * RAW_ROWS
+SPARE = SEGS * WIDE
+TAIL = 2 * PASSES + 4
 PARTS = 4
 UNROLL = 7
 SHADED = 8
@@ -41,14 +46,15 @@
 
 def window_masks():
     lane = lane_index()
-    segment, left, right = [], [], []
+    segment, left, right, spare = [], [], [], []
     for m in range(4):
         local = (lane - (TILE * m - HALO)) % LANES
         segment.append([(local >= WIDE * k) & (local < WIDE * (k + 1)) for k in range(SEGS)])
         column = local % WIDE
         left.append(column < HALO)
         right.append(column >= WIDE - HALO)
-    return segment, left, right
+        spare.append(local >= SPARE)
+    return segment, left, right, spare
 
 
 def windows(tiles, joined, left, right):
@@ -79,8 +85,7 @@
         two[p] = jnp.where(even, first, last)
 
 
-def pack_kernel(density, out, own, ext, sems):
-    rows = SEGS * SEG_ROWS
+def pack_kernel(density, out, own, sems):
     part = BAND // PARTS
     copies = []
     for p in range(PLANES):
@@ -92,31 +97,27 @@
     for copy in copies:
         copy.start()
     for p in range(PLANES):
-        ext[p, :8, :] = jnp.zeros((8, COLS), jnp.float32)
-        ext[p, rows - 16 :, :] = jnp.zeros((16, COLS), jnp.float32)
-    segment, left, right = window_masks()
+        own[p, BAND:, :] = jnp.zeros((8, COLS), jnp.float32)
+    segment, left, right, _ = window_masks()
 
     def joined(rolled, q, m):
         rest = jnp.where(segment[m][1], rolled[1][q], rolled[2][q])
         return jnp.where(segment[m][0], rolled[0][q], rest)
 
-    def step(j, p):
-        row = pl.multiple_of(8 * j, 8)
-        rolled = []
-        for k in range(SEGS):
-            start = pl.multiple_of(row + SEG_ROWS * k, 8)
-            tiles = [ext[p, pl.ds(start, 8), LANES * q : LANES * (q + 1)] for q in range(4)]
-            rolled.append([pltpu.roll(x, WIDE * k, 1) if k else x for x in tiles])
-        for t, m, value in windows(rolled, joined, left, right):
-            out[t, p, pl.ds(row, 8), :] = value
-        return p
-
     for p in range(PLANES):
         for copy in copies[PARTS * p : PARTS * (p + 1)]:
             copy.wait()
-        ext[p, HALO : HALO + BAND, :] = own[p]
         for j in range(TILES):
-            step(j, p)
+            count = min(8, RAW_ROWS - 8 * j)
+            rolled = []
+            for k in range(SEGS):
+                start = RAW_ROWS * k + 8 * j
+                rows = own[p, start : start + 8, :]
+                tiles = [rows[:, LANES * q : LANES * (q + 1)] for q in range(4)]
+                rolled.append([pltpu.roll(x, WIDE * k, 1) if k else x for x in tiles])
+            for t, m, value in windows(rolled, joined, left, right):
+                start = CHUNK * t + RAW_ROWS * p + 8 * j
+                out[start : start + count, :] = value[:count]
 
 
 def halo_kernel(sent, two, from_one, from_two, out, edge):
@@ -160,20 +161,19 @@
             for i in range(HALO):
                 edge[p, HALO + i : HALO + i + 1, :] = two[p, HALO - 1 - i : HALO - i, :]
 
-    segment, left, right = window_masks()
-    row = lax.broadcasted_iota(jnp.int32, (8, LANES), 0)
-    places = ((0, 0, row < HALO), (2, SEG_ROWS - 16, row >= HALO))
-
-    def joined(rolled, q, m):
-        return rolled[q]
+    _, left, right, spare = window_masks()
+
+    def joined(tiles, q, m):
+        return tiles[q]
 
     for p in range(PLANES):
         tiles = [edge[p, :, LANES * q : LANES * (q + 1)] for q in range(4)]
-        for k, at, rows in places:
-            rolled = [pltpu.roll(x, WIDE * k, 1) for x in tiles] if k else tiles
-            for t, m, value in windows(rolled, joined, left, right):
-                here = sent[t, p, at : at + 8, :]
-                out[t, p, at : at + 8, :] = jnp.where(rows & segment[m][k], value, here)
+        for t, m, value in windows(tiles, joined, left, right):
+            for g in range(WIDE // 8):
+                start = CHUNK * t + RAW_ROWS * p + 8 * g
+                moved = pltpu.roll(value, SPARE - 8 * g, 1)
+                here = sent[start : start + 8, :]
+                out[start : start + 8, :] = jnp.where(spare[m], moved, here)
 
 
 def flux(change):
@@ -189,7 +189,8 @@
 def put(ref, p, tiles):
     for j in range(TILES):
         ref[p, rows_at(j), :] = tiles[j]
-    ref[p, TOP - 1 : TOP, :] = pltpu.roll(tiles[-1], WIDE, 1)[7:8]
+    last = SEG_ROWS - 8 * (TILES - 1) - 1
+    ref[p, TOP - 1 : TOP, :] = pltpu.roll(tiles[-1], WIDE, 1)[last : last + 1]
     ref[p, TOP + SEG_ROWS : TOP + SEG_ROWS + 1, :] = pltpu.roll(tiles[0], LANES - WIDE, 1)[0:1]
 
 
@@ -210,6 +211,40 @@
         self.open_face = jnp.where(
             jnp.logical_or(self.at_last, jnp.logical_and(column == HALO - 1, first)), 0.0, 1.0
         )
+        row = lax.broadcasted_iota(jnp.int32, (8, LANES), 0)
+        self.local = local
+        self.segment = [(local >= WIDE * k) & (local < WIDE * (k + 1)) for k in range(SEGS)]
+        self.top = self.segment[0] & (row < HALO)
+        self.bottom = self.segment[2] & (row < HALO)
+        self.head = self.segment[1] & (row == 0)
+        self.foot = self.segment[1] & (row >= 4) & (row < 6)
+
+    def unpack(self, raw, start):
+        def load(by):
+            return raw[pl.ds(start + by, 8), :]
+
+        zeroth, end = load(0), load(RAW_ROWS - 8)
+        tiles = []
+        for j in range(TILES):
+            if j == 0:
+                parts = (pltpu.roll(zeroth, 4, 0), pltpu.roll(zeroth, 1, 0), load(2))
+            elif j < TILES - 1:
+                parts = (load(8 * j - 4), load(8 * j - 1), load(8 * j + 2))
+            else:
+                parts = (pltpu.roll(end, 7, 0), pltpu.roll(end, 4, 0), end)
+            rest = jnp.where(self.segment[1], parts[1], parts[2])
+            tiles.append(jnp.where(self.segment[0], parts[0], rest))
+        halo = None
+        for g in range(WIDE // 8):
+            rows = load(8 * g) if g else zeroth
+            moved = pltpu.roll(rows, LANES - SPARE + 8 * g, 1)
+            halo = moved if halo is None else jnp.where(self.local >= 8 * g, moved, halo)
+        head = pltpu.roll(pltpu.roll(end, WIDE, 1), 1, 0)
+        foot = pltpu.roll(pltpu.roll(zeroth, LANES - WIDE, 1), 4, 0)
+        below = pltpu.roll(pltpu.roll(halo, 2 * WIDE, 1), 4, 0)
+        tiles[0] = jnp.where(self.top, halo, jnp.where(self.head, head, tiles[0]))
+        tiles[-1] = jnp.where(self.bottom, below, jnp.where(self.foot, foot, tiles[-1]))
+        return tiles
 
 
 def diffuse(src, p, dst, to, fluxes, slot, flux_nearer, tile):
@@ -220,7 +255,8 @@
     row = [flux(below[j] - f[j]) for j in range(TILES)]
     for j in range(TILES):
         fluxes[slot, rows_at(j), :] = row[j]
-    fluxes[slot, TOP - 1 : TOP, :] = pltpu.roll(row[-1], WIDE, 1)[7:8]
+    last = SEG_ROWS - 8 * (TILES - 1) - 1
+    fluxes[slot, TOP - 1 : TOP, :] = pltpu.roll(row[-1], WIDE, 1)[last : last + 1]
     row_prev = take(fluxes, slot, -1)
     new = []
     for j in range(TILES):
@@ -303,22 +339,23 @@
     zero = jnp.zeros((8, LANES), jnp.float32)
     is_first = tile.block == 0
 
-    def plane_of(i, p):
-        return [mine[i, p, 8 * j : 8 * j + 8, :] for j in range(TILES)]
-
     def fill(i, carry):
         for u in range(4):
             for p in range(PLANES):
                 k = 4 * i + u
-                put(fa, FRONT + PLANES * k + p, plane_of(k, p))
+                put(fa, FRONT + PLANES * k + p, tile.unpack(mine, CHUNK * k + RAW_ROWS * p))
         return carry
 
     lax.fori_loop(0, GROUP // 4, fill, 0)
+    for i in range(HALO):
+        for j in range(TILES):
+            plane = fa[FRONT + DEEP - HALO + i, rows_at(j), :]
+            out[TAIL + i, 8 * j : 8 * j + 8, :] = plane
 
     @pl.when(is_first)
     def _():
         for i in range(HALO):
-            put(fa, FRONT - 1 - i, plane_of(i // 2, i % 2))
+            fa[FRONT - 1 - i] = fa[FRONT + i]
 
     src, dst = fa, fb
     for sweep in range(PASSES):
@@ -390,27 +427,27 @@
     lax.fori_loop(0, TILES, shaded, 0)
 
 
-def outer_kernel(tail, after, inner, knots, out, fa, fb, fluxes):
+def outer_kernel(after, inner, knots, out, fa, fb, fluxes):
     tile = Tile()
     lookup = tables(knots)
     is_last = tile.block == BLOCKS - 1
 
-    def fill(to, source, i):
-        put(fa, to, [source[i // 2, i % 2, 8 * j : 8 * j + 8, :] for j in range(TILES)])
-
-    near = HALO // PLANES
+    def tail(to, i):
+        put(fa, to, [inner[TAIL + i, 8 * j : 8 * j + 8, :] for j in range(TILES)])
+
     for i in range(2):
-        fill(i, tail, 2 * near - 2 + i)
+        tail(i, HALO - 2 + i)
 
     @pl.when(jnp.logical_not(is_last))
     def _():
         for i in range(2 * HALO):
-            fill(2 + i, after, i)
+            k, p = divmod(i, PLANES)
+            put(fa, 2 + i, tile.unpack(after, CHUNK * k + RAW_ROWS * p))
 
     @pl.when(is_last)
     def _():
         for i in range(2 * HALO):
-            fill(2 + i, tail, max(HALO - 1 - i, 0))
+            tail(2 + i, max(HALO - 1 - i, 0))
 
     src, dst = fa, fb
     for sweep in range(PASSES):
@@ -437,7 +474,7 @@
                 moved = pltpu.roll(sums[c], lax.rem(by, LANES), 1)
                 value = moved if value is None else jnp.where(lane >= TILE * c, moved, value)
             first = SEG_ROWS * k + 8 * j - HALO
-            lo, hi = max(first, 0), min(first + 8, BAND)
+            lo, hi = max(first, 0), min(first + min(8, SEG_ROWS - 8 * j), BAND)
             if lo < hi:
                 out[lo:hi, :] = value[lo - first : hi - first]
 
@@ -504,15 +541,14 @@
     from_one = lax.ppermute(one, "rows", pairs + [(b, a) for a, b in pairs])
     pairs = [(i, i + 1) for i in range(1, bands - 1, 2)]
     from_two = lax.ppermute(two, "rows", pairs + [(b, a) for a, b in pairs])
-    chunks = (GROUP, PLANES, SEG_ROWS, LANES)
+    chunks = (GROUP * CHUNK, LANES)
     cut = pl.pallas_call(
         pack_kernel,
         out_shape=VMEM(chunks, jnp.float32),
         in_specs=[pl.BlockSpec(memory_space=pl.ANY)],
         out_specs=pl.BlockSpec(memory_space=VMEM),
         scratch_shapes=[
-            VMEM((PLANES, BAND, COLS), jnp.float32),
-            VMEM((PLANES, SEGS * SEG_ROWS, COLS), jnp.float32),
+            VMEM((PLANES, BAND + 8, COLS), jnp.float32),
             pltpu.SemaphoreType.DMA((PLANES, PARTS)),
         ],
         name="pack_kernel",
@@ -528,16 +564,16 @@
         input_output_aliases={0: 0},
     )
     groups = [[GROUP * b + i for i in range(GROUP)] for b in range(BLOCKS)]
+    sent = sent.reshape(GROUP, CHUNK, 1, LANES)
     mine = lax.all_to_all(sent, "depth", 0, 0, axis_index_groups=groups, tiled=True)
-    near = HALO // PLANES
-    tail = mine[GROUP - near :]
-    after = shifted(mine[: 2 * near], "depth", -GROUP)
+    mine = mine.reshape(GROUP * CHUNK, LANES)
+    after = shifted(mine[: 2 * HALO // PLANES * CHUNK], "depth", -GROUP)
     knots = transfer_table.T
     field = (FRONT + DEEP, TALL, LANES)
     inner = call(
         inner_kernel,
-        (2 * PASSES + 4, SEG_ROWS, LANES),
-        [field, field, (UNROLL, TALL, LANES), (4, SEG_ROWS, LANES)],
+        (TAIL + HALO, LINES, LANES),
+        [field, field, (UNROLL, TALL, LANES), (4, LINES, LANES)],
         mine,
         knots,
     )
@@ -546,7 +582,6 @@
         outer_kernel,
         (BAND, LANES),
         [few, few, (2 * HALO, TALL, LANES)],
-        tail,
         after,
         inner,
         knots,

time: 76.6 us -> 75 us (0.979)
  blocking collectives: 55.2 us -> 53.6 us
  waiting for transfers between devices: 0.93 us -> 0.01 us
  Pallas kernels: 11.6 us -> 12.4 us
    all_to_all x1, blocking collectives: 31.3 us -> 29.7 us  [rendered(): lax.all_to_all(sent, 'depth', 0, 0, axis_index_groups=groups, tiled=True)]
    ppermute x1, waiting for transfers between devices: 0.92 us -> 0.01 us  [shifted(): return lax.ppermute(value, axis, pairs)]
    pallas_call x3, Pallas kernels: 8.71 us -> 9.59 us  [call(): pl.pallas_call(kernel, out_shape=VMEM(shape, jnp.float32), in_specs=[spec...]
  transfers between devices with their start and end apart: 3 -> 3, of which waited for: 1 -> 0; matrix products, arithmetic and copies ran while one was open for 0% -> 0% of each run, Pallas kernels for 10% -> 12%
where the time goes in v10:
time: 75 us; the launch traced here: 74.6 us
  blocking collectives  53.6 us (71%)
  Pallas kernels  12.4 us (17%)
  starting transfers between devices  8.35 us (11%)
    all_to_all x1, blocking collectives, rendered(): lax.all_to_all(sent, 'depth', 0, 0, axis_index_groups=groups, tiled=True)  29.7 us
    all_to_all x1, blocking collectives, rendered(): parts = lax.all_to_all(partial, 'depth', 0, 0, tiled=True)  23.9 us
    pallas_call x3, Pallas kernels, call(): pl.pallas_call(kernel, out_shape=VMEM(shape, jnp.float32), in_specs=[spec...  9.59 us
    ppermute x1, starting transfers between devices, rendered(): from_one = lax.ppermute(one, 'rows', pairs + [(b, a) for a, b in pairs])  6.39 us
  transfers between devices with their start and end apart: 3, of which 0 were waited for; matrix products, arithmetic and copies ran while one was open for 0% of the time, Pallas kernels for 12%

profile of v10, /device:TPU:1, one launch (start us, length us, event | category | flops | bytes accessed | tf_op | source)
XLA Modules:
  0.0 74.6 jit_solution(14212342891048920274)
XLA Ops:
  0.0 0.8 %slice_kernel.1 = (f32[2,4,512]{2,1,0:T(4,128)S(1)}, f32[2,4,512]{2,1,0:T(4,128)S(1)}) custom-call(f32[2,128,512]{2,1,0:T(8,128)} %density.3), custom_call_target="tpu_custom_call" | custom-call | tf_op jit(solution)/shard_map/slice_kernel/pallas_call | solution.py:529
  0.8 0.7 collective-permute-start.1
  1.5 6.4 %collective-permute-start = (f32[2,4,512]{2,1,0:T(4,128)S(1)}, f32[2,4,512]{2,1,0:T(4,128)S(1)}, u32[]{:S(2)}, u32[]{:S(2)}) collective-permute-start(f32[2,4,512]{2,1,0:T(4,128)S(1)} %get-tuple-element.8), channel_id=1, source_target_pairs={{0,1},{2,3},{1,0},{3,2},{4,5},{6,7},{5,4},{7,6},{8,9},{10,11},{9,8... | collective-permute-start | bytes 49160 | tf_op jit(solution)/shard_map/ppermute | solution.py:541
  7.9 1.3 %pack_kernel.1.sent = f32[1376,128]{1,0:T(8,128)S(1)} custom-call(f32[2,128,512]{2,1,0:T(8,128)} %density.3), custom_call_target="tpu_custom_call" | custom-call | tf_op jit(solution)/shard_map/pack_kernel/pallas_call | solution.py:545
  9.1 0.0 collective-permute-done.1.from_two
  9.2 0.0 collective-permute-done.from_one
  9.2 0.3 shard_map.28
  9.4 29.7 %all_to_all.16 = f32[16,86,1,128]{3,2,1,0:T(1,128)S(1)} all-to-all(f32[16,86,1,128]{3,2,1,0:T(1,128)S(1)} %bitcast.8), channel_id=1, replica_groups={{0,4,8,12,16,20,24,28,32,36,40,44,48,52,56,60},{64,68,72,76,80,84,88,92..., dimensions={0} | all-to-all | bytes 1409024 | tf_op jit(solution)/shard_map/all_to_all | solution.py:568
  39.1 0.0 copy-start
  39.1 1.3 %collective-permute-start.2 = (f32[344,128]{1,0:T(8,128)S(1)}, f32[344,128]{1,0:T(8,128)S(1)}, u32[]{:S(2)}, u32[]{:S(2)}) collective-permute-start(f32[344,128]{1,0:T(8,128)S(1)} %bitcast.14), channel_id=1, source_target_pairs={{64,0},{68,4},{72,8},{76,12},{80,16},{84,20},{88,24},{92,28},{96,3... | collective-permute-start | bytes 528392 | tf_op jit(solution)/shard_map/ppermute | solution.py:523
  40.4 0.0 copy-done
  40.4 0.1 copy.7
  40.5 7.4 %shard_map.29.inner = f32[14,48,128]{2,1,0:T(8,128)S(1)} custom-call(f32[1376,128]{1,0:T(8,128)S(1)} %bitcast.9, f32[16,4]{1,0:T(8,128)S(1)} %bitcast.12), custom_call_target="tpu_custom_call" | custom-call | tf_op jit(solution)/shard_map/pallas_call | solution.py:510
  47.9 0.0 collective-permute-done.2.after
  47.9 2.0 %shard_map.30 = f32[128,128]{1,0:T(8,128)S(1)} custom-call(f32[344,128]{1,0:T(8,128)S(1)} %collective-permute-done.2.after, f32[14,48,128]{2,1,0:T(8,128)S(1)} %shard_map.29.inner, f32[16,4]{1,0:T(8,128)S(1)} %bitcast.13), custom_call_target="tpu_custom_call" | custom-call | tf_op jit(solution)/shard_map/pallas_call | solution.py:510
  49.9 23.9 %all_to_all.17 = f32[128,1,128]{2,1,0:T(1,128)S(1)} all-to-all(f32[128,1,128]{2,1,0:T(1,128)S(1)} %bitcast.10), channel_id=1, replica_groups=mesh['depth'=128,'rows'=4] {'depth'}, dimensions={0} | all-to-all | bytes 131072 | tf_op jit(solution)/shard_map/all_to_all | solution.py:589
  73.8 0.8 %gather_kernel.1 = f32[4,1,512]{2,1,0:T(1,128)} custom-call(f32[128,128]{1,0:T(8,128)S(1)} %bitcast.11), custom_call_target="tpu_custom_call" | custom-call | tf_op jit(solution)/shard_map/gather_kernel/pallas_call | solution.py:591
  (1 shorter events, 0.0 us)
Async XLA Ops:
  0.8 8.3 %collective-permute-start.1 = (f32[2,4,512]{2,1,0:T(4,128)S(1)}, f32[2,4,512]{2,1,0:T(4,128)S(1)}, u32[]{:S(2)}, u32[]{:S(2)}) collective-permute-start(f32[2,4,512]{2,1,0:T(4,128)S(1)} %get-tuple-element.7.two), channel_id=1, source_target_pairs={{1,2},{2,1},{5,6},{6,5},{9,10},{10,9},{13,14},{14,13},{17,18},{18,... | collective-permute-start | bytes 49160 | tf_op jit(solution)/shard_map/ppermute | solution.py:543
  1.5 7.7 %collective-permute-start = (f32[2,4,512]{2,1,0:T(4,128)S(1)}, f32[2,4,512]{2,1,0:T(4,128)S(1)}, u32[]{:S(2)}, u32[]{:S(2)}) collective-permute-start(f32[2,4,512]{2,1,0:T(4,128)S(1)} %get-tuple-element.8), channel_id=1, source_target_pairs={{0,1},{2,3},{1,0},{3,2},{4,5},{6,7},{5,4},{7,6},{8,9},{10,11},{9,8... | collective-permute-start | bytes 49160 | tf_op jit(solution)/shard_map/ppermute | solution.py:541
  39.1 1.3 %copy-start = (f32[4,16]{1,0:T(4,128)S(1)}, f32[4,16]{1,0:T(4,128)}, u32[]{:S(2)}) copy-start(f32[4,16]{1,0:T(4,128)} %param.3) | copy-start | bytes 772
  39.1 8.8 %collective-permute-start.2 = (f32[344,128]{1,0:T(8,128)S(1)}, f32[344,128]{1,0:T(8,128)S(1)}, u32[]{:S(2)}, u32[]{:S(2)}) collective-permute-start(f32[344,128]{1,0:T(8,128)S(1)} %bitcast.14), channel_id=1, source_target_pairs={{64,0},{68,4},{72,8},{76,12},{80,16},{84,20},{88,24},{92,28},{96,3... | collective-permute-start | bytes 528392 | tf_op jit(solution)/shard_map/ppermute | solution.py:523

commit v11 on v10

--- a/solution.py
+++ b/solution.py
@@ -12,6 +12,7 @@
 OPTICAL_DEPTH = 3.0
 UPPER_DENSITY = 6.0
 AMBIENT = 0.35
+SCALE = TIME_STEP**-0.5
 
 GROUP = 16
 BLOCKS = 8
@@ -117,7 +118,7 @@
                 rolled.append([pltpu.roll(x, WIDE * k, 1) if k else x for x in tiles])
             for t, m, value in windows(rolled, joined, left, right):
                 start = CHUNK * t + RAW_ROWS * p + 8 * j
-                out[start : start + count, :] = value[:count]
+                out[start : start + count, :] = (value * SCALE)[:count]
 
 
 def halo_kernel(sent, two, from_one, from_two, out, edge):
@@ -173,11 +174,11 @@
                 start = CHUNK * t + RAW_ROWS * p + 8 * g
                 moved = pltpu.roll(value, SPARE - 8 * g, 1)
                 here = sent[start : start + 8, :]
-                out[start : start + 8, :] = jnp.where(spare[m], moved, here)
+                out[start : start + 8, :] = jnp.where(spare[m], moved * SCALE, here)
 
 
 def flux(change):
-    return change / (1.0 + change * change)
+    return change / (SCALE * SCALE + change * change)
 
 
 def rows_at(j, by=0):
@@ -264,7 +265,7 @@
         total = flux_deeper[j] - flux_nearer[j]
         total = total + (row[j] - row_prev[j])
         total = total + (col - pltpu.roll(col, 1, 1))
-        new.append(f[j] + TIME_STEP * total)
+        new.append(f[j] + total)
     put(dst, to, new)
     return flux_deeper
 
@@ -289,41 +290,38 @@
     )
 
 
-def pick(parts, k, high):
-    return jnp.where(high, along_rows(parts[1], k), along_rows(parts[0], k))
-
-
 def tables(transfer):
-    base, slope = [], []
+    even, odd = [], []
     for c in range(4):
-        knots = jnp.broadcast_to(transfer[:, c : c + 1], (KNOTS, LANES))
-        row = lax.broadcasted_iota(jnp.int32, (KNOTS, LANES), 0)
-        after = jnp.where(row == KNOTS - 1, 0.0, pltpu.roll(knots, KNOTS - 1, 0))
-        step = after - knots
-        base.append((knots[:8], knots[8:]))
-        slope.append((step[:8], step[8:]))
-    return base, slope
+        for half, first in ((even, 0), (odd, 1)):
+            knots = transfer[pl.ds(first, 8, stride=2), :]
+            half.append(jnp.broadcast_to(knots[:, c : c + 1], (8, LANES)))
+    return even, odd
 
 
 def shade(src, p, j, carry, lookup, tile):
     red, green, blue, remaining = carry
-    base, slope = lookup
+    even, odd = lookup
     f = src[p, rows_at(j), :]
     depth = src[p + 1, rows_at(j), :] - src[p - 1, rows_at(j), :]
     row = src[p, rows_at(j, 1), :] - src[p, rows_at(j, -1), :]
     right = jnp.where(tile.at_last, f, pltpu.roll(f, LANES - 1, 1))
     left = jnp.where(tile.at_first, f, pltpu.roll(f, 1, 1))
     col = right - left
-    square = depth * depth + row * row + col * col + 1.0
+    square = depth * depth + row * row + col * col + SCALE * SCALE
     gain = 1.0 - AMBIENT
     along = jnp.abs(0.64 * gain * depth + 0.6 * gain * row + 0.48 * gain * col)
     shading = AMBIENT + along * lax.rsqrt(square)
-    position = f * ((KNOTS - 1) / UPPER_DENSITY)
+    position = f * ((KNOTS - 1) / UPPER_DENSITY / SCALE)
     k = position.astype(jnp.int32)
     frac = position - k.astype(jnp.float32)
-    high = k >= 8
-    k = jnp.bitwise_and(k, 7)
-    mixed = [pick(base[c], k, high) + frac * pick(slope[c], k, high) for c in range(4)]
+    near_odd = lax.shift_right_logical(k, 1)
+    near_even = jnp.bitwise_and(lax.shift_right_logical(k + 1, 1), 7)
+    weight_odd = jnp.where(jnp.bitwise_and(k, 1) == 0, frac, 1.0 - frac)
+    mixed = []
+    for c in range(4):
+        low = along_rows(even[c], near_even)
+        mixed.append(low + weight_odd * (along_rows(odd[c], near_odd) - low))
     kept = jnp.exp(mixed[3] * (-OPTICAL_DEPTH / (DEEP * BLOCKS)))
     weight = remaining * (1.0 - kept) * shading
     return (

time: 75 us -> 74.9 us (level)
  no operation moved by 1% of the time
where the time goes in v11:
time: 74.9 us; the launch traced here: 74.6 us
  blocking collectives  53.6 us (72%)
  Pallas kernels  12.4 us (17%)
  starting transfers between devices  8.35 us (11%)
    all_to_all x1, blocking collectives, rendered(): lax.all_to_all(sent, 'depth', 0, 0, axis_index_groups=groups, tiled=True)  29.7 us
    all_to_all x1, blocking collectives, rendered(): parts = lax.all_to_all(partial, 'depth', 0, 0, tiled=True)  23.9 us
    pallas_call x3, Pallas kernels, call(): pl.pallas_call(kernel, out_shape=VMEM(shape, jnp.float32), in_specs=[spec...  9.55 us
    ppermute x1, starting transfers between devices, rendered(): from_one = lax.ppermute(one, 'rows', pairs + [(b, a) for a, b in pairs])  6.39 us
  transfers between devices with their start and end apart: 3, of which 0 were waited for; matrix products, arithmetic and copies ran while one was open for 0% of the time, Pallas kernels for 12%

profile of v11, /device:TPU:1, one launch (start us, length us, event | category | flops | bytes accessed | tf_op | source)
XLA Modules:
  0.0 74.6 jit_solution(16547501543519913447)
XLA Ops:
  0.0 0.8 %slice_kernel.1 = (f32[2,4,512]{2,1,0:T(4,128)S(1)}, f32[2,4,512]{2,1,0:T(4,128)S(1)}) custom-call(f32[2,128,512]{2,1,0:T(8,128)} %density.3), custom_call_target="tpu_custom_call" | custom-call | tf_op jit(solution)/shard_map/slice_kernel/pallas_call | solution.py:527
  0.8 0.7 collective-permute-start.1
  1.5 6.4 %collective-permute-start = (f32[2,4,512]{2,1,0:T(4,128)S(1)}, f32[2,4,512]{2,1,0:T(4,128)S(1)}, u32[]{:S(2)}, u32[]{:S(2)}) collective-permute-start(f32[2,4,512]{2,1,0:T(4,128)S(1)} %get-tuple-element.8), channel_id=1, source_target_pairs={{0,1},{2,3},{1,0},{3,2},{4,5},{6,7},{5,4},{7,6},{8,9},{10,11},{9,8... | collective-permute-start | bytes 49160 | tf_op jit(solution)/shard_map/ppermute | solution.py:539
  7.9 1.3 %pack_kernel.1.sent = f32[1376,128]{1,0:T(8,128)S(1)} custom-call(f32[2,128,512]{2,1,0:T(8,128)} %density.3), custom_call_target="tpu_custom_call" | custom-call | tf_op jit(solution)/shard_map/pack_kernel/pallas_call | solution.py:543
  9.2 0.0 collective-permute-done.1.from_two
  9.2 0.0 collective-permute-done.from_one
  9.2 0.3 shard_map.28
  9.5 29.7 %all_to_all.16 = f32[16,86,1,128]{3,2,1,0:T(1,128)S(1)} all-to-all(f32[16,86,1,128]{3,2,1,0:T(1,128)S(1)} %bitcast.8), channel_id=1, replica_groups={{0,4,8,12,16,20,24,28,32,36,40,44,48,52,56,60},{64,68,72,76,80,84,88,92..., dimensions={0} | all-to-all | bytes 1409024 | tf_op jit(solution)/shard_map/all_to_all | solution.py:566
  39.2 0.0 copy-start
  39.2 1.3 %collective-permute-start.2 = (f32[344,128]{1,0:T(8,128)S(1)}, f32[344,128]{1,0:T(8,128)S(1)}, u32[]{:S(2)}, u32[]{:S(2)}) collective-permute-start(f32[344,128]{1,0:T(8,128)S(1)} %bitcast.14), channel_id=1, source_target_pairs={{64,0},{68,4},{72,8},{76,12},{80,16},{84,20},{88,24},{92,28},{96,3... | collective-permute-start | bytes 528392 | tf_op jit(solution)/shard_map/ppermute | solution.py:521
  40.5 0.0 copy-done
  40.5 0.1 copy.7
  40.6 7.4 %shard_map.29.inner = f32[14,48,128]{2,1,0:T(8,128)S(1)} custom-call(f32[1376,128]{1,0:T(8,128)S(1)} %bitcast.9, f32[16,4]{1,0:T(8,128)S(1)} %bitcast.12), custom_call_target="tpu_custom_call" | custom-call | tf_op jit(solution)/shard_map/pallas_call | solution.py:508
  47.9 0.0 collective-permute-done.2.after
  47.9 1.9 %shard_map.30 = f32[128,128]{1,0:T(8,128)S(1)} custom-call(f32[344,128]{1,0:T(8,128)S(1)} %collective-permute-done.2.after, f32[14,48,128]{2,1,0:T(8,128)S(1)} %shard_map.29.inner, f32[16,4]{1,0:T(8,128)S(1)} %bitcast.13), custom_call_target="tpu_custom_call" | custom-call | tf_op jit(solution)/shard_map/pallas_call | solution.py:508
  49.8 23.9 %all_to_all.17 = f32[128,1,128]{2,1,0:T(1,128)S(1)} all-to-all(f32[128,1,128]{2,1,0:T(1,128)S(1)} %bitcast.10), channel_id=1, replica_groups=mesh['depth'=128,'rows'=4] {'depth'}, dimensions={0} | all-to-all | bytes 131072 | tf_op jit(solution)/shard_map/all_to_all | solution.py:587
  73.8 0.8 %gather_kernel.1 = f32[4,1,512]{2,1,0:T(1,128)} custom-call(f32[128,128]{1,0:T(8,128)S(1)} %bitcast.11), custom_call_target="tpu_custom_call" | custom-call | tf_op jit(solution)/shard_map/gather_kernel/pallas_call | solution.py:589
  (1 shorter events, 0.0 us)
Async XLA Ops:
  0.8 8.3 %collective-permute-start.1 = (f32[2,4,512]{2,1,0:T(4,128)S(1)}, f32[2,4,512]{2,1,0:T(4,128)S(1)}, u32[]{:S(2)}, u32[]{:S(2)}) collective-permute-start(f32[2,4,512]{2,1,0:T(4,128)S(1)} %get-tuple-element.7.two), channel_id=1, source_target_pairs={{1,2},{2,1},{5,6},{6,5},{9,10},{10,9},{13,14},{14,13},{17,18},{18,... | collective-permute-start | bytes 49160 | tf_op jit(solution)/shard_map/ppermute | solution.py:541
  1.5 7.7 %collective-permute-start = (f32[2,4,512]{2,1,0:T(4,128)S(1)}, f32[2,4,512]{2,1,0:T(4,128)S(1)}, u32[]{:S(2)}, u32[]{:S(2)}) collective-permute-start(f32[2,4,512]{2,1,0:T(4,128)S(1)} %get-tuple-element.8), channel_id=1, source_target_pairs={{0,1},{2,3},{1,0},{3,2},{4,5},{6,7},{5,4},{7,6},{8,9},{10,11},{9,8... | collective-permute-start | bytes 49160 | tf_op jit(solution)/shard_map/ppermute | solution.py:539
  39.2 1.3 %copy-start = (f32[4,16]{1,0:T(4,128)S(1)}, f32[4,16]{1,0:T(4,128)}, u32[]{:S(2)}) copy-start(f32[4,16]{1,0:T(4,128)} %param.3) | copy-start | bytes 772
  39.2 8.8 %collective-permute-start.2 = (f32[344,128]{1,0:T(8,128)S(1)}, f32[344,128]{1,0:T(8,128)S(1)}, u32[]{:S(2)}, u32[]{:S(2)}) collective-permute-start(f32[344,128]{1,0:T(8,128)S(1)} %bitcast.14), channel_id=1, source_target_pairs={{64,0},{68,4},{72,8},{76,12},{80,16},{84,20},{88,24},{92,28},{96,3... | collective-permute-start | bytes 528392 | tf_op jit(solution)/shard_map/ppermute | solution.py:521

commit v12 on v11

--- a/solution.py
+++ b/solution.py
@@ -24,6 +24,7 @@
 SEGS = 3
 SEG_ROWS = 46
 RAW_ROWS = 43
+STARTS = (0, 42, 88)
 TILES = 6
 LINES = 8 * TILES
 PLANES = 2
@@ -112,7 +113,7 @@
             count = min(8, RAW_ROWS - 8 * j)
             rolled = []
             for k in range(SEGS):
-                start = RAW_ROWS * k + 8 * j
+                start = STARTS[k] + 8 * j if (k, j) != (2, TILES - 1) else STARTS[2] - 3
                 rows = own[p, start : start + 8, :]
                 tiles = [rows[:, LANES * q : LANES * (q + 1)] for q in range(4)]
                 rolled.append([pltpu.roll(x, WIDE * k, 1) if k else x for x in tiles])
@@ -217,34 +218,28 @@
         self.segment = [(local >= WIDE * k) & (local < WIDE * (k + 1)) for k in range(SEGS)]
         self.top = self.segment[0] & (row < HALO)
         self.bottom = self.segment[2] & (row < HALO)
-        self.head = self.segment[1] & (row == 0)
-        self.foot = self.segment[1] & (row >= 4) & (row < 6)
+        self.foot = self.segment[1] & (row >= 3)
 
     def unpack(self, raw, start):
         def load(by):
             return raw[pl.ds(start + by, 8), :]
 
-        zeroth, end = load(0), load(RAW_ROWS - 8)
+        lines = [load(8 * j) for j in range(TILES - 1)]
+        zeroth, end = lines[0], load(RAW_ROWS - 8)
         tiles = []
-        for j in range(TILES):
-            if j == 0:
-                parts = (pltpu.roll(zeroth, 4, 0), pltpu.roll(zeroth, 1, 0), load(2))
-            elif j < TILES - 1:
-                parts = (load(8 * j - 4), load(8 * j - 1), load(8 * j + 2))
-            else:
-                parts = (pltpu.roll(end, 7, 0), pltpu.roll(end, 4, 0), end)
-            rest = jnp.where(self.segment[1], parts[1], parts[2])
-            tiles.append(jnp.where(self.segment[0], parts[0], rest))
+        for j in range(TILES - 1):
+            first = load(8 * j - HALO) if j else pltpu.roll(zeroth, HALO, 0)
+            tiles.append(jnp.where(self.segment[0], first, lines[j]))
+        foot = pltpu.roll(pltpu.roll(end, LANES - WIDE, 1), 6, 0)
+        rest = jnp.where(self.foot, foot, pltpu.roll(end, 3, 0))
+        tiles.append(jnp.where(self.segment[0], pltpu.roll(end, 7, 0), rest))
         halo = None
         for g in range(WIDE // 8):
-            rows = load(8 * g) if g else zeroth
-            moved = pltpu.roll(rows, LANES - SPARE + 8 * g, 1)
+            moved = pltpu.roll(lines[g], LANES - SPARE + 8 * g, 1)
             halo = moved if halo is None else jnp.where(self.local >= 8 * g, moved, halo)
-        head = pltpu.roll(pltpu.roll(end, WIDE, 1), 1, 0)
-        foot = pltpu.roll(pltpu.roll(zeroth, LANES - WIDE, 1), 4, 0)
-        below = pltpu.roll(pltpu.roll(halo, 2 * WIDE, 1), 4, 0)
-        tiles[0] = jnp.where(self.top, halo, jnp.where(self.head, head, tiles[0]))
-        tiles[-1] = jnp.where(self.bottom, below, jnp.where(self.foot, foot, tiles[-1]))
+        below = pltpu.roll(pltpu.roll(halo, 2 * WIDE, 1), HALO, 0)
+        tiles[0] = jnp.where(self.top, halo, tiles[0])
+        tiles[-1] = jnp.where(self.bottom, below, tiles[-1])
         return tiles
 
 
@@ -315,7 +310,7 @@
     position = f * ((KNOTS - 1) / UPPER_DENSITY / SCALE)
     k = position.astype(jnp.int32)
     frac = position - k.astype(jnp.float32)
-    near_odd = lax.shift_right_logical(k, 1)
+    near_odd = jnp.bitwise_and(lax.shift_right_logical(k, 1), 7)
     near_even = jnp.bitwise_and(lax.shift_right_logical(k + 1, 1), 7)
     weight_odd = jnp.where(jnp.bitwise_and(k, 1) == 0, frac, 1.0 - frac)
     mixed = []
@@ -338,13 +333,13 @@
     is_first = tile.block == 0
 
     def fill(i, carry):
-        for u in range(4):
+        for u in range(2):
             for p in range(PLANES):
-                k = 4 * i + u
+                k = 2 * i + u
                 put(fa, FRONT + PLANES * k + p, tile.unpack(mine, CHUNK * k + RAW_ROWS * p))
         return carry
 
-    lax.fori_loop(0, GROUP // 4, fill, 0)
+    lax.fori_loop(0, GROUP // 2, fill, 0)
     for i in range(HALO):
         for j in range(TILES):
             plane = fa[FRONT + DEEP - HALO + i, rows_at(j), :]
@@ -430,22 +425,18 @@
     lookup = tables(knots)
     is_last = tile.block == BLOCKS - 1
 
-    def tail(to, i):
-        put(fa, to, [inner[TAIL + i, 8 * j : 8 * j + 8, :] for j in range(TILES)])
+    def tail(i):
+        return [inner[TAIL + i, 8 * j : 8 * j + 8, :] for j in range(TILES)]
 
     for i in range(2):
-        tail(i, HALO - 2 + i)
-
-    @pl.when(jnp.logical_not(is_last))
-    def _():
-        for i in range(2 * HALO):
-            k, p = divmod(i, PLANES)
-            put(fa, 2 + i, tile.unpack(after, CHUNK * k + RAW_ROWS * p))
-
-    @pl.when(is_last)
-    def _():
-        for i in range(2 * HALO):
-            tail(2 + i, max(HALO - 1 - i, 0))
+        put(fa, i, tail(HALO - 2 + i))
+    for i in range(2 * HALO):
+        k, p = divmod(i, PLANES)
+        plane = tile.unpack(after, CHUNK * k + RAW_ROWS * p)
+        if i < HALO:
+            mirror = tail(HALO - 1 - i)
+            plane = [jnp.where(is_last, mirror[j], plane[j]) for j in range(TILES)]
+        put(fa, 2 + i, plane)
 
     src, dst = fa, fb
     for sweep in range(PASSES):

time: 74.9 us -> 76.5 us (1.021)
  Pallas kernels: 12.4 us -> 14 us
    pallas_call x3, Pallas kernels: 9.55 us -> 11.1 us  [call(): pl.pallas_call(kernel, out_shape=VMEM(shape, jnp.float32), in_specs=[spec...]
where the time goes in v12:
time: 76.5 us; the launch traced here: 76.1 us
  blocking collectives  53.6 us (70%)
  Pallas kernels  14 us (18%)
  starting transfers between devices  8.35 us (11%)
    all_to_all x1, blocking collectives, rendered(): lax.all_to_all(sent, 'depth', 0, 0, axis_index_groups=groups, tiled=True)  29.7 us
    all_to_all x1, blocking collectives, rendered(): parts = lax.all_to_all(partial, 'depth', 0, 0, tiled=True)  23.9 us
    pallas_call x3, Pallas kernels, call(): pl.pallas_call(kernel, out_shape=VMEM(shape, jnp.float32), in_specs=[spec...  11.1 us
    ppermute x1, starting transfers between devices, rendered(): from_one = lax.ppermute(one, 'rows', pairs + [(b, a) for a, b in pairs])  6.39 us
  transfers between devices with their start and end apart: 3, of which 0 were waited for; matrix products, arithmetic and copies ran while one was open for 0% of the time, Pallas kernels for 12%

profile of v12, /device:TPU:1, one launch (start us, length us, event | category | flops | bytes accessed | tf_op | source)
XLA Modules:
  0.0 76.1 jit_solution(3973504642470277990)
XLA Ops:
  0.0 0.8 %slice_kernel.1 = (f32[2,4,512]{2,1,0:T(4,128)S(1)}, f32[2,4,512]{2,1,0:T(4,128)S(1)}) custom-call(f32[2,128,512]{2,1,0:T(8,128)} %density.3), custom_call_target="tpu_custom_call" | custom-call | tf_op jit(solution)/shard_map/slice_kernel/pallas_call | solution.py:518
  0.8 0.7 collective-permute-start.1
  1.5 6.4 %collective-permute-start = (f32[2,4,512]{2,1,0:T(4,128)S(1)}, f32[2,4,512]{2,1,0:T(4,128)S(1)}, u32[]{:S(2)}, u32[]{:S(2)}) collective-permute-start(f32[2,4,512]{2,1,0:T(4,128)S(1)} %get-tuple-element.8), channel_id=1, source_target_pairs={{0,1},{2,3},{1,0},{3,2},{4,5},{6,7},{5,4},{7,6},{8,9},{10,11},{9,8... | collective-permute-start | bytes 49160 | tf_op jit(solution)/shard_map/ppermute | solution.py:530
  7.9 1.3 %pack_kernel.1.sent = f32[1376,128]{1,0:T(8,128)S(1)} custom-call(f32[2,128,512]{2,1,0:T(8,128)} %density.3), custom_call_target="tpu_custom_call" | custom-call | tf_op jit(solution)/shard_map/pack_kernel/pallas_call | solution.py:534
  9.1 0.0 collective-permute-done.1.from_two
  9.2 0.0 collective-permute-done.from_one
  9.2 0.3 shard_map.28
  9.5 29.7 %all_to_all.16 = f32[16,86,1,128]{3,2,1,0:T(1,128)S(1)} all-to-all(f32[16,86,1,128]{3,2,1,0:T(1,128)S(1)} %bitcast.8), channel_id=1, replica_groups={{0,4,8,12,16,20,24,28,32,36,40,44,48,52,56,60},{64,68,72,76,80,84,88,92..., dimensions={0} | all-to-all | bytes 1409024 | tf_op jit(solution)/shard_map/all_to_all | solution.py:557
  39.2 0.0 copy-start
  39.2 1.3 %collective-permute-start.2 = (f32[344,128]{1,0:T(8,128)S(1)}, f32[344,128]{1,0:T(8,128)S(1)}, u32[]{:S(2)}, u32[]{:S(2)}) collective-permute-start(f32[344,128]{1,0:T(8,128)S(1)} %bitcast.14), channel_id=1, source_target_pairs={{64,0},{68,4},{72,8},{76,12},{80,16},{84,20},{88,24},{92,28},{96,3... | collective-permute-start | bytes 528392 | tf_op jit(solution)/shard_map/ppermute | solution.py:512
  40.5 0.0 copy-done
  40.5 0.1 copy.7
  40.6 8.2 %shard_map.29.inner = f32[14,48,128]{2,1,0:T(8,128)S(1)} custom-call(f32[1376,128]{1,0:T(8,128)S(1)} %bitcast.9, f32[16,4]{1,0:T(8,128)S(1)} %bitcast.12), custom_call_target="tpu_custom_call" | custom-call | tf_op jit(solution)/shard_map/pallas_call | solution.py:499
  48.7 0.0 collective-permute-done.2.after
  48.7 2.6 %shard_map.30 = f32[128,128]{1,0:T(8,128)S(1)} custom-call(f32[344,128]{1,0:T(8,128)S(1)} %collective-permute-done.2.after, f32[14,48,128]{2,1,0:T(8,128)S(1)} %shard_map.29.inner, f32[16,4]{1,0:T(8,128)S(1)} %bitcast.13), custom_call_target="tpu_custom_call" | custom-call | tf_op jit(solution)/shard_map/pallas_call | solution.py:499
  51.4 23.9 %all_to_all.17 = f32[128,1,128]{2,1,0:T(1,128)S(1)} all-to-all(f32[128,1,128]{2,1,0:T(1,128)S(1)} %bitcast.10), channel_id=1, replica_groups=mesh['depth'=128,'rows'=4] {'depth'}, dimensions={0} | all-to-all | bytes 131072 | tf_op jit(solution)/shard_map/all_to_all | solution.py:578
  75.3 0.8 %gather_kernel.1 = f32[4,1,512]{2,1,0:T(1,128)} custom-call(f32[128,128]{1,0:T(8,128)S(1)} %bitcast.11), custom_call_target="tpu_custom_call" | custom-call | tf_op jit(solution)/shard_map/gather_kernel/pallas_call | solution.py:580
  (1 shorter events, 0.0 us)
Async XLA Ops:
  0.8 8.3 %collective-permute-start.1 = (f32[2,4,512]{2,1,0:T(4,128)S(1)}, f32[2,4,512]{2,1,0:T(4,128)S(1)}, u32[]{:S(2)}, u32[]{:S(2)}) collective-permute-start(f32[2,4,512]{2,1,0:T(4,128)S(1)} %get-tuple-element.7.two), channel_id=1, source_target_pairs={{1,2},{2,1},{5,6},{6,5},{9,10},{10,9},{13,14},{14,13},{17,18},{18,... | collective-permute-start | bytes 49160 | tf_op jit(solution)/shard_map/ppermute | solution.py:532
  1.5 7.7 %collective-permute-start = (f32[2,4,512]{2,1,0:T(4,128)S(1)}, f32[2,4,512]{2,1,0:T(4,128)S(1)}, u32[]{:S(2)}, u32[]{:S(2)}) collective-permute-start(f32[2,4,512]{2,1,0:T(4,128)S(1)} %get-tuple-element.8), channel_id=1, source_target_pairs={{0,1},{2,3},{1,0},{3,2},{4,5},{6,7},{5,4},{7,6},{8,9},{10,11},{9,8... | collective-permute-start | bytes 49160 | tf_op jit(solution)/shard_map/ppermute | solution.py:530
  39.2 1.3 %copy-start = (f32[4,16]{1,0:T(4,128)S(1)}, f32[4,16]{1,0:T(4,128)}, u32[]{:S(2)}) copy-start(f32[4,16]{1,0:T(4,128)} %param.3) | copy-start | bytes 772
  39.2 9.6 %collective-permute-start.2 = (f32[344,128]{1,0:T(8,128)S(1)}, f32[344,128]{1,0:T(8,128)S(1)}, u32[]{:S(2)}, u32[]{:S(2)}) collective-permute-start(f32[344,128]{1,0:T(8,128)S(1)} %bitcast.14), channel_id=1, source_target_pairs={{64,0},{68,4},{72,8},{76,12},{80,16},{84,20},{88,24},{92,28},{96,3... | collective-permute-start | bytes 528392 | tf_op jit(solution)/shard_map/ppermute | solution.py:512

commit v13 on v11

--- a/solution.py
+++ b/solution.py
@@ -315,7 +315,7 @@
     position = f * ((KNOTS - 1) / UPPER_DENSITY / SCALE)
     k = position.astype(jnp.int32)
     frac = position - k.astype(jnp.float32)
-    near_odd = lax.shift_right_logical(k, 1)
+    near_odd = jnp.bitwise_and(lax.shift_right_logical(k, 1), 7)
     near_even = jnp.bitwise_and(lax.shift_right_logical(k + 1, 1), 7)
     weight_odd = jnp.where(jnp.bitwise_and(k, 1) == 0, frac, 1.0 - frac)
     mixed = []
@@ -338,13 +338,13 @@
     is_first = tile.block == 0
 
     def fill(i, carry):
-        for u in range(4):
+        for u in range(8):
             for p in range(PLANES):
-                k = 4 * i + u
+                k = 8 * i + u
                 put(fa, FRONT + PLANES * k + p, tile.unpack(mine, CHUNK * k + RAW_ROWS * p))
         return carry
 
-    lax.fori_loop(0, GROUP // 4, fill, 0)
+    lax.fori_loop(0, GROUP // 8, fill, 0)
     for i in range(HALO):
         for j in range(TILES):
             plane = fa[FRONT + DEEP - HALO + i, rows_at(j), :]

time: 74.9 us -> 74.7 us (level)
  transfers between devices with their start and end apart: 3 -> 3, of which waited for: 0 -> 0; matrix products, arithmetic and copies ran while one was open for 0% -> 0% of each run, Pallas kernels for 12% -> 11%
where the time goes in v13:
time: 74.7 us; the launch traced here: 74.3 us
  blocking collectives  53.6 us (72%)
  Pallas kernels  12.2 us (16%)
  starting transfers between devices  8.35 us (11%)
    all_to_all x1, blocking collectives, rendered(): lax.all_to_all(sent, 'depth', 0, 0, axis_index_groups=groups, tiled=True)  29.7 us
    all_to_all x1, blocking collectives, rendered(): parts = lax.all_to_all(partial, 'depth', 0, 0, tiled=True)  23.9 us
    pallas_call x3, Pallas kernels, call(): pl.pallas_call(kernel, out_shape=VMEM(shape, jnp.float32), in_specs=[spec...  9.29 us
    ppermute x1, starting transfers between devices, rendered(): from_one = lax.ppermute(one, 'rows', pairs + [(b, a) for a, b in pairs])  6.39 us
  transfers between devices with their start and end apart: 3, of which 0 were waited for; matrix products, arithmetic and copies ran while one was open for 0% of the time, Pallas kernels for 11%

profile of v13, /device:TPU:1, one launch (start us, length us, event | category | flops | bytes accessed | tf_op | source)
XLA Modules:
  0.0 74.3 jit_solution(14482907427409274323)
XLA Ops:
  0.0 0.8 %slice_kernel.1 = (f32[2,4,512]{2,1,0:T(4,128)S(1)}, f32[2,4,512]{2,1,0:T(4,128)S(1)}) custom-call(f32[2,128,512]{2,1,0:T(8,128)} %density.3), custom_call_target="tpu_custom_call" | custom-call | tf_op jit(solution)/shard_map/slice_kernel/pallas_call | solution.py:527
  0.8 0.7 collective-permute-start.1
  1.5 6.4 %collective-permute-start = (f32[2,4,512]{2,1,0:T(4,128)S(1)}, f32[2,4,512]{2,1,0:T(4,128)S(1)}, u32[]{:S(2)}, u32[]{:S(2)}) collective-permute-start(f32[2,4,512]{2,1,0:T(4,128)S(1)} %get-tuple-element.8), channel_id=1, source_target_pairs={{0,1},{2,3},{1,0},{3,2},{4,5},{6,7},{5,4},{7,6},{8,9},{10,11},{9,8... | collective-permute-start | bytes 49160 | tf_op jit(solution)/shard_map/ppermute | solution.py:539
  7.9 1.3 %pack_kernel.1.sent = f32[1376,128]{1,0:T(8,128)S(1)} custom-call(f32[2,128,512]{2,1,0:T(8,128)} %density.3), custom_call_target="tpu_custom_call" | custom-call | tf_op jit(solution)/shard_map/pack_kernel/pallas_call | solution.py:543
  9.2 0.0 collective-permute-done.1.from_two
  9.2 0.0 collective-permute-done.from_one
  9.2 0.3 shard_map.28
  9.5 29.7 %all_to_all.16 = f32[16,86,1,128]{3,2,1,0:T(1,128)S(1)} all-to-all(f32[16,86,1,128]{3,2,1,0:T(1,128)S(1)} %bitcast.8), channel_id=1, replica_groups={{0,4,8,12,16,20,24,28,32,36,40,44,48,52,56,60},{64,68,72,76,80,84,88,92..., dimensions={0} | all-to-all | bytes 1409024 | tf_op jit(solution)/shard_map/all_to_all | solution.py:566
  39.2 0.0 copy-start
  39.2 1.3 %collective-permute-start.2 = (f32[344,128]{1,0:T(8,128)S(1)}, f32[344,128]{1,0:T(8,128)S(1)}, u32[]{:S(2)}, u32[]{:S(2)}) collective-permute-start(f32[344,128]{1,0:T(8,128)S(1)} %bitcast.14), channel_id=1, source_target_pairs={{64,0},{68,4},{72,8},{76,12},{80,16},{84,20},{88,24},{92,28},{96,3... | collective-permute-start | bytes 528392 | tf_op jit(solution)/shard_map/ppermute | solution.py:521
  40.5 0.0 copy-done
  40.5 0.1 copy.7
  40.6 7.1 %shard_map.29.inner = f32[14,48,128]{2,1,0:T(8,128)S(1)} custom-call(f32[1376,128]{1,0:T(8,128)S(1)} %bitcast.9, f32[16,4]{1,0:T(8,128)S(1)} %bitcast.12), custom_call_target="tpu_custom_call" | custom-call | tf_op jit(solution)/shard_map/pallas_call | solution.py:508
  47.7 0.0 collective-permute-done.2.after
  47.7 1.9 %shard_map.30 = f32[128,128]{1,0:T(8,128)S(1)} custom-call(f32[344,128]{1,0:T(8,128)S(1)} %collective-permute-done.2.after, f32[14,48,128]{2,1,0:T(8,128)S(1)} %shard_map.29.inner, f32[16,4]{1,0:T(8,128)S(1)} %bitcast.13), custom_call_target="tpu_custom_call" | custom-call | tf_op jit(solution)/shard_map/pallas_call | solution.py:508
  49.6 23.9 %all_to_all.17 = f32[128,1,128]{2,1,0:T(1,128)S(1)} all-to-all(f32[128,1,128]{2,1,0:T(1,128)S(1)} %bitcast.10), channel_id=1, replica_groups=mesh['depth'=128,'rows'=4] {'depth'}, dimensions={0} | all-to-all | bytes 131072 | tf_op jit(solution)/shard_map/all_to_all | solution.py:587
  73.5 0.8 %gather_kernel.1 = f32[4,1,512]{2,1,0:T(1,128)} custom-call(f32[128,128]{1,0:T(8,128)S(1)} %bitcast.11), custom_call_target="tpu_custom_call" | custom-call | tf_op jit(solution)/shard_map/gather_kernel/pallas_call | solution.py:589
  (1 shorter events, 0.0 us)
Async XLA Ops:
  0.8 8.3 %collective-permute-start.1 = (f32[2,4,512]{2,1,0:T(4,128)S(1)}, f32[2,4,512]{2,1,0:T(4,128)S(1)}, u32[]{:S(2)}, u32[]{:S(2)}) collective-permute-start(f32[2,4,512]{2,1,0:T(4,128)S(1)} %get-tuple-element.7.two), channel_id=1, source_target_pairs={{1,2},{2,1},{5,6},{6,5},{9,10},{10,9},{13,14},{14,13},{17,18},{18,... | collective-permute-start | bytes 49160 | tf_op jit(solution)/shard_map/ppermute | solution.py:541
  1.5 7.7 %collective-permute-start = (f32[2,4,512]{2,1,0:T(4,128)S(1)}, f32[2,4,512]{2,1,0:T(4,128)S(1)}, u32[]{:S(2)}, u32[]{:S(2)}) collective-permute-start(f32[2,4,512]{2,1,0:T(4,128)S(1)} %get-tuple-element.8), channel_id=1, source_target_pairs={{0,1},{2,3},{1,0},{3,2},{4,5},{6,7},{5,4},{7,6},{8,9},{10,11},{9,8... | collective-permute-start | bytes 49160 | tf_op jit(solution)/shard_map/ppermute | solution.py:539
  39.2 1.3 %copy-start = (f32[4,16]{1,0:T(4,128)S(1)}, f32[4,16]{1,0:T(4,128)}, u32[]{:S(2)}) copy-start(f32[4,16]{1,0:T(4,128)} %param.3) | copy-start | bytes 772
  39.2 8.5 %collective-permute-start.2 = (f32[344,128]{1,0:T(8,128)S(1)}, f32[344,128]{1,0:T(8,128)S(1)}, u32[]{:S(2)}, u32[]{:S(2)}) collective-permute-start(f32[344,128]{1,0:T(8,128)S(1)} %bitcast.14), channel_id=1, source_target_pairs={{64,0},{68,4},{72,8},{76,12},{80,16},{84,20},{88,24},{92,28},{96,3... | collective-permute-start | bytes 528392 | tf_op jit(solution)/shard_map/ppermute | solution.py:521

commit v14 on v13

--- a/solution.py
+++ b/solution.py
@@ -346,9 +346,7 @@
 
     lax.fori_loop(0, GROUP // 8, fill, 0)
     for i in range(HALO):
-        for j in range(TILES):
-            plane = fa[FRONT + DEEP - HALO + i, rows_at(j), :]
-            out[TAIL + i, 8 * j : 8 * j + 8, :] = plane
+        out[TAIL + i] = fa[FRONT + DEEP - HALO + i]
 
     @pl.when(is_first)
     def _():
@@ -381,8 +379,7 @@
             p = lo + unroll * whole + u
             carry = diffuse(src, p, dst, p, fluxes, u, carry, tile)
         for i in range(2):
-            for j in range(TILES):
-                out[2 * sweep + i, 8 * j : 8 * j + 8, :] = dst[hi - 2 + i, rows_at(j), :]
+            out[2 * sweep + i] = dst[hi - 2 + i]
         src, dst = dst, src
 
     lookup = tables(knots)
@@ -431,7 +428,7 @@
     is_last = tile.block == BLOCKS - 1
 
     def tail(to, i):
-        put(fa, to, [inner[TAIL + i, 8 * j : 8 * j + 8, :] for j in range(TILES)])
+        fa[to] = inner[TAIL + i]
 
     for i in range(2):
         tail(i, HALO - 2 + i)
@@ -453,8 +450,7 @@
         for i in range(2 * HALO):
             carry = diffuse(src, i + 1, dst, i + 2, fluxes, i, carry, tile)
         for i in range(2):
-            rest = [inner[2 * sweep + i, 8 * j : 8 * j + 8, :] for j in range(TILES)]
-            put(dst, i, rest)
+            dst[i] = inner[2 * sweep + i]
         src, dst = dst, src
 
     lane = lane_index()
@@ -570,7 +566,7 @@
     field = (FRONT + DEEP, TALL, LANES)
     inner = call(
         inner_kernel,
-        (TAIL + HALO, LINES, LANES),
+        (TAIL + HALO, TALL, LANES),
         [field, field, (UNROLL, TALL, LANES), (4, LINES, LANES)],
         mine,
         knots,

time: 74.7 us -> 74.5 us (level)
  no operation moved by 1% of the time
where the time goes in v14:
time: 74.5 us; the launch traced here: 74.2 us
  blocking collectives  53.6 us (72%)
  Pallas kernels  12 us (16%)
  starting transfers between devices  8.35 us (11%)
    all_to_all x1, blocking collectives, rendered(): lax.all_to_all(sent, 'depth', 0, 0, axis_index_groups=groups, tiled=True)  29.7 us
    all_to_all x1, blocking collectives, rendered(): parts = lax.all_to_all(partial, 'depth', 0, 0, tiled=True)  23.9 us
    pallas_call x3, Pallas kernels, call(): pl.pallas_call(kernel, out_shape=VMEM(shape, jnp.float32), in_specs=[spec...  9.18 us
    ppermute x1, starting transfers between devices, rendered(): from_one = lax.ppermute(one, 'rows', pairs + [(b, a) for a, b in pairs])  6.39 us
  transfers between devices with their start and end apart: 3, of which 0 were waited for; matrix products, arithmetic and copies ran while one was open for 0% of the time, Pallas kernels for 11%

profile of v14, /device:TPU:1, one launch (start us, length us, event | category | flops | bytes accessed | tf_op | source)
XLA Modules:
  0.0 74.2 jit_solution(12302332502166355677)
XLA Ops:
  0.0 0.8 %slice_kernel.1 = (f32[2,4,512]{2,1,0:T(4,128)S(1)}, f32[2,4,512]{2,1,0:T(4,128)S(1)}) custom-call(f32[2,128,512]{2,1,0:T(8,128)} %density.3), custom_call_target="tpu_custom_call" | custom-call | tf_op jit(solution)/shard_map/slice_kernel/pallas_call | solution.py:523
  0.8 0.7 collective-permute-start.1
  1.5 6.4 %collective-permute-start = (f32[2,4,512]{2,1,0:T(4,128)S(1)}, f32[2,4,512]{2,1,0:T(4,128)S(1)}, u32[]{:S(2)}, u32[]{:S(2)}) collective-permute-start(f32[2,4,512]{2,1,0:T(4,128)S(1)} %get-tuple-element.8), channel_id=1, source_target_pairs={{0,1},{2,3},{1,0},{3,2},{4,5},{6,7},{5,4},{7,6},{8,9},{10,11},{9,8... | collective-permute-start | bytes 49160 | tf_op jit(solution)/shard_map/ppermute | solution.py:535
  7.9 1.3 %pack_kernel.1.sent = f32[1376,128]{1,0:T(8,128)S(1)} custom-call(f32[2,128,512]{2,1,0:T(8,128)} %density.3), custom_call_target="tpu_custom_call" | custom-call | tf_op jit(solution)/shard_map/pack_kernel/pallas_call | solution.py:539
  9.2 0.0 collective-permute-done.1.from_two
  9.2 0.0 collective-permute-done.from_one
  9.2 0.3 shard_map.28
  9.5 29.7 %all_to_all.16 = f32[16,86,1,128]{3,2,1,0:T(1,128)S(1)} all-to-all(f32[16,86,1,128]{3,2,1,0:T(1,128)S(1)} %bitcast.8), channel_id=1, replica_groups={{0,4,8,12,16,20,24,28,32,36,40,44,48,52,56,60},{64,68,72,76,80,84,88,92..., dimensions={0} | all-to-all | bytes 1409024 | tf_op jit(solution)/shard_map/all_to_all | solution.py:562
  39.2 0.0 copy-start
  39.2 1.3 %collective-permute-start.2 = (f32[344,128]{1,0:T(8,128)S(1)}, f32[344,128]{1,0:T(8,128)S(1)}, u32[]{:S(2)}, u32[]{:S(2)}) collective-permute-start(f32[344,128]{1,0:T(8,128)S(1)} %bitcast.14), channel_id=1, source_target_pairs={{64,0},{68,4},{72,8},{76,12},{80,16},{84,20},{88,24},{92,28},{96,3... | collective-permute-start | bytes 528392 | tf_op jit(solution)/shard_map/ppermute | solution.py:517
  40.5 0.0 copy-done
  40.5 0.1 copy.7
  40.6 7.1 %shard_map.29.inner = f32[14,64,128]{2,1,0:T(8,128)S(1)} custom-call(f32[1376,128]{1,0:T(8,128)S(1)} %bitcast.9, f32[16,4]{1,0:T(8,128)S(1)} %bitcast.12), custom_call_target="tpu_custom_call" | custom-call | tf_op jit(solution)/shard_map/pallas_call | solution.py:504
  47.7 0.0 collective-permute-done.2.after
  47.7 1.8 %shard_map.30 = f32[128,128]{1,0:T(8,128)S(1)} custom-call(f32[344,128]{1,0:T(8,128)S(1)} %collective-permute-done.2.after, f32[14,64,128]{2,1,0:T(8,128)S(1)} %shard_map.29.inner, f32[16,4]{1,0:T(8,128)S(1)} %bitcast.13), custom_call_target="tpu_custom_call" | custom-call | tf_op jit(solution)/shard_map/pallas_call | solution.py:504
  49.5 23.9 %all_to_all.17 = f32[128,1,128]{2,1,0:T(1,128)S(1)} all-to-all(f32[128,1,128]{2,1,0:T(1,128)S(1)} %bitcast.11), channel_id=1, replica_groups=mesh['depth'=128,'rows'=4] {'depth'}, dimensions={0} | all-to-all | bytes 131072 | tf_op jit(solution)/shard_map/all_to_all | solution.py:583
  73.4 0.8 %gather_kernel.1 = f32[4,1,512]{2,1,0:T(1,128)} custom-call(f32[128,128]{1,0:T(8,128)S(1)} %bitcast.10), custom_call_target="tpu_custom_call" | custom-call | tf_op jit(solution)/shard_map/gather_kernel/pallas_call | solution.py:585
  (1 shorter events, 0.0 us)
Async XLA Ops:
  0.8 8.3 %collective-permute-start.1 = (f32[2,4,512]{2,1,0:T(4,128)S(1)}, f32[2,4,512]{2,1,0:T(4,128)S(1)}, u32[]{:S(2)}, u32[]{:S(2)}) collective-permute-start(f32[2,4,512]{2,1,0:T(4,128)S(1)} %get-tuple-element.7.two), channel_id=1, source_target_pairs={{1,2},{2,1},{5,6},{6,5},{9,10},{10,9},{13,14},{14,13},{17,18},{18,... | collective-permute-start | bytes 49160 | tf_op jit(solution)/shard_map/ppermute | solution.py:537
  1.5 7.7 %collective-permute-start = (f32[2,4,512]{2,1,0:T(4,128)S(1)}, f32[2,4,512]{2,1,0:T(4,128)S(1)}, u32[]{:S(2)}, u32[]{:S(2)}) collective-permute-start(f32[2,4,512]{2,1,0:T(4,128)S(1)} %get-tuple-element.8), channel_id=1, source_target_pairs={{0,1},{2,3},{1,0},{3,2},{4,5},{6,7},{5,4},{7,6},{8,9},{10,11},{9,8... | collective-permute-start | bytes 49160 | tf_op jit(solution)/shard_map/ppermute | solution.py:535
  39.2 1.3 %copy-start = (f32[4,16]{1,0:T(4,128)S(1)}, f32[4,16]{1,0:T(4,128)}, u32[]{:S(2)}) copy-start(f32[4,16]{1,0:T(4,128)} %param.3) | copy-start | bytes 772
  39.2 8.5 %collective-permute-start.2 = (f32[344,128]{1,0:T(8,128)S(1)}, f32[344,128]{1,0:T(8,128)S(1)}, u32[]{:S(2)}, u32[]{:S(2)}) collective-permute-start(f32[344,128]{1,0:T(8,128)S(1)} %bitcast.14), channel_id=1, source_target_pairs={{64,0},{68,4},{72,8},{76,12},{80,16},{84,20},{88,24},{92,28},{96,3... | collective-permute-start | bytes 528392 | tf_op jit(solution)/shard_map/ppermute | solution.py:517

commit v15 on v14

--- a/solution.py
+++ b/solution.py
@@ -24,6 +24,7 @@
 SEGS = 3
 SEG_ROWS = 46
 RAW_ROWS = 43
+TURN = WIDE - TILE
 TILES = 6
 LINES = 8 * TILES
 PLANES = 2
@@ -461,12 +462,17 @@
                 own = sums
             sums = shade(src, i + 1, j, sums, lookup, tile)
         sums = [jnp.where(is_last, own[c], sums[c]) for c in range(4)]
+        turned = []
+        for m in range(4):
+            rest = jnp.where(tile.segment[1], sums[(m + 1) % 4], sums[(m + 2) % 4])
+            picked = jnp.where(tile.segment[0], sums[m], rest)
+            by = TILE * m - HALO - tile.start + LANES * 2
+            turned.append(pltpu.roll(picked, lax.rem(by, LANES), 1))
         for k in range(SEGS):
-            value = None
-            for c in range(4):
-                by = TILE * c - WIDE * k - HALO - tile.start + LANES * 2
-                moved = pltpu.roll(sums[c], lax.rem(by, LANES), 1)
-                value = moved if value is None else jnp.where(lane >= TILE * c, moved, value)
+            place = (lane - TURN * k + LANES) % LANES
+            value = turned[-k % 4]
+            for c in range(1, 4):
+                value = jnp.where(place >= TILE * c, turned[(c - k) % 4], value)
             first = SEG_ROWS * k + 8 * j - HALO
             lo, hi = max(first, 0), min(first + min(8, SEG_ROWS - 8 * j), BAND)
             if lo < hi:
@@ -475,10 +481,12 @@
 
 def gather_kernel(parts, out):
     lane = lane_index(GROUP)
+    segment = (lax.axis_index("depth") + HALO) // SEG_ROWS
+    back = lax.rem(LANES - TURN * segment, LANES)
     total = jnp.zeros((GROUP, LANES), jnp.float32)
     remaining = jnp.ones((GROUP, LANES), jnp.float32)
     for b in range(BLOCKS):
-        v = parts[GROUP * b : GROUP * (b + 1)]
+        v = pltpu.roll(parts[GROUP * b : GROUP * (b + 1)], back, 1)
         kept = v
         for c in range(3):
             kept = jnp.where(

time: 74.5 us -> 74.6 us (level)
  no operation moved by 1% of the time
where the time goes in v15:
time: 74.6 us; the launch traced here: 74.3 us
  blocking collectives  53.6 us (72%)
  Pallas kernels  12.1 us (16%)
  starting transfers between devices  8.35 us (11%)
    all_to_all x1, blocking collectives, rendered(): lax.all_to_all(sent, 'depth', 0, 0, axis_index_groups=groups, tiled=True)  29.7 us
    all_to_all x1, blocking collectives, rendered(): parts = lax.all_to_all(partial, 'depth', 0, 0, tiled=True)  23.9 us
    pallas_call x3, Pallas kernels, call(): pl.pallas_call(kernel, out_shape=VMEM(shape, jnp.float32), in_specs=[spec...  9.18 us
    ppermute x1, starting transfers between devices, rendered(): from_one = lax.ppermute(one, 'rows', pairs + [(b, a) for a, b in pairs])  6.39 us
  transfers between devices with their start and end apart: 3, of which 0 were waited for; matrix products, arithmetic and copies ran while one was open for 0% of the time, Pallas kernels for 11%

profile of v15, /device:TPU:1, one launch (start us, length us, event | category | flops | bytes accessed | tf_op | source)
XLA Modules:
  0.0 74.3 jit_solution(1350866245360419293)
XLA Ops:
  0.0 0.8 %slice_kernel.1 = (f32[2,4,512]{2,1,0:T(4,128)S(1)}, f32[2,4,512]{2,1,0:T(4,128)S(1)}) custom-call(f32[2,128,512]{2,1,0:T(8,128)} %density.3), custom_call_target="tpu_custom_call" | custom-call | tf_op jit(solution)/shard_map/slice_kernel/pallas_call | solution.py:531
  0.8 0.7 collective-permute-start.1
  1.5 6.4 %collective-permute-start = (f32[2,4,512]{2,1,0:T(4,128)S(1)}, f32[2,4,512]{2,1,0:T(4,128)S(1)}, u32[]{:S(2)}, u32[]{:S(2)}) collective-permute-start(f32[2,4,512]{2,1,0:T(4,128)S(1)} %get-tuple-element.8), channel_id=1, source_target_pairs={{0,1},{2,3},{1,0},{3,2},{4,5},{6,7},{5,4},{7,6},{8,9},{10,11},{9,8... | collective-permute-start | bytes 49160 | tf_op jit(solution)/shard_map/ppermute | solution.py:543
  7.9 1.3 %pack_kernel.1.sent = f32[1376,128]{1,0:T(8,128)S(1)} custom-call(f32[2,128,512]{2,1,0:T(8,128)} %density.3), custom_call_target="tpu_custom_call" | custom-call | tf_op jit(solution)/shard_map/pack_kernel/pallas_call | solution.py:547
  9.2 0.0 collective-permute-done.1.from_two
  9.2 0.0 collective-permute-done.from_one
  9.2 0.3 shard_map.28
  9.5 29.7 %all_to_all.16 = f32[16,86,1,128]{3,2,1,0:T(1,128)S(1)} all-to-all(f32[16,86,1,128]{3,2,1,0:T(1,128)S(1)} %bitcast.8), channel_id=1, replica_groups={{0,4,8,12,16,20,24,28,32,36,40,44,48,52,56,60},{64,68,72,76,80,84,88,92..., dimensions={0} | all-to-all | bytes 1409024 | tf_op jit(solution)/shard_map/all_to_all | solution.py:570
  39.2 0.0 copy-start
  39.2 1.3 %collective-permute-start.2 = (f32[344,128]{1,0:T(8,128)S(1)}, f32[344,128]{1,0:T(8,128)S(1)}, u32[]{:S(2)}, u32[]{:S(2)}) collective-permute-start(f32[344,128]{1,0:T(8,128)S(1)} %bitcast.14), channel_id=1, source_target_pairs={{64,0},{68,4},{72,8},{76,12},{80,16},{84,20},{88,24},{92,28},{96,3... | collective-permute-start | bytes 528392 | tf_op jit(solution)/shard_map/ppermute | solution.py:525
  40.5 0.0 copy-done
  40.5 0.1 copy.7
  40.6 7.1 %shard_map.29.inner = f32[14,64,128]{2,1,0:T(8,128)S(1)} custom-call(f32[1376,128]{1,0:T(8,128)S(1)} %bitcast.9, f32[16,4]{1,0:T(8,128)S(1)} %bitcast.12), custom_call_target="tpu_custom_call" | custom-call | tf_op jit(solution)/shard_map/pallas_call | solution.py:512
  47.7 0.0 collective-permute-done.2.after
  47.7 1.8 %shard_map.30 = f32[128,128]{1,0:T(8,128)S(1)} custom-call(f32[344,128]{1,0:T(8,128)S(1)} %collective-permute-done.2.after, f32[14,64,128]{2,1,0:T(8,128)S(1)} %shard_map.29.inner, f32[16,4]{1,0:T(8,128)S(1)} %bitcast.13), custom_call_target="tpu_custom_call" | custom-call | tf_op jit(solution)/shard_map/pallas_call | solution.py:512
  49.5 23.9 %all_to_all.17 = f32[128,1,128]{2,1,0:T(1,128)S(1)} all-to-all(f32[128,1,128]{2,1,0:T(1,128)S(1)} %bitcast.11), channel_id=1, replica_groups=mesh['depth'=128,'rows'=4] {'depth'}, dimensions={0} | all-to-all | bytes 131072 | tf_op jit(solution)/shard_map/all_to_all | solution.py:591
  73.4 0.9 %gather_kernel.1 = f32[4,1,512]{2,1,0:T(1,128)} custom-call(f32[128,128]{1,0:T(8,128)S(1)} %bitcast.10), custom_call_target="tpu_custom_call" | custom-call | tf_op jit(solution)/shard_map/gather_kernel/pallas_call | solution.py:593
  (1 shorter events, 0.0 us)
Async XLA Ops:
  0.8 8.3 %collective-permute-start.1 = (f32[2,4,512]{2,1,0:T(4,128)S(1)}, f32[2,4,512]{2,1,0:T(4,128)S(1)}, u32[]{:S(2)}, u32[]{:S(2)}) collective-permute-start(f32[2,4,512]{2,1,0:T(4,128)S(1)} %get-tuple-element.7.two), channel_id=1, source_target_pairs={{1,2},{2,1},{5,6},{6,5},{9,10},{10,9},{13,14},{14,13},{17,18},{18,... | collective-permute-start | bytes 49160 | tf_op jit(solution)/shard_map/ppermute | solution.py:545
  1.5 7.7 %collective-permute-start = (f32[2,4,512]{2,1,0:T(4,128)S(1)}, f32[2,4,512]{2,1,0:T(4,128)S(1)}, u32[]{:S(2)}, u32[]{:S(2)}) collective-permute-start(f32[2,4,512]{2,1,0:T(4,128)S(1)} %get-tuple-element.8), channel_id=1, source_target_pairs={{0,1},{2,3},{1,0},{3,2},{4,5},{6,7},{5,4},{7,6},{8,9},{10,11},{9,8... | collective-permute-start | bytes 49160 | tf_op jit(solution)/shard_map/ppermute | solution.py:543
  39.2 1.3 %copy-start = (f32[4,16]{1,0:T(4,128)S(1)}, f32[4,16]{1,0:T(4,128)}, u32[]{:S(2)}) copy-start(f32[4,16]{1,0:T(4,128)} %param.3) | copy-start | bytes 772
  39.2 8.5 %collective-permute-start.2 = (f32[344,128]{1,0:T(8,128)S(1)}, f32[344,128]{1,0:T(8,128)S(1)}, u32[]{:S(2)}, u32[]{:S(2)}) collective-permute-start(f32[344,128]{1,0:T(8,128)S(1)} %bitcast.14), channel_id=1, source_target_pairs={{64,0},{68,4},{72,8},{76,12},{80,16},{84,20},{88,24},{92,28},{96,3... | collective-permute-start | bytes 528392 | tf_op jit(solution)/shard_map/ppermute | solution.py:525

commit v16 on v15

--- a/solution.py
+++ b/solution.py
@@ -339,13 +339,13 @@
     is_first = tile.block == 0
 
     def fill(i, carry):
-        for u in range(8):
+        for u in range(GROUP):
             for p in range(PLANES):
-                k = 8 * i + u
+                k = GROUP * i + u
                 put(fa, FRONT + PLANES * k + p, tile.unpack(mine, CHUNK * k + RAW_ROWS * p))
         return carry
 
-    lax.fori_loop(0, GROUP // 8, fill, 0)
+    lax.fori_loop(0, 1, fill, 0)
     for i in range(HALO):
         out[TAIL + i] = fa[FRONT + DEEP - HALO + i]
 

time: 74.6 us -> 75.9 us (1.017)
  Pallas kernels: 12.1 us -> 13.4 us
    pallas_call x3, Pallas kernels: 9.18 us -> 10.5 us  [call(): pl.pallas_call(kernel, out_shape=VMEM(shape, jnp.float32), in_specs=[spec...]
  transfers between devices with their start and end apart: 3 -> 3, of which waited for: 0 -> 0; matrix products, arithmetic and copies ran while one was open for 0% -> 0% of each run, Pallas kernels for 11% -> 13%
where the time goes in v16:
time: 75.9 us; the launch traced here: 75.5 us
  blocking collectives  53.6 us (71%)
  Pallas kernels  13.4 us (18%)
  starting transfers between devices  8.35 us (11%)
    all_to_all x1, blocking collectives, rendered(): lax.all_to_all(sent, 'depth', 0, 0, axis_index_groups=groups, tiled=True)  29.7 us
    all_to_all x1, blocking collectives, rendered(): parts = lax.all_to_all(partial, 'depth', 0, 0, tiled=True)  23.9 us
    pallas_call x3, Pallas kernels, call(): pl.pallas_call(kernel, out_shape=VMEM(shape, jnp.float32), in_specs=[spec...  10.5 us
    ppermute x1, starting transfers between devices, rendered(): from_one = lax.ppermute(one, 'rows', pairs + [(b, a) for a, b in pairs])  6.39 us
  transfers between devices with their start and end apart: 3, of which 0 were waited for; matrix products, arithmetic and copies ran while one was open for 0% of the time, Pallas kernels for 13%

profile of v16, /device:TPU:1, one launch (start us, length us, event | category | flops | bytes accessed | tf_op | source)
XLA Modules:
  0.0 75.5 jit_solution(6477267541860527658)
XLA Ops:
  0.0 0.8 %slice_kernel.1 = (f32[2,4,512]{2,1,0:T(4,128)S(1)}, f32[2,4,512]{2,1,0:T(4,128)S(1)}) custom-call(f32[2,128,512]{2,1,0:T(8,128)} %density.3), custom_call_target="tpu_custom_call" | custom-call | tf_op jit(solution)/shard_map/slice_kernel/pallas_call | solution.py:531
  0.8 0.7 collective-permute-start.1
  1.5 6.4 %collective-permute-start = (f32[2,4,512]{2,1,0:T(4,128)S(1)}, f32[2,4,512]{2,1,0:T(4,128)S(1)}, u32[]{:S(2)}, u32[]{:S(2)}) collective-permute-start(f32[2,4,512]{2,1,0:T(4,128)S(1)} %get-tuple-element.8), channel_id=1, source_target_pairs={{0,1},{2,3},{1,0},{3,2},{4,5},{6,7},{5,4},{7,6},{8,9},{10,11},{9,8... | collective-permute-start | bytes 49160 | tf_op jit(solution)/shard_map/ppermute | solution.py:543
  7.9 1.3 %pack_kernel.1.sent = f32[1376,128]{1,0:T(8,128)S(1)} custom-call(f32[2,128,512]{2,1,0:T(8,128)} %density.3), custom_call_target="tpu_custom_call" | custom-call | tf_op jit(solution)/shard_map/pack_kernel/pallas_call | solution.py:547
  9.2 0.0 collective-permute-done.1.from_two
  9.2 0.0 collective-permute-done.from_one
  9.2 0.3 shard_map.28
  9.5 29.7 %all_to_all.16 = f32[16,86,1,128]{3,2,1,0:T(1,128)S(1)} all-to-all(f32[16,86,1,128]{3,2,1,0:T(1,128)S(1)} %bitcast.8), channel_id=1, replica_groups={{0,4,8,12,16,20,24,28,32,36,40,44,48,52,56,60},{64,68,72,76,80,84,88,92..., dimensions={0} | all-to-all | bytes 1409024 | tf_op jit(solution)/shard_map/all_to_all | solution.py:570
  39.2 0.0 copy-start
  39.2 1.3 %collective-permute-start.2 = (f32[344,128]{1,0:T(8,128)S(1)}, f32[344,128]{1,0:T(8,128)S(1)}, u32[]{:S(2)}, u32[]{:S(2)}) collective-permute-start(f32[344,128]{1,0:T(8,128)S(1)} %bitcast.14), channel_id=1, source_target_pairs={{64,0},{68,4},{72,8},{76,12},{80,16},{84,20},{88,24},{92,28},{96,3... | collective-permute-start | bytes 528392 | tf_op jit(solution)/shard_map/ppermute | solution.py:525
  40.5 0.0 copy-done
  40.5 0.1 copy.7
  40.6 8.4 %shard_map.29.inner = f32[14,64,128]{2,1,0:T(8,128)S(1)} custom-call(f32[1376,128]{1,0:T(8,128)S(1)} %bitcast.9, f32[16,4]{1,0:T(8,128)S(1)} %bitcast.12), custom_call_target="tpu_custom_call" | custom-call | tf_op jit(solution)/shard_map/pallas_call | solution.py:512
  49.0 0.0 collective-permute-done.2.after
  49.0 1.8 %shard_map.30 = f32[128,128]{1,0:T(8,128)S(1)} custom-call(f32[344,128]{1,0:T(8,128)S(1)} %collective-permute-done.2.after, f32[14,64,128]{2,1,0:T(8,128)S(1)} %shard_map.29.inner, f32[16,4]{1,0:T(8,128)S(1)} %bitcast.13), custom_call_target="tpu_custom_call" | custom-call | tf_op jit(solution)/shard_map/pallas_call | solution.py:512
  50.7 23.9 %all_to_all.17 = f32[128,1,128]{2,1,0:T(1,128)S(1)} all-to-all(f32[128,1,128]{2,1,0:T(1,128)S(1)} %bitcast.11), channel_id=1, replica_groups=mesh['depth'=128,'rows'=4] {'depth'}, dimensions={0} | all-to-all | bytes 131072 | tf_op jit(solution)/shard_map/all_to_all | solution.py:591
  74.7 0.9 %gather_kernel.1 = f32[4,1,512]{2,1,0:T(1,128)} custom-call(f32[128,128]{1,0:T(8,128)S(1)} %bitcast.10), custom_call_target="tpu_custom_call" | custom-call | tf_op jit(solution)/shard_map/gather_kernel/pallas_call | solution.py:593
  (1 shorter events, 0.0 us)
Async XLA Ops:
  0.8 8.3 %collective-permute-start.1 = (f32[2,4,512]{2,1,0:T(4,128)S(1)}, f32[2,4,512]{2,1,0:T(4,128)S(1)}, u32[]{:S(2)}, u32[]{:S(2)}) collective-permute-start(f32[2,4,512]{2,1,0:T(4,128)S(1)} %get-tuple-element.7.two), channel_id=1, source_target_pairs={{1,2},{2,1},{5,6},{6,5},{9,10},{10,9},{13,14},{14,13},{17,18},{18,... | collective-permute-start | bytes 49160 | tf_op jit(solution)/shard_map/ppermute | solution.py:545
  1.5 7.7 %collective-permute-start = (f32[2,4,512]{2,1,0:T(4,128)S(1)}, f32[2,4,512]{2,1,0:T(4,128)S(1)}, u32[]{:S(2)}, u32[]{:S(2)}) collective-permute-start(f32[2,4,512]{2,1,0:T(4,128)S(1)} %get-tuple-element.8), channel_id=1, source_target_pairs={{0,1},{2,3},{1,0},{3,2},{4,5},{6,7},{5,4},{7,6},{8,9},{10,11},{9,8... | collective-permute-start | bytes 49160 | tf_op jit(solution)/shard_map/ppermute | solution.py:543
  39.2 1.3 %copy-start = (f32[4,16]{1,0:T(4,128)S(1)}, f32[4,16]{1,0:T(4,128)}, u32[]{:S(2)}) copy-start(f32[4,16]{1,0:T(4,128)} %param.3) | copy-start | bytes 772
  39.2 9.8 %collective-permute-start.2 = (f32[344,128]{1,0:T(8,128)S(1)}, f32[344,128]{1,0:T(8,128)S(1)}, u32[]{:S(2)}, u32[]{:S(2)}) collective-permute-start(f32[344,128]{1,0:T(8,128)S(1)} %bitcast.14), channel_id=1, source_target_pairs={{64,0},{68,4},{72,8},{76,12},{80,16},{84,20},{88,24},{92,28},{96,3... | collective-permute-start | bytes 528392 | tf_op jit(solution)/shard_map/ppermute | solution.py:525
